TPU v7x, 32 devices: a whole 2x2x4 slice. The times are simulated.
32 devices in a mesh: exp: 4 (over z), tile: 8 (over y, x, core).
Axes of the slice: x: 2, y: 2, z: 4, core: 2. Of those that a mesh axis runs over, the one named last changes fastest.
Arguments:
- science: bfloat16 [4, 8, 128, 256], P('exp', 'tile'), may hold values from -6 to 6
- mask_bits: int32 [4, 8, 128, 256], P('exp', 'tile'), may hold values from 0 to 1023, as said below
- variance: bfloat16 [4, 8, 128, 256], P('exp', 'tile'), may hold values from 0.25 to 4
- kernel_poly: float32 [4, 8, 8, 3], P('exp', 'tile'), may hold values from -5 to 5
- basis_rows: bfloat16 [8, 31], replicated, may hold values from -1 to 1
- basis_cols: bfloat16 [8, 31], replicated, may hold values from -1 to 1
- destination: int32 [4, 8, 16, 1], P('exp', 'tile'), may hold values from 0 to 7, as said below
- row_offset: int32 [4, 8, 16], P('exp', 'tile'), may hold values from 0 to 1023, as said below
Outputs:
- template: bfloat16 [8192, 128], P('tile')
- difference: bfloat16 [4, 8, 128, 256], P('exp', 'tile')
Inputs may be any that keep to these rules, and one draw needn't show every extreme that they name: `destination`: the pieces of the CCD region at tile index t land, in order of piece number, in contiguous runs on tiles t, t + 1 and t + 2 modulo 8; at most 8 pieces of one region land in one tile, and in every draw some region has exactly 8 in one tile. `row_offset`: offsets of consecutive rows of pieces mostly rise by about 16, wrapping within a tile. `mask_bits`: A pixel is rejected where any of bits 0, 1 or 2 is set; only bits 0 to 9 are used, and in every draw some pixel has all ten set.
All inputs are finite; a program needn't handle non-finite values.
Results may differ from a plain program's by a relative error of at most 0.0063.
Values may be sent and summed in bfloat16 or wider, within the bound.
No kernel may reach another device: no remote copies, remote signals or barrier semaphores. Data moves between devices by JAX's collectives and lax.ppermute only.
A program may use at most 64 MiB of HBM per device.

v0:
```python
import jax
import jax.numpy as jnp
from jax import lax
from jax.sharding import PartitionSpec as P

PR = 16
PC = 128
TR = 1024


def shifted(shard, axis, by):
    length = lax.axis_size(axis)
    return lax.ppermute(shard, axis, [(i, (i + by) % length) for i in range(length)])


def padded_2(cells, sides, width):
    for axis, dim in sides:
        count = lax.axis_size(axis)
        ends = count - 1
        head = lax.slice_in_dim(cells, 0, width, axis=dim)
        tail = lax.slice_in_dim(cells, cells.shape[dim] - width, cells.shape[dim], axis=dim)
        cells = jnp.concatenate(
            [
                lax.ppermute(tail, axis, [(i, (i + 1) % count) for i in range(ends)]),
                cells,
                lax.ppermute(head, axis, [((i + 1) % count, i) for i in range(ends)]),
            ],
            axis=dim,
        )
    return cells


def toeplitz(kernel_taps, length):
    half_width = kernel_taps.shape[1] // 2
    position = jnp.arange(length, dtype=jnp.int32)
    offset_index = position[:, None] - position[None, :] + half_width
    inside = (offset_index >= 0) & (offset_index < kernel_taps.shape[1])
    tap_index = jnp.where(inside, offset_index, 0)
    band_table = jnp.take(kernel_taps, tap_index, axis=1)
    return jnp.where(inside[None], band_table, jnp.zeros_like(band_table))


def coefficient_maps(kernel_terms, height, across):
    y_norm = (jnp.arange(height, dtype=jnp.int32).astype(jnp.float32) - (height - 1) / 2.0) / (
        height / 2.0
    )
    x_norm = (jnp.arange(across, dtype=jnp.int32).astype(jnp.float32) - (across - 1) / 2.0) / (
        across / 2.0
    )
    return (
        kernel_terms[:, 0, None, None]
        + kernel_terms[:, 1, None, None] * y_norm[None, :, None]
        + kernel_terms[:, 2, None, None] * x_norm[None, None, :]
    )


def send_along(bundle, step):
    return shifted((bundle[0], bundle[1], bundle[2]), "tile", step)


def send_back(bundle, step):
    return shifted(bundle, "tile", -step)


def body(
    science, mask_bits, variance, kernel_poly, basis_rows, basis_cols, destination, row_offset
):
    region = science[0, 0]
    height, across = region.shape
    col_band = toeplitz(basis_cols, across)
    row_band = toeplitz(basis_rows, height)
    first_pass = jnp.einsum(
        "yc,bcx->byx", region, col_band, preferred_element_type=jnp.float32
    ).astype(jnp.bfloat16)
    second_pass = jnp.einsum(
        "biy,bix->byx", row_band, first_pass, preferred_element_type=jnp.float32
    )
    matched = jnp.sum(coefficient_maps(kernel_poly[0, 0], height, across) * second_pass, axis=0)
    rejected = jnp.bitwise_and(mask_bits[0, 0], 7) != 0
    weight = jnp.where(rejected, jnp.float32(0.0), 1.0 / variance[0, 0].astype(jnp.float32))
    weighted = (matched * weight).astype(jnp.bfloat16)
    weight_sent = weight.astype(jnp.bfloat16)
    block_rows = height // PR
    block_cols = across // PC

    def to_pieces(picture):
        return (
            picture.reshape(block_rows, PR, block_cols, PC)
            .transpose(0, 2, 1, 3)
            .reshape(-1, PR, PC)
        )

    target = destination.reshape(-1)
    offset = row_offset.reshape(-1)
    pieces_count = target.shape[0]
    tile_count = lax.axis_size("tile")
    reach = 3
    slot_count = pieces_count // 2
    slot_total = reach * slot_count
    offset = jnp.where(target == tile_count - 1, jnp.minimum(offset, TR - PR), offset)
    relative = (target - lax.axis_index("tile") + tile_count) % tile_count
    one_hot = (relative[:, None] == jnp.arange(reach, dtype=jnp.int32)[None, :]).astype(jnp.int32)
    earlier = jnp.cumsum(one_hot, axis=0) - one_hot
    slot_rank = jnp.sum(earlier * one_hot, axis=1)
    send_index = relative * slot_count + slot_rank
    send_pixels = (
        jnp.zeros((slot_total, PR, PC), jnp.bfloat16).at[send_index].set(to_pieces(weighted))
    )
    send_weights = (
        jnp.zeros((slot_total, PR, PC), jnp.bfloat16).at[send_index].set(to_pieces(weight_sent))
    )
    send_offsets = jnp.full((slot_total,), -1, jnp.int32).at[send_index].set(offset)
    send_pixels = send_pixels.reshape(reach, slot_count, PR, PC)
    send_weights = send_weights.reshape(reach, slot_count, PR, PC)
    send_offsets = send_offsets.reshape(reach, slot_count)
    got_list = [(send_pixels[0], send_weights[0], send_offsets[0])]
    for step in range(1, reach):
        got_list.append(
            send_along((send_pixels[step], send_weights[step], send_offsets[step]), step)
        )
    got_pixels = jnp.stack([item[0] for item in got_list])
    got_weights = jnp.stack([item[1] for item in got_list])
    got_offsets = jnp.stack([item[2] for item in got_list])
    extent = TR + PR
    is_live = got_offsets >= 0
    sky_row = jnp.where(
        is_live[..., None], got_offsets[..., None] + jnp.arange(PR, dtype=jnp.int32), extent - 1
    ).reshape(-1)
    pixel_sum = (
        jnp.zeros((extent, PC), jnp.float32)
        .at[sky_row]
        .add(got_pixels.reshape(-1, PC).astype(jnp.float32))
    )
    weight_sum = (
        jnp.zeros((extent, PC), jnp.float32)
        .at[sky_row]
        .add(got_weights.reshape(-1, PC).astype(jnp.float32))
    )
    local_sums = jnp.stack([pixel_sum, weight_sum])[:, : extent - 1]
    rim_rows = PR - 1
    padded = padded_2(local_sums, (("tile", 1),), rim_rows)
    core_rows = padded[:, rim_rows : rim_rows + extent - 1]
    core_rows = core_rows.at[:, :rim_rows].add(padded[:, :rim_rows])
    core_rows = core_rows.at[:, TR : TR + rim_rows].add(padded[:, rim_rows + extent - 1 :])
    extended = jnp.concatenate([core_rows, jnp.zeros((2, 1, PC), jnp.float32)], axis=1)
    totals = lax.psum(extended, "exp")
    template_ext = (totals[0] / jnp.maximum(totals[1], 1.0)).astype(jnp.bfloat16)
    cutout = template_ext[sky_row].reshape(reach, slot_count, PR, PC)
    returned_list = [cutout[0]]
    for step in range(1, reach):
        returned_list.append(send_back(cutout[step], step))
    returned = jnp.stack(returned_list)
    own_cutouts = returned.reshape(slot_total, PR, PC)[send_index]
    back_image = (
        own_cutouts.reshape(block_rows, block_cols, PR, PC)
        .transpose(0, 2, 1, 3)
        .reshape(height, across)
    )
    difference = (matched - back_image.astype(jnp.float32)).astype(jnp.bfloat16)
    return (template_ext[:TR], difference[None, None])


def solution(mesh):
    placed = (
        P("exp", "tile", None, None),
        P("exp", "tile", None, None),
        P("exp", "tile", None, None),
        P("exp", "tile", None, None),
        P(),
        P(),
        P("exp", "tile", None, None),
        P("exp", "tile", None),
    )
    return jax.shard_map(
        body,
        mesh=mesh,
        in_specs=placed,
        out_specs=(P("tile", None), P("exp", "tile", None, None)),
        check_vma=False,
    )
```

profile of v0, /device:TPU:0, one launch (start us, length us, event | category | flops | bytes accessed | tf_op | source)
XLA Modules:
  0.0 417.1 jit_solution(487939907609007611)
XLA Ops:
  10.1 2.5 collective-permute-start.1
  13.9 228.9 %gather_fusion.1 = bf16[65536,8]{1,0:T(8,128)(2,1)} fusion(bf16[8,31]{0,1:T(8,128)(2,1)S(1)} %copy.22, s32[65536]{0:T(1024)S(1)} %broadcast_clamp_fusion), kind=kCustom, calls=%fused_computation.1 | custom fusion | bytes 2359296 | tf_op jit(solution)/shard_map/jit(_take)/gather | solution.py:39
  242.8 15.9 %copy.23 = bf16[256,256,8]{0,1,2:T(8,128)(2,1)S(1)} copy(bf16[256,256,8]{2,1,0:T(8,128)(2,1)} %bitcast.92) | data formatting | bytes 2097152 | tf_op jit(solution)/shard_map/jit(_take)/gather | solution.py:39
  258.8 57.8 %gather_fusion = bf16[16384,8]{1,0:T(8,128)(2,1)} fusion(bf16[8,31]{0,1:T(8,128)(2,1)S(1)} %copy.20, s32[16384]{0:T(1024)S(1)} %fusion.44), kind=kCustom, calls=%fused_computation | custom fusion | bytes 589824 | tf_op jit(solution)/shard_map/jit(_take)/gather | solution.py:39
  316.6 6.3 %copy.21 = bf16[128,128,8]{0,1,2:T(8,128)(2,1)S(1)} copy(bf16[128,128,8]{2,1,0:T(8,128)(2,1)} %bitcast.99) | data formatting | bytes 524288 | tf_op jit(solution)/shard_map/jit(_take)/gather | solution.py:39
  323.1 0.8 fusion
  324.3 1.0 scatter_fusion.1
  325.3 1.3 collective-permute-start.4
  326.6 1.5 collective-permute-start.5
  328.2 1.0 scatter_fusion
  329.9 1.6 collective-permute-done.5
  331.5 2.5 scatter_custom_fusion.4
  334.2 2.5 scatter_custom_fusion.2
  336.7 1.7 collective-permute-start.6
  338.4 0.8 collective-permute-done.6
  339.2 1.3 collective-permute-start.7
  340.8 1.6 collective-permute-done.7
  342.4 1.1 concatenate.11
  343.5 56.6 %all-reduce.3.cloned.1.call-done = f32[2,1040,128]{2,1,0:T(8,128)} async-done(((f32[2,1040,128]{2,1,0:T(8,128)}), f32[2,1040,128]{2,1,0:T(8,128)}) %all-reduce.3.cloned.1.call-update) | async-done | bytes 1064976 | tf_op jit(solution)/shard_map/psum | solution.py:146
  400.1 1.4 fusion.74
  401.5 1.4 gather_fusion.2
  403.0 2.0 collective-permute-start.8
  405.6 0.7 slice_bitcast_fusion
  406.7 2.1 collective-permute-done.9
  (77 shorter events, 8.4 us)
Async XLA Ops:
  7.2 315.9 %copy-start = (bf16[1,1,128,256]{3,2,1,0:T(8,128)(2,1)S(1)}, bf16[1,1,128,256]{3,2,1,0:T(8,128)(2,1)}, u32[]{:S(2)}) copy-start(bf16[1,1,128,256]{3,2,1,0:T(8,128)(2,1)} %param.12) | copy-start | bytes 196612
  7.2 6.6 %copy-start.4 = (bf16[8,31]{1,0:T(8,128)(2,1)S(1)}, bf16[8,31]{1,0:T(8,128)(2,1)}, u32[]{:S(2)}) copy-start(bf16[8,31]{1,0:T(8,128)(2,1)} %param.17) | copy-start | bytes 1492
  7.2 392.9 %all-reduce.3.cloned.1.call-start = ((), (), s32[]{:S(2)}) async-start(), calls=%async_computation | async-start | bytes 2129920 | tf_op jit(solution)/shard_map/psum | solution.py:146
  9.6 319.7 %collective-permute-start = (s32[8]{0:T(128)S(1)}, s32[8]{0:T(128)S(1)}, u32[]{:S(2)}, u32[]{:S(2)}) collective-permute-start(s32[8]{0:T(128)S(1)} %get-tuple-element.44), channel_id=1, source_target_pairs={{0,1},{1,2},{2,3},{3,4},{4,5},{5,6},{6,7},{7,0},{8,9},{9,10},{10,1... | collective-permute-start | bytes 104 | tf_op jit(solution)/shard_map/ppermute | solution.py:13
  10.1 319.5 %collective-permute-start.1 = (s32[8]{0:T(128)S(1)}, s32[8]{0:T(128)S(1)}, u32[]{:S(2)}, u32[]{:S(2)}) collective-permute-start(s32[8]{0:T(128)S(1)} %get-tuple-element.43), channel_id=1, source_target_pairs={{0,2},{1,3},{2,4},{3,5},{4,6},{5,7},{6,0},{7,1},{8,10},{9,11},{10,... | collective-permute-start | bytes 104 | tf_op jit(solution)/shard_map/ppermute | solution.py:13
  242.8 15.9 %copy-start.5 = (bf16[8,31]{1,0:T(8,128)(2,1)S(1)}, bf16[8,31]{1,0:T(8,128)(2,1)}, u32[]{:S(2)}) copy-start(bf16[8,31]{1,0:T(8,128)(2,1)} %param.16) | copy-start | bytes 1492
  323.1 0.9 copy-start.2
  323.1 0.9 copy-start.3
  325.3 4.5 %collective-permute-start.4 = (bf16[8,16,128]{2,1,0:T(8,128)(2,1)S(1)}, bf16[8,16,128]{2,1,0:T(8,128)(2,1)S(1)}, u32[]{:S(2)}, u32[]{:S(2)}) collective-permute-start(bf16[8,16,128]{2,1,0:T(8,128)(2,1)S(1)} %get-tuple-element.35), channel_id=1, source_target_pairs={{0,1},{1,2},{2,3},{3,4},{4,5},{5,6},{6,7},{7,0},{8,9},{9,10},{10,1... | collective-permute-start | bytes 98312 | tf_op jit(solution)/shard_map/ppermute | solution.py:13
  326.6 4.8 %collective-permute-start.5 = (bf16[8,16,128]{2,1,0:T(8,128)(2,1)S(1)}, bf16[8,16,128]{2,1,0:T(8,128)(2,1)S(1)}, u32[]{:S(2)}, u32[]{:S(2)}) collective-permute-start(bf16[8,16,128]{2,1,0:T(8,128)(2,1)S(1)} %get-tuple-element.34), channel_id=1, source_target_pairs={{0,2},{1,3},{2,4},{3,5},{4,6},{5,7},{6,0},{7,1},{8,10},{9,11},{10,... | collective-permute-start | bytes 98312 | tf_op jit(solution)/shard_map/ppermute | solution.py:13
  329.2 4.7 %collective-permute-start.2 = (bf16[8,16,128]{2,1,0:T(8,128)(2,1)S(1)}, bf16[8,16,128]{2,1,0:T(8,128)(2,1)S(1)}, u32[]{:S(2)}, u32[]{:S(2)}) collective-permute-start(bf16[8,16,128]{2,1,0:T(8,128)(2,1)S(1)} %get-tuple-element.38), channel_id=1, source_target_pairs={{0,1},{1,2},{2,3},{3,4},{4,5},{5,6},{6,7},{7,0},{8,9},{9,10},{10,1... | collective-permute-start | bytes 98312 | tf_op jit(solution)/shard_map/ppermute | solution.py:13
  329.3 4.9 %collective-permute-start.3 = (bf16[8,16,128]{2,1,0:T(8,128)(2,1)S(1)}, bf16[8,16,128]{2,1,0:T(8,128)(2,1)S(1)}, u32[]{:S(2)}, u32[]{:S(2)}) collective-permute-start(bf16[8,16,128]{2,1,0:T(8,128)(2,1)S(1)} %get-tuple-element.37), channel_id=1, source_target_pairs={{0,2},{1,3},{2,4},{3,5},{4,6},{5,7},{6,0},{7,1},{8,10},{9,11},{10,... | collective-permute-start | bytes 98312 | tf_op jit(solution)/shard_map/ppermute | solution.py:13
  336.7 2.5 collective-permute-start.6
  339.2 3.1 collective-permute-start.7
  400.1 5.4 %copy-start.1 = (f32[2,1040,128]{2,1,0:T(8,128)S(1)}, f32[2,1040,128]{2,1,0:T(8,128)}, u32[]{:S(2)}) copy-start(f32[2,1040,128]{2,1,0:T(8,128)} %all-reduce.3.cloned.1.call-done) | copy-start | bytes 3194884
  403.0 3.7 collective-permute-start.8
  404.9 3.9 collective-permute-start.9
Sparse Core Ops, SparseCore 0:
  343.6 56.4 all-reduce.2
where the time goes:
time: 418 us; the launch traced here: 417 us
  local copies, waits for them, and re-layouts  317 us (76%)
  waiting for transfers between devices  63.4 us (15%)
  between operations  14.4 us (3%)
  starting transfers between devices  11.8 us (3%)
  other arithmetic  9.48 us (2%)
    gather x4, local copies, waits for them, and re-layouts, toeplitz(): band_table = jnp.take(kernel_taps, tap_index, axis=1)  309 us
    psum x1, waiting for transfers between devices, body(): totals = lax.psum(extended, 'exp')  56.6 us
    ppermute x8, starting transfers between devices, shifted(): lax.ppermute(shard, axis, [(i, (i + by) % length) for i in range(length)])  8.77 us
  transfers between devices with their start and end apart: 11, of which 7 were waited for; matrix products, arithmetic and copies ran while one was open for 76% of the time, Pallas kernels for 0%

commit v1 on v0

v1 whole, which is shorter than its diff:
```python
import jax
import jax.numpy as jnp
from jax import lax
from jax.experimental import pallas as pl
from jax.experimental.pallas import tpu as pltpu
from jax.sharding import PartitionSpec as P

PR = 16
PC = 128
TR = 1024
F32 = jnp.float32
BF16 = jnp.bfloat16
SENT = 32.0
REACH = 3
PARAMS = pltpu.CompilerParams(vmem_limit_bytes=24 * 1024 * 1024)


def iota(shape, dim):
    return lax.broadcasted_iota(jnp.int32, shape, dim)


def dot(a, b, ca=1, cb=0):
    return lax.dot_general(a, b, (((ca,), (cb,)), ((), ())), preferred_element_type=F32)


def circulant(taps, reverse):
    count, ks = taps.shape
    half = ks // 2
    tap, lane = iota((ks, PC), 0), iota((ks, PC), 1)
    place = (half - tap) if reverse else (tap - half)
    pick = jnp.where((place + PC) % PC == lane, 1.0, 0.0).astype(BF16)
    row = dot(taps, pick)
    return [
        pltpu.roll(jnp.broadcast_to(row[b : b + 1], (PC, PC)), 0, 1, stride=1, stride_axis=0)
        for b in range(count)
    ]


def shares(exps):
    return PC // exps, PC // 4


def piece_scalars(dest_ref, off_ref, p, tile, tiles):
    target = dest_ref[p]
    offset = off_ref[p]
    offset = jnp.where(target == tiles - 1, jnp.minimum(offset, TR - PR), offset)
    return (target - tile + tiles) % tiles, offset


def match_body(
    exps, tiles, sci_ref, mask_ref, var_ref, poly_ref, brow_ref, bcol_ref, dest_ref, off_ref,
    matched_ref, *z_refs,
):
    exp, tile = lax.axis_index("exp"), lax.axis_index("tile")
    height, across = sci_ref.shape
    bases = brow_ref.shape[0]
    d = iota((PC, PC), 1) - iota((PC, PC), 0)
    zero = jnp.zeros((PC, PC), F32)
    cols = circulant(bcol_ref[...], True)
    rows = circulant(brow_ref[...], False)
    sci = sci_ref[...]
    y = (iota((height, across), 0).astype(F32) - (height - 1) / 2.0) / (height / 2.0)
    x = (iota((height, across), 1).astype(F32) - (across - 1) / 2.0) / (across / 2.0)
    matched = jnp.zeros((height, across), F32)
    for b in range(bases):
        mid = jnp.where(jnp.abs(d) < PC // 2, cols[b], zero)
        up = jnp.where(d < -(PC // 2), cols[b], zero)
        low = jnp.where(d > PC // 2, cols[b], zero)
        band = jnp.concatenate(
            [jnp.concatenate([mid, up], 1), jnp.concatenate([low, mid], 1)], 0
        ).astype(BF16)
        first = dot(sci, band).astype(BF16)
        row_band = jnp.where(jnp.abs(d) < PC // 2, rows[b], zero).astype(BF16)
        second = dot(row_band, first)
        matched += (poly_ref[b, 0] + poly_ref[b, 1] * y + poly_ref[b, 2] * x) * second
    matched_ref[...] = matched
    rejected = jnp.bitwise_and(mask_ref[...], 7) != 0
    weight = jnp.where(rejected, 0.0, 1.0 / var_ref[...].astype(F32))
    weighted = matched * weight
    parts = [weighted[:, :PC], weighted[:, PC:], weight[:, :PC], weight[:, PC:]]
    share, span = shares(exps)
    group = iota((height, PC), 1) // span

    lane = iota((1, PC), 1)
    meta = jnp.zeros((PR, PC), F32)
    sub = iota((PR, PC), 0)
    for c in range(2):
        pos = jnp.zeros((1, PC), jnp.int32)
        step = jnp.zeros((1, PC), jnp.int32)
        for rb in range(height // PR):
            rel, offset = piece_scalars(dest_ref, off_ref, 2 * rb + c, tile, tiles)
            here = lane // PR == rb
            pos = jnp.where(here, offset + lane % PR, pos)
            step = jnp.where(here, rel, step)
        for i, v in enumerate((pos // 32, pos % 32, step)):
            meta = jnp.where(sub == 3 * c + i, v.astype(F32), meta)
    meta = meta.astype(BF16)
    for k in range(exps):
        j = jnp.bitwise_xor(exp, k)
        out = jnp.zeros((height, PC), F32)
        for g in range(4):
            moved = pltpu.roll(parts[g], (PC + span * g - share * j) % PC, 1)
            out = jnp.where(group == g, moved, out)
        z_refs[k][0:height] = out.astype(BF16)
        z_refs[k][height : height + PR] = meta


def pick_body(exps, *refs):
    z_refs, (m1_ref, m2_ref, m3_ref) = refs[:exps], refs[exps:]
    height = z_refs[0].shape[0] - PR
    half = height // 2
    _, span = shares(exps)
    lanes = iota((height, PC), 1)
    odd = (lanes // span) % 2 == 1
    sub16, lane16 = iota((PR, PC), 0), iota((PR, PC), 1)
    to_cols = jnp.where(sub16 == 2 + 3 * ((lane16 // span) % 2), 1.0, 0.0).astype(BF16)
    spill_row = iota((REACH * PR, PC), 0)
    spill = jnp.zeros((REACH * PR, PC), F32)
    metas1 = [jnp.zeros((PR, PC), F32) for _ in range(meta_tiles(exps))]
    metas2 = [jnp.zeros((PR, PC), F32) for _ in range(meta_tiles(exps))]
    first_half = iota((1, PC), 1) < half
    for k in range(exps):
        data = z_refs[k][0:height]
        meta = z_refs[k][height : height + PR]
        step_at = dot(meta, to_cols, 0, 0)
        top, bottom = data[:half], data[half:]
        m1_ref[half * k : half * (k + 1)] = jnp.where(step_at[:half] == 1.0, top, bottom)
        m2_ref[half * k : half * (k + 1)] = bottom
        meta = meta.astype(F32)
        sums = []
        for c in range(2):
            hi, lo, step = (meta[3 * c + i : 3 * c + i + 1] for i in range(3))
            over = hi * 32.0 + lo - TR
            at = jnp.where(over >= 0.0, over + PR * step, -1.0).astype(jnp.int32)
            sums.append(dot(jnp.where(spill_row == at, 1.0, 0.0).astype(BF16), data))
            hi1 = jnp.where(step == 1.0, hi, -SENT)
            hi2 = jnp.where(step == 2.0, hi, -SENT)
            swapped = [pltpu.roll(v, half, 1) for v in (hi1, lo, hi2, lo)]
            use_top = step == 1.0
            hi_1 = jnp.where(use_top, hi1, swapped[0])
            lo_1 = jnp.where(use_top, lo, swapped[1])
            hi_2, lo_2 = swapped[2], swapped[3]
            if k % 2 == 1:
                hi_1, lo_1 = pltpu.roll(hi_1, half, 1), pltpu.roll(lo_1, half, 1)
                hi_2, lo_2 = hi2, lo
            keep = first_half if k % 2 == 0 else jnp.logical_not(first_half)
            row = 4 * (k // 2) + 2 * c
            tile_at, row = row // PR, row % PR
            for metas, values in ((metas1, (hi_1, lo_1)), (metas2, (hi_2, lo_2))):
                for i, v in enumerate(values):
                    metas[tile_at] = jnp.where((sub16 == row + i) & keep, v, metas[tile_at])
        spill += jnp.where((iota((REACH * PR, PC), 1) // span) % 2 == 1, sums[1], sums[0])
    coarse = spill.astype(BF16)
    fine = (spill - coarse.astype(F32)).astype(BF16)
    base = half * exps
    for ref, metas, s in ((m1_ref, metas1, 0), (m2_ref, metas2, 1)):
        for i, m in enumerate(metas):
            ref[base + PR * i : base + PR * (i + 1)] = m.astype(BF16)
        at = base + PR * len(metas)
        ref[at : at + PR] = coarse[PR * s : PR * (s + 1)]
        ref[at + PR : at + 2 * PR] = fine[PR * s : PR * (s + 1)]
    m3_ref[0:PR] = coarse[2 * PR :]
    m3_ref[PR : 2 * PR] = fine[2 * PR :]


def meta_tiles(exps):
    return -(-2 * exps // PR)


def sum_body(exps, *refs):
    z_refs, (m1_ref, m2_ref, m3_ref, out_ref) = refs[:exps], refs[exps:]
    height = z_refs[0].shape[0] - PR
    half = height // 2
    share, span = shares(exps)
    base = half * exps
    tiles = meta_tiles(exps)
    first_half = iota((1, PC), 1) < half
    data = []
    places = ([], [])
    for p in range(exps // 2):
        data += [z_refs[2 * p][0:half], z_refs[2 * p + 1][0:half]]
        metas = [z_refs[2 * p + i][height : height + PR].astype(F32) for i in range(2)]
        for c in range(2):
            pos = []
            for m in metas:
                hi, lo, step = (m[3 * c + i : 3 * c + i + 1] for i in range(3))
                pos.append(jnp.where(step == 0.0, hi * 32.0 + lo, -1.0))
            places[c].append(jnp.where(first_half, pos[0], pltpu.roll(pos[1], half, 1)))
    for ref in (m1_ref, m2_ref):
        data.append(ref[0:base])
        for p in range(exps // 2):
            tile_at, row = 4 * p // PR, 4 * p % PR
            m = ref[base + PR * tile_at : base + PR * (tile_at + 1)].astype(F32)
            for c in range(2):
                at = row + 2 * c
                places[c].append(m[at : at + 1] * 32.0 + m[at + 1 : at + 2])
    data = jnp.concatenate(data, 0)
    at = base + PR * tiles
    spill = jnp.zeros((PR, PC), F32)
    for ref, start in ((m1_ref, at), (m2_ref, at), (m3_ref, 0)):
        for i in range(2):
            spill += ref[start + PR * i : start + PR * (i + 1)].astype(F32)
    rows = TR // exps
    group = iota((rows, PC), 1) // span
    owned = iota((rows, PC), 1) // share
    packed = jnp.zeros((rows, PC), F32)
    places = [[v.astype(jnp.int32) for v in vs] for vs in places]
    for q in range(exps):
        row = iota((rows, PC), 0) + rows * q
        both = []
        for c in range(2):
            hot = jnp.concatenate(
                [jnp.where(row == v, 1.0, 0.0).astype(BF16) for v in places[c]], 1
            )
            both.append(dot(hot, data))
        total = jnp.where(group % 2 == 1, both[1], both[0])
        if q == 0:
            total = jnp.concatenate([total[:PR] + spill, total[PR:]], 0)
        total += pltpu.roll(total, PC - span, 1)
        quotient = total / jnp.maximum(pltpu.roll(total, PC - 2 * span, 1), 1.0)
        if q:
            quotient = pltpu.roll(quotient, share * q, 1)
        packed = jnp.where(owned == q, quotient, packed)
    out_ref[...] = packed.astype(BF16)


def cut_body(exps, *refs):
    packed_refs = refs[:exps]
    z_ref, m1_ref, m2_ref = refs[exps : exps + 3]
    template_ref, own_ref, n1_ref, n2_ref, n3_ref = refs[exps + 3 :]
    exp = lax.axis_index("exp")
    height = z_ref.shape[0] - PR
    half = height // 2
    share, _ = shares(exps)
    base = half * exps
    rows = TR // exps
    lane = iota((rows, PC), 1) // share
    packed = [r[...].astype(F32) for r in packed_refs]
    blocks = []
    for q in range(exps):
        block = jnp.zeros((rows, PC), F32)
        for k in range(exps):
            j = jnp.bitwise_xor(exp, k)
            moved = pltpu.roll(packed[k], (PC + share * (j - q)) % PC, 1)
            block = jnp.where(lane == j, moved, block)
        blocks.append(block.astype(BF16))
    template = jnp.concatenate(blocks, 0)
    template_ref[...] = template
    sub16 = iota((PR, PC), 0)
    hots = []
    for ref, at, first, invalid in (
        (z_ref, height, (0, 3), True), (m1_ref, base, (0, 2), False), (m2_ref, base, (0, 2), False),
    ):
        meta = ref[at : at + PR]
        for c in range(2):
            scale = jnp.where(sub16 == first[c], 32.0, jnp.where(sub16 == first[c] + 1, 1.0, 0.0))
            if invalid:
                scale = jnp.where(sub16 == 3 * c + 2, -2.0 * TR, scale)
            pos = dot(meta, scale.astype(BF16), 0, 0)[:half].astype(jnp.int32)
            lanes = iota((half, PC), 1)
            hots.append(
                jnp.concatenate(
                    [
                        jnp.where(lanes + PC * i == pos, 1.0, 0.0).astype(BF16)
                        for i in range(TR // PC)
                    ],
                    1,
                )
            )
    cut = dot(jnp.concatenate(hots, 0), template).astype(BF16)
    head = template[:PR]
    own_ref[...] = cut[:height]
    n1_ref[0:height] = cut[height : 2 * height]
    n1_ref[height : height + PR] = head
    n2_ref[0:height] = cut[2 * height :]
    n2_ref[height : height + PR] = head
    n3_ref[...] = head


def subtract_body(tiles, matched_ref, own_ref, n1_ref, n2_ref, n3_ref, dest_ref, off_ref, out_ref):
    tile = lax.axis_index("tile")
    height = own_ref.shape[0]
    half = height // 2
    lane = iota((PR, PC), 1)
    sub = iota((PR, PC), 0)
    heads = [n1_ref[height : height + PR], n2_ref[height : height + PR], n3_ref[...]]
    heads.append(jnp.zeros((PC - REACH * PR, PC), BF16))
    heads = jnp.concatenate(heads, 0)
    for c in range(2):
        hots, backs = [], []
        for rb in range(height // PR):
            rel, offset = piece_scalars(dest_ref, off_ref, 2 * rb + c, tile, tiles)
            at = half * c + (PR * rb) % half
            middle = n1_ref[at : at + PR].astype(F32)
            if PR * rb < half:
                backs.append(jnp.where(rel == 0, own_ref[at : at + PR].astype(F32), middle))
            else:
                backs.append(jnp.where(rel == 2, n2_ref[at : at + PR].astype(F32), middle))
            over = sub + (offset - TR)
            hots.append(jnp.where((over >= 0) & (lane == over + PR * rel), 1.0, 0.0).astype(BF16))
        back = jnp.concatenate(backs, 0) + dot(jnp.concatenate(hots, 0), heads)
        out_ref[:, PC * c : PC * (c + 1)] = (matched_ref[:, PC * c : PC * (c + 1)] - back).astype(BF16)


VM = pl.BlockSpec(memory_space=pltpu.VMEM)
SM = pl.BlockSpec(memory_space=pltpu.SMEM)


def call(body, outs, specs, name):
    return pl.pallas_call(
        body,
        out_shape=tuple(jax.ShapeDtypeStruct(s, t) for s, t in outs),
        in_specs=specs,
        out_specs=tuple(VM for _ in outs),
        compiler_params=PARAMS,
        name=name,
    )


def along_exp(x, k, exps):
    return lax.ppermute(x, "exp", [(i, i ^ k) for i in range(exps)])


def along_tile(x, by, tiles):
    return lax.ppermute(x, "tile", [(i, (i + by) % tiles) for i in range(tiles)])


def program_of(exps, tiles):
    def body(science, mask_bits, variance, kernel_poly, basis_rows, basis_cols, destination, row_offset):
        height, across = science.shape[2:]
        bases = basis_rows.shape[0]
        half = height // 2
        dest, off = destination.reshape(-1), row_offset.reshape(-1)
        message = ((height + PR, PC), BF16)
        matched, *z = call(
            lambda *r: match_body(exps, tiles, *r),
            [((height, across), F32)] + [message] * exps,
            [VM, VM, VM, SM, VM, VM, SM, SM],
            "match",
        )(
            science.reshape(height, across), mask_bits.reshape(height, across),
            variance.reshape(height, across), kernel_poly.reshape(bases, 3),
            basis_rows, basis_cols, dest, off,
        )
        z = [z[0]] + [along_exp(z[k], k, exps) for k in range(1, exps)]
        big = ((half * exps + PR * meta_tiles(exps) + 2 * PR, PC), BF16)
        m1, m2, m3 = call(
            lambda *r: pick_body(exps, *r), [big, big, ((2 * PR, PC), BF16)], [VM] * exps, "pick"
        )(*z)
        m1, m2, m3 = (along_tile(m, i + 1, tiles) for i, m in enumerate((m1, m2, m3)))
        (packed,) = call(
            lambda *r: sum_body(exps, *r), [((TR // exps, PC), BF16)], [VM] * (exps + 3), "sum"
        )(*z, m1, m2, m3)
        all_packed = [packed] + [along_exp(packed, k, exps) for k in range(1, exps)]
        template, own, n1, n2, n3 = call(
            lambda *r: cut_body(exps, *r),
            [((TR, PC), BF16), ((height, PC), BF16), message, message, ((PR, PC), BF16)],
            [VM] * (exps + 3),
            "cut",
        )(*all_packed, z[0], m1, m2)
        n1, n2, n3 = (along_tile(n, -1 - i, tiles) for i, n in enumerate((n1, n2, n3)))
        (difference,) = call(
            lambda *r: subtract_body(tiles, *r), [((height, across), BF16)],
            [VM] * 5 + [SM] * 2, "subtract",
        )(matched, own, n1, n2, n3, dest, off)
        return template, difference[None, None]

    return body


def solution(mesh):
    placed = (
        P("exp", "tile", None, None),
        P("exp", "tile", None, None),
        P("exp", "tile", None, None),
        P("exp", "tile", None, None),
        P(),
        P(),
        P("exp", "tile", None, None),
        P("exp", "tile", None),
    )
    return jax.shard_map(
        program_of(mesh.shape["exp"], mesh.shape["tile"]),
        mesh=mesh,
        in_specs=placed,
        out_specs=(P("tile", None), P("exp", "tile", None, None)),
        check_vma=False,
    )
```

time: 418 us -> 41.9 us (0.10)
  local copies, waits for them, and re-layouts: 317 us -> 4.03 us
  waiting for transfers between devices: 63.4 us -> 15.2 us
  between operations: 14.4 us -> 0.68 us
  other arithmetic: 9.48 us -> 0 us
  Pallas kernels: 0 us -> 5.68 us
  starting transfers between devices: 11.8 us -> 16 us
    gather x6 -> x0, local copies, waits for them, and re-layouts: 311 us -> none  [the longest x4 309 us: toeplitz(): band_table = jnp.take(kernel_taps, tap_index, axis=1)]
    psum x1 -> x0, waiting for transfers between devices: 56.6 us -> none  [body(): totals = lax.psum(extended, 'exp')]
    ppermute x10 -> x12, waiting for transfers between devices: 6.8 us -> 15.2 us  [the longest x6 10 us: along_exp(): return lax.ppermute(x, 'exp', [(i, i ^ k) for i in range(exps)])]
    pallas_call x0 -> x5, Pallas kernels: none -> 5.68 us  [the longest x1 1.68 us: body(): call(lambda *r: match_body(exps, tiles, *r), [((height, across), F32)] +...]
    scatter-add x3 -> x0, other arithmetic: 4.91 us -> none  [the longest x1 2.45 us: body(): weight_sum = jnp.zeros((extent, PC), jnp.float32).at[sky_row].add(got_wei...]
    ppermute x10 -> x12, starting transfers between devices: 11.8 us -> 16 us  [the longest x6 10.2 us: along_exp(): return lax.ppermute(x, 'exp', [(i, i ^ k) for i in range(exps)])]
  transfers between devices with their start and end apart: 11 -> 12, of which waited for: 7 -> 7; matrix products, arithmetic and copies ran while one was open for 76% -> 0% of each run, Pallas kernels for 0% -> 0%
where the time goes in v1:
time: 41.9 us; the launch traced here: 41.6 us
  starting transfers between devices  16 us (38%)
  waiting for transfers between devices  15.2 us (36%)
  Pallas kernels  5.68 us (14%)
  local copies, waits for them, and re-layouts  4.03 us (10%)
  between operations  0.68 us (2%)
    ppermute x6, starting transfers between devices, along_exp(): return lax.ppermute(x, 'exp', [(i, i ^ k) for i in range(exps)])  10.2 us
    ppermute x6, waiting for transfers between devices, along_exp(): return lax.ppermute(x, 'exp', [(i, i ^ k) for i in range(exps)])  10 us
    ppermute x6, starting transfers between devices, along_tile(): lax.ppermute(x, 'tile', [(i, (i + by) % tiles) for i in range(tiles)])  5.84 us
    ppermute x6, waiting for transfers between devices, along_tile(): lax.ppermute(x, 'tile', [(i, (i + by) % tiles) for i in range(tiles)])  5.18 us
    unnamed x14, local copies, waits for them, and re-layouts  3.28 us
    pallas_call x1, Pallas kernels, body(): call(lambda *r: match_body(exps, tiles, *r), [((height, across), F32)] +...  1.68 us
    pallas_call x1, Pallas kernels, body(): call(lambda *r: subtract_body(tiles, *r), [((height, across), BF16)], [VM...  1.38 us
    pallas_call x1, Pallas kernels, body(): call(lambda *r: sum_body(exps, *r), [((TR // exps, PC), BF16)], [VM] * (e...  1.24 us
  transfers between devices with their start and end apart: 12, of which 7 were waited for; matrix products, arithmetic and copies ran while one was open for 0% of the time, Pallas kernels for 0%

profile of v1, /device:TPU:0, one launch (start us, length us, event | category | flops | bytes accessed | tf_op | source)
XLA Modules:
  0.0 41.6 jit_solution(10053047151914554357)
XLA Ops:
  0.6 0.8 %copy.11 = f32[1,1,8,3]{3,2,1,0:T(8,128)S(1)} copy(f32[1,1,8,3]{2,1,3,0:T(1,128)} %param.11) | data formatting | bytes 192 | tf_op jit(solution)/shard_map/reshape | solution.py:342
  1.4 0.7 %copy-done.4 = bf16[8,31]{1,0:T(8,128)(2,1)S(1)} copy-done((bf16[8,31]{1,0:T(8,128)(2,1)S(1)}, bf16[8,31]{1,0:T(8,128)(2,1)}, u32[]{:S(2)}) %copy-start.4) | copy-done | bytes 520
  2.1 0.9 %copy-done = s32[1,1,128,256]{3,2,1,0:T(8,128)S(1)} copy-done((s32[1,1,128,256]{3,2,1,0:T(8,128)S(1)}, s32[1,1,128,256]{3,2,1,0:T(8,128)}, u32[]{:S(2)}) %copy-start) | copy-done | bytes 131096
  3.0 0.8 %copy-done.1 = bf16[1,1,128,256]{3,2,1,0:T(8,128)(2,1)S(1)} copy-done((bf16[1,1,128,256]{3,2,1,0:T(8,128)(2,1)S(1)}, bf16[1,1,128,256]{3,2,1,0:T(8,128)(2,1)}, u32[]{:S(2)}) %copy-start.1) | copy-done | bytes 65560
  3.8 0.8 %copy-done.2 = bf16[1,1,128,256]{3,2,1,0:T(8,128)(2,1)S(1)} copy-done((bf16[1,1,128,256]{3,2,1,0:T(8,128)(2,1)S(1)}, bf16[1,1,128,256]{3,2,1,0:T(8,128)(2,1)}, u32[]{:S(2)}) %copy-start.2) | copy-done | bytes 65560
  4.7 1.7 %match.1 = (f32[128,256]{1,0:T(8,128)S(1)}, bf16[144,128]{1,0:T(8,128)(2,1)S(1)}, bf16[144,128]{1,0:T(8,128)(2,1)S(1)}, bf16[144,128]{1,0:T(8,128)(2,1)S(1)}, bf16[144,128]{1,0:T(8,128)(2,1)S(1)}) custom-call(bf16[128,256]{1,0:T(8,128)(2,1)S(1)} %bitcast.8, s32[128,256]{1,0:T(8,128)S(1)} %bitcast.7, bf16[128,256]{1,0:T(8,128)(2,1)S(1)} %bitcast.9, ...), custom_call_target="tpu_custom_call" | custom-call | tf_op jit(solution)/shard_map/match/pallas_call | solution.py:335
  6.4 3.1 %collective-permute-start = (bf16[144,128]{1,0:T(8,128)(2,1)S(1)}, bf16[144,128]{1,0:T(8,128)(2,1)S(1)}, u32[]{:S(2)}, u32[]{:S(2)}) collective-permute-start(bf16[144,128]{1,0:T(8,128)(2,1)S(1)} %get-tuple-element.16), channel_id=1, source_target_pairs={{0,8},{8,0},{16,24},{24,16},{1,9},{9,1},{17,25},{25,17},{2,10},{10... | collective-permute-start | bytes 110600 | tf_op jit(solution)/shard_map/ppermute | solution.py:321
  9.5 2.6 %collective-permute-start.1 = (bf16[144,128]{1,0:T(8,128)(2,1)S(1)}, bf16[144,128]{1,0:T(8,128)(2,1)S(1)}, u32[]{:S(2)}, u32[]{:S(2)}) collective-permute-start(bf16[144,128]{1,0:T(8,128)(2,1)S(1)} %get-tuple-element.17), channel_id=1, source_target_pairs={{0,16},{8,24},{16,0},{24,8},{1,17},{9,25},{17,1},{25,9},{2,18},{10... | collective-permute-start | bytes 110600 | tf_op jit(solution)/shard_map/ppermute | solution.py:321
  12.1 2.9 %collective-permute-done.1.r_2_ = bf16[144,128]{1,0:T(8,128)(2,1)S(1)} collective-permute-done((bf16[144,128]{1,0:T(8,128)(2,1)S(1)}, bf16[144,128]{1,0:T(8,128)(2,1)S(1)}, u32[]{:S(2)}, u32[]{:S(2)}) %collective-permute-start.1) | collective-permute-done | bytes 36896 | tf_op jit(solution)/shard_map/ppermute | solution.py:321
  15.0 2.8 %collective-permute-done.2.r_3_ = bf16[144,128]{1,0:T(8,128)(2,1)S(1)} collective-permute-done((bf16[144,128]{1,0:T(8,128)(2,1)S(1)}, bf16[144,128]{1,0:T(8,128)(2,1)S(1)}, u32[]{:S(2)}, u32[]{:S(2)}) %collective-permute-start.2) | collective-permute-done | bytes 36896 | tf_op jit(solution)/shard_map/ppermute | solution.py:321
  17.8 0.3 pick.1
  18.2 1.5 %collective-permute-start.4 = (bf16[304,128]{1,0:T(8,128)(2,1)S(1)}, bf16[304,128]{1,0:T(8,128)(2,1)S(1)}, u32[]{:S(2)}, u32[]{:S(2)}) collective-permute-start(bf16[304,128]{1,0:T(8,128)(2,1)S(1)} %get-tuple-element.20), channel_id=1, source_target_pairs={{0,2},{1,3},{2,4},{3,5},{4,6},{5,7},{6,0},{7,1},{8,10},{9,11},{10,... | collective-permute-start | bytes 233480 | tf_op jit(solution)/shard_map/ppermute | solution.py:325
  19.7 2.4 %collective-permute-start.5 = (bf16[32,128]{1,0:T(8,128)(2,1)S(1)}, bf16[32,128]{1,0:T(8,128)(2,1)S(1)}, u32[]{:S(2)}, u32[]{:S(2)}) collective-permute-start(bf16[32,128]{1,0:T(8,128)(2,1)S(1)} %get-tuple-element.21), channel_id=1, source_target_pairs={{0,3},{1,4},{2,5},{3,6},{4,7},{5,0},{6,1},{7,2},{8,11},{9,12},{10,... | collective-permute-start | bytes 24584 | tf_op jit(solution)/shard_map/ppermute | solution.py:325
  22.1 1.5 %collective-permute-done.5.r_6_ = bf16[32,128]{1,0:T(8,128)(2,1)S(1)} collective-permute-done((bf16[32,128]{1,0:T(8,128)(2,1)S(1)}, bf16[32,128]{1,0:T(8,128)(2,1)S(1)}, u32[]{:S(2)}, u32[]{:S(2)}) %collective-permute-start.5) | collective-permute-done | bytes 8224 | tf_op jit(solution)/shard_map/ppermute | solution.py:325
  23.6 0.7 %collective-permute-done.4.r_5_.r_6_ = bf16[304,128]{1,0:T(8,128)(2,1)S(1)} collective-permute-done((bf16[304,128]{1,0:T(8,128)(2,1)S(1)}, bf16[304,128]{1,0:T(8,128)(2,1)S(1)}, u32[]{:S(2)}, u32[]{:S(2)}) %collective-permute-start.4) | collective-permute-done | bytes 77856 | tf_op jit(solution)/shard_map/ppermute | solution.py:325
  24.2 1.2 %sum.1.r_0_ = bf16[256,128]{1,0:T(8,128)(2,1)S(1)} custom-call(bf16[144,128]{1,0:T(8,128)(2,1)S(1)} %get-tuple-element.15.r_0_.r_4_, bf16[144,128]{1,0:T(8,128)(2,1)S(1)} %collective-permute-done.r_1_, bf16[144,128]{1,0:T(8,128)(2,1)S(1)} %collective-permute-done.1.r_2_, bf16[144,128]{1,0:T(8,128)(2,1)S(1)} %collective-permute-done.2.r_3_, ...), custom_call_target="tpu_custom_call" | custom-call | tf_op jit(solution)/shard_map/sum/pallas_call | solution.py:351
  25.5 0.6 %collective-permute-start.8 = (bf16[256,128]{1,0:T(8,128)(2,1)S(1)}, bf16[256,128]{1,0:T(8,128)(2,1)S(1)}, u32[]{:S(2)}, u32[]{:S(2)}) collective-permute-start(bf16[256,128]{1,0:T(8,128)(2,1)S(1)} %sum.1.r_0_), channel_id=1, source_target_pairs={{0,24},{8,16},{16,8},{24,0},{1,25},{9,17},{17,9},{25,1},{2,26},{10... | collective-permute-start | bytes 196616 | tf_op jit(solution)/shard_map/ppermute | solution.py:321
  26.1 3.9 %collective-permute-start.6 = (bf16[256,128]{1,0:T(8,128)(2,1)S(1)}, bf16[256,128]{1,0:T(8,128)(2,1)S(1)}, u32[]{:S(2)}, u32[]{:S(2)}) collective-permute-start(bf16[256,128]{1,0:T(8,128)(2,1)S(1)} %sum.1.r_0_), channel_id=1, source_target_pairs={{0,8},{8,0},{16,24},{24,16},{1,9},{9,1},{17,25},{25,17},{2,10},{10... | collective-permute-start | bytes 196616 | tf_op jit(solution)/shard_map/ppermute | solution.py:321
  29.9 2.5 %collective-permute-done.8.r_3_ = bf16[256,128]{1,0:T(8,128)(2,1)S(1)} collective-permute-done((bf16[256,128]{1,0:T(8,128)(2,1)S(1)}, bf16[256,128]{1,0:T(8,128)(2,1)S(1)}, u32[]{:S(2)}, u32[]{:S(2)}) %collective-permute-start.8) | collective-permute-done | bytes 65568 | tf_op jit(solution)/shard_map/ppermute | solution.py:321
  32.4 1.8 %collective-permute-done.7.r_2_ = bf16[256,128]{1,0:T(8,128)(2,1)S(1)} collective-permute-done((bf16[256,128]{1,0:T(8,128)(2,1)S(1)}, bf16[256,128]{1,0:T(8,128)(2,1)S(1)}, u32[]{:S(2)}, u32[]{:S(2)}) %collective-permute-start.7) | collective-permute-done | bytes 65568 | tf_op jit(solution)/shard_map/ppermute | solution.py:321
  34.2 1.1 %cut.1 = (bf16[1024,128]{1,0:T(8,128)(2,1)}, bf16[128,128]{1,0:T(8,128)(2,1)S(1)}, bf16[144,128]{1,0:T(8,128)(2,1)S(1)}, bf16[144,128]{1,0:T(8,128)(2,1)S(1)}, bf16[16,128]{1,0:T(8,128)(2,1)S(1)}) custom-call(bf16[256,128]{1,0:T(8,128)(2,1)S(1)} %sum.1.r_0_, bf16[256,128]{1,0:T(8,128)(2,1)S(1)} %collective-permute-done.6.r_1_, ...), custom_call_target="tpu_custom_call" | custom-call | tf_op jit(solution)/shard_map/cut/pallas_call | solution.py:355
  35.5 1.7 %collective-permute-start.10 = (bf16[144,128]{1,0:T(8,128)(2,1)S(1)}, bf16[144,128]{1,0:T(8,128)(2,1)S(1)}, u32[]{:S(2)}, u32[]{:S(2)}) collective-permute-start(bf16[144,128]{1,0:T(8,128)(2,1)S(1)} %get-tuple-element.26), channel_id=1, source_target_pairs={{0,6},{1,7},{2,0},{3,1},{4,2},{5,3},{6,4},{7,5},{8,14},{9,15},{10,... | collective-permute-start | bytes 110600 | tf_op jit(solution)/shard_map/ppermute | solution.py:325
  37.2 3.0 %collective-permute-done.11.r_4_ = bf16[16,128]{1,0:T(8,128)(2,1)S(1)} collective-permute-done((bf16[16,128]{1,0:T(8,128)(2,1)S(1)}, bf16[16,128]{1,0:T(8,128)(2,1)S(1)}, u32[]{:S(2)}, u32[]{:S(2)}) %collective-permute-start.11) | collective-permute-done | bytes 4128 | tf_op jit(solution)/shard_map/ppermute | solution.py:325
  40.2 1.4 %subtract.1 = bf16[128,256]{1,0:T(8,128)(2,1)} custom-call(f32[128,256]{1,0:T(8,128)S(1)} %get-tuple-element.23.r_0_, bf16[128,128]{1,0:T(8,128)(2,1)S(1)} %get-tuple-element.24.r_1_, bf16[144,128]{1,0:T(8,128)(2,1)S(1)} %collective-permute-done.9.r_2_, bf16[144,128]{1,0:T(8,128)(2,1)S(1)} %collective-permute-done.10.r_3_, ...), custom_call_target="tpu_custom_call" | custom-call | tf_op jit(solution)/shard_map/subtract/pallas_call | solution.py:362
  (20 shorter events, 0.3 us)
Async XLA Ops:
  1.4 0.7 %copy-start.4 = (bf16[8,31]{1,0:T(8,128)(2,1)S(1)}, bf16[8,31]{1,0:T(8,128)(2,1)}, u32[]{:S(2)}) copy-start(bf16[8,31]{1,0:T(8,128)(2,1)} %r_5_.1) | copy-start | bytes 1492
  1.4 0.7 %copy-start.3 = (bf16[8,31]{1,0:T(8,128)(2,1)S(1)}, bf16[8,31]{1,0:T(8,128)(2,1)}, u32[]{:S(2)}) copy-start(bf16[8,31]{1,0:T(8,128)(2,1)} %r_4_.1) | copy-start | bytes 1492
  1.4 0.7 %copy-start.5 = (s32[1,1,16,1]{2,3,1,0:T(1,128)S(1)}, s32[1,1,16,1]{2,3,1,0:T(1,128)}, u32[]{:S(2)}) copy-start(s32[1,1,16,1]{2,3,1,0:T(1,128)} %param.14) | copy-start | bytes 196
  1.4 0.7 %copy-start.6 = (s32[1,1,16]{2,1,0:T(1,128)S(1)}, s32[1,1,16]{2,1,0:T(1,128)}, u32[]{:S(2)}) copy-start(s32[1,1,16]{2,1,0:T(1,128)} %param.15) | copy-start | bytes 196
  2.1 0.9 %copy-start = (s32[1,1,128,256]{3,2,1,0:T(8,128)S(1)}, s32[1,1,128,256]{3,2,1,0:T(8,128)}, u32[]{:S(2)}) copy-start(s32[1,1,128,256]{3,2,1,0:T(8,128)} %param.9) | copy-start | bytes 393220
  3.0 0.8 %copy-start.1 = (bf16[1,1,128,256]{3,2,1,0:T(8,128)(2,1)S(1)}, bf16[1,1,128,256]{3,2,1,0:T(8,128)(2,1)}, u32[]{:S(2)}) copy-start(bf16[1,1,128,256]{3,2,1,0:T(8,128)(2,1)} %param.8) | copy-start | bytes 196612
  3.8 0.8 %copy-start.2 = (bf16[1,1,128,256]{3,2,1,0:T(8,128)(2,1)S(1)}, bf16[1,1,128,256]{3,2,1,0:T(8,128)(2,1)}, u32[]{:S(2)}) copy-start(bf16[1,1,128,256]{3,2,1,0:T(8,128)(2,1)} %param.10) | copy-start | bytes 196612
  6.4 5.7 %collective-permute-start = (bf16[144,128]{1,0:T(8,128)(2,1)S(1)}, bf16[144,128]{1,0:T(8,128)(2,1)S(1)}, u32[]{:S(2)}, u32[]{:S(2)}) collective-permute-start(bf16[144,128]{1,0:T(8,128)(2,1)S(1)} %get-tuple-element.16), channel_id=1, source_target_pairs={{0,8},{8,0},{16,24},{24,16},{1,9},{9,1},{17,25},{25,17},{2,10},{10... | collective-permute-start | bytes 110600 | tf_op jit(solution)/shard_map/ppermute | solution.py:321
  9.5 5.5 %collective-permute-start.1 = (bf16[144,128]{1,0:T(8,128)(2,1)S(1)}, bf16[144,128]{1,0:T(8,128)(2,1)S(1)}, u32[]{:S(2)}, u32[]{:S(2)}) collective-permute-start(bf16[144,128]{1,0:T(8,128)(2,1)S(1)} %get-tuple-element.17), channel_id=1, source_target_pairs={{0,16},{8,24},{16,0},{24,8},{1,17},{9,25},{17,1},{25,9},{2,18},{10... | collective-permute-start | bytes 110600 | tf_op jit(solution)/shard_map/ppermute | solution.py:321
  12.1 5.8 %collective-permute-start.2 = (bf16[144,128]{1,0:T(8,128)(2,1)S(1)}, bf16[144,128]{1,0:T(8,128)(2,1)S(1)}, u32[]{:S(2)}, u32[]{:S(2)}) collective-permute-start(bf16[144,128]{1,0:T(8,128)(2,1)S(1)} %get-tuple-element.18), channel_id=1, source_target_pairs={{0,24},{8,16},{16,8},{24,0},{1,25},{9,17},{17,9},{25,1},{2,26},{10... | collective-permute-start | bytes 110600 | tf_op jit(solution)/shard_map/ppermute | solution.py:321
  18.1 5.5 %collective-permute-start.3 = (bf16[304,128]{1,0:T(8,128)(2,1)S(1)}, bf16[304,128]{1,0:T(8,128)(2,1)S(1)}, u32[]{:S(2)}, u32[]{:S(2)}) collective-permute-start(bf16[304,128]{1,0:T(8,128)(2,1)S(1)} %get-tuple-element.19), channel_id=1, source_target_pairs={{0,1},{1,2},{2,3},{3,4},{4,5},{5,6},{6,7},{7,0},{8,9},{9,10},{10,1... | collective-permute-start | bytes 233480 | tf_op jit(solution)/shard_map/ppermute | solution.py:325
  18.2 6.1 %collective-permute-start.4 = (bf16[304,128]{1,0:T(8,128)(2,1)S(1)}, bf16[304,128]{1,0:T(8,128)(2,1)S(1)}, u32[]{:S(2)}, u32[]{:S(2)}) collective-permute-start(bf16[304,128]{1,0:T(8,128)(2,1)S(1)} %get-tuple-element.20), channel_id=1, source_target_pairs={{0,2},{1,3},{2,4},{3,5},{4,6},{5,7},{6,0},{7,1},{8,10},{9,11},{10,... | collective-permute-start | bytes 233480 | tf_op jit(solution)/shard_map/ppermute | solution.py:325
  19.7 3.9 %collective-permute-start.5 = (bf16[32,128]{1,0:T(8,128)(2,1)S(1)}, bf16[32,128]{1,0:T(8,128)(2,1)S(1)}, u32[]{:S(2)}, u32[]{:S(2)}) collective-permute-start(bf16[32,128]{1,0:T(8,128)(2,1)S(1)} %get-tuple-element.21), channel_id=1, source_target_pairs={{0,3},{1,4},{2,5},{3,6},{4,7},{5,0},{6,1},{7,2},{8,11},{9,12},{10,... | collective-permute-start | bytes 24584 | tf_op jit(solution)/shard_map/ppermute | solution.py:325
  25.5 6.9 %collective-permute-start.8 = (bf16[256,128]{1,0:T(8,128)(2,1)S(1)}, bf16[256,128]{1,0:T(8,128)(2,1)S(1)}, u32[]{:S(2)}, u32[]{:S(2)}) collective-permute-start(bf16[256,128]{1,0:T(8,128)(2,1)S(1)} %sum.1.r_0_), channel_id=1, source_target_pairs={{0,24},{8,16},{16,8},{24,0},{1,25},{9,17},{17,9},{25,1},{2,26},{10... | collective-permute-start | bytes 196616 | tf_op jit(solution)/shard_map/ppermute | solution.py:321
  26.0 8.1 %collective-permute-start.7 = (bf16[256,128]{1,0:T(8,128)(2,1)S(1)}, bf16[256,128]{1,0:T(8,128)(2,1)S(1)}, u32[]{:S(2)}, u32[]{:S(2)}) collective-permute-start(bf16[256,128]{1,0:T(8,128)(2,1)S(1)} %sum.1.r_0_), channel_id=1, source_target_pairs={{0,16},{8,24},{16,0},{24,8},{1,17},{9,25},{17,1},{25,9},{2,18},{10... | collective-permute-start | bytes 196616 | tf_op jit(solution)/shard_map/ppermute | solution.py:321
  26.1 8.1 %collective-permute-start.6 = (bf16[256,128]{1,0:T(8,128)(2,1)S(1)}, bf16[256,128]{1,0:T(8,128)(2,1)S(1)}, u32[]{:S(2)}, u32[]{:S(2)}) collective-permute-start(bf16[256,128]{1,0:T(8,128)(2,1)S(1)} %sum.1.r_0_), channel_id=1, source_target_pairs={{0,8},{8,0},{16,24},{24,16},{1,9},{9,1},{17,25},{25,17},{2,10},{10... | collective-permute-start | bytes 196616 | tf_op jit(solution)/shard_map/ppermute | solution.py:321
  35.3 4.9 %collective-permute-start.9 = (bf16[144,128]{1,0:T(8,128)(2,1)S(1)}, bf16[144,128]{1,0:T(8,128)(2,1)S(1)}, u32[]{:S(2)}, u32[]{:S(2)}) collective-permute-start(bf16[144,128]{1,0:T(8,128)(2,1)S(1)} %get-tuple-element.25), channel_id=1, source_target_pairs={{0,7},{1,0},{2,1},{3,2},{4,3},{5,4},{6,5},{7,6},{8,15},{9,8},{10,9... | collective-permute-start | bytes 110600 | tf_op jit(solution)/shard_map/ppermute | solution.py:325
  35.5 4.7 %collective-permute-start.10 = (bf16[144,128]{1,0:T(8,128)(2,1)S(1)}, bf16[144,128]{1,0:T(8,128)(2,1)S(1)}, u32[]{:S(2)}, u32[]{:S(2)}) collective-permute-start(bf16[144,128]{1,0:T(8,128)(2,1)S(1)} %get-tuple-element.26), channel_id=1, source_target_pairs={{0,6},{1,7},{2,0},{3,1},{4,2},{5,3},{6,4},{7,5},{8,14},{9,15},{10,... | collective-permute-start | bytes 110600 | tf_op jit(solution)/shard_map/ppermute | solution.py:325
  37.2 3.0 %collective-permute-start.11 = (bf16[16,128]{1,0:T(8,128)(2,1)S(1)}, bf16[16,128]{1,0:T(8,128)(2,1)S(1)}, u32[]{:S(2)}, u32[]{:S(2)}) collective-permute-start(bf16[16,128]{1,0:T(8,128)(2,1)S(1)} %get-tuple-element.27), channel_id=1, source_target_pairs={{0,5},{1,6},{2,7},{3,0},{4,1},{5,2},{6,3},{7,4},{8,13},{9,14},{10,... | collective-permute-start | bytes 12296 | tf_op jit(solution)/shard_map/ppermute | solution.py:325

commit v2 on v1

--- a/solution.py
+++ b/solution.py
@@ -47,17 +47,24 @@
     return (target - tile + tiles) % tiles, offset
 
 
-def match_body(
-    exps, tiles, sci_ref, mask_ref, var_ref, poly_ref, brow_ref, bcol_ref, dest_ref, off_ref,
-    matched_ref, *z_refs,
-):
+def match_body(exps, tiles, *refs):
+    args, matched_ref, z_refs = refs[:8], refs[8], refs[9 : 9 + exps]
+    held, sems = refs[9 + exps : 17 + exps], refs[17 + exps]
+    copies = [pltpu.make_async_copy(a, h, sems.at[i]) for i, (a, h) in enumerate(zip(args, held))]
+    for copy in copies:
+        copy.start()
+    brow_ref, bcol_ref, sci_ref, poly_ref, mask_ref, var_ref, dest_ref, off_ref = held
     exp, tile = lax.axis_index("exp"), lax.axis_index("tile")
     height, across = sci_ref.shape
     bases = brow_ref.shape[0]
+    copies[0].wait()
+    copies[1].wait()
     d = iota((PC, PC), 1) - iota((PC, PC), 0)
     zero = jnp.zeros((PC, PC), F32)
     cols = circulant(bcol_ref[...], True)
     rows = circulant(brow_ref[...], False)
+    copies[2].wait()
+    copies[3].wait()
     sci = sci_ref[...]
     y = (iota((height, across), 0).astype(F32) - (height - 1) / 2.0) / (height / 2.0)
     x = (iota((height, across), 1).astype(F32) - (across - 1) / 2.0) / (across / 2.0)
@@ -72,8 +79,10 @@
         first = dot(sci, band).astype(BF16)
         row_band = jnp.where(jnp.abs(d) < PC // 2, rows[b], zero).astype(BF16)
         second = dot(row_band, first)
-        matched += (poly_ref[b, 0] + poly_ref[b, 1] * y + poly_ref[b, 2] * x) * second
+        matched += (poly_ref[0, 0, 0, b] + poly_ref[0, 1, 0, b] * y + poly_ref[0, 2, 0, b] * x) * second
     matched_ref[...] = matched
+    for copy in copies[4:]:
+        copy.wait()
     rejected = jnp.bitwise_and(mask_ref[...], 7) != 0
     weight = jnp.where(rejected, 0.0, 1.0 / var_ref[...].astype(F32))
     weighted = matched * weight
@@ -167,13 +176,19 @@
     return -(-2 * exps // PR)
 
 
-def sum_body(exps, *refs):
-    z_refs, (m1_ref, m2_ref, m3_ref, out_ref) = refs[:exps], refs[exps:]
+def hot_sums(places, data, row_count, q):
+    row = iota((row_count, PC), 0) + row_count * q
+    return [
+        dot(jnp.concatenate([jnp.where(row == v, 1.0, 0.0).astype(BF16) for v in vs], 1), data)
+        for vs in places
+    ]
+
+
+def own_body(exps, *refs):
+    z_refs, out_ref = refs[:exps], refs[exps]
     height = z_refs[0].shape[0] - PR
     half = height // 2
-    share, span = shares(exps)
-    base = half * exps
-    tiles = meta_tiles(exps)
+    _, span = shares(exps)
     first_half = iota((1, PC), 1) < half
     data = []
     places = ([], [])
@@ -185,7 +200,22 @@
             for m in metas:
                 hi, lo, step = (m[3 * c + i : 3 * c + i + 1] for i in range(3))
                 pos.append(jnp.where(step == 0.0, hi * 32.0 + lo, -1.0))
-            places[c].append(jnp.where(first_half, pos[0], pltpu.roll(pos[1], half, 1)))
+            pos = jnp.where(first_half, pos[0], pltpu.roll(pos[1], half, 1))
+            places[c].append(pos.astype(jnp.int32))
+    data = jnp.concatenate(data, 0)
+    rows = TR // exps
+    odd = (iota((rows, PC), 1) // span) % 2 == 1
+    for q in range(exps):
+        both = hot_sums(places, data, rows, q)
+        out_ref[rows * q : rows * (q + 1)] = jnp.where(odd, both[1], both[0])
+
+
+def sum_body(exps, own_ref, m1_ref, m2_ref, m3_ref, out_ref):
+    share, span = shares(exps)
+    tiles = meta_tiles(exps)
+    base = m1_ref.shape[0] - PR * tiles - 2 * PR
+    data = []
+    places = ([], [])
     for ref in (m1_ref, m2_ref):
         data.append(ref[0:base])
         for p in range(exps // 2):
@@ -193,7 +223,7 @@
             m = ref[base + PR * tile_at : base + PR * (tile_at + 1)].astype(F32)
             for c in range(2):
                 at = row + 2 * c
-                places[c].append(m[at : at + 1] * 32.0 + m[at + 1 : at + 2])
+                places[c].append((m[at : at + 1] * 32.0 + m[at + 1 : at + 2]).astype(jnp.int32))
     data = jnp.concatenate(data, 0)
     at = base + PR * tiles
     spill = jnp.zeros((PR, PC), F32)
@@ -204,16 +234,9 @@
     group = iota((rows, PC), 1) // span
     owned = iota((rows, PC), 1) // share
     packed = jnp.zeros((rows, PC), F32)
-    places = [[v.astype(jnp.int32) for v in vs] for vs in places]
     for q in range(exps):
-        row = iota((rows, PC), 0) + rows * q
-        both = []
-        for c in range(2):
-            hot = jnp.concatenate(
-                [jnp.where(row == v, 1.0, 0.0).astype(BF16) for v in places[c]], 1
-            )
-            both.append(dot(hot, data))
-        total = jnp.where(group % 2 == 1, both[1], both[0])
+        both = hot_sums(places, data, rows, q)
+        total = jnp.where(group % 2 == 1, both[1], both[0]) + own_ref[rows * q : rows * (q + 1)]
         if q == 0:
             total = jnp.concatenate([total[:PR] + spill, total[PR:]], 0)
         total += pltpu.roll(total, PC - span, 1)
@@ -224,15 +247,9 @@
     out_ref[...] = packed.astype(BF16)
 
 
-def cut_body(exps, *refs):
-    packed_refs = refs[:exps]
-    z_ref, m1_ref, m2_ref = refs[exps : exps + 3]
-    template_ref, own_ref, n1_ref, n2_ref, n3_ref = refs[exps + 3 :]
+def unpack(exps, packed_refs):
     exp = lax.axis_index("exp")
-    height = z_ref.shape[0] - PR
-    half = height // 2
     share, _ = shares(exps)
-    base = half * exps
     rows = TR // exps
     lane = iota((rows, PC), 1) // share
     packed = [r[...].astype(F32) for r in packed_refs]
@@ -244,8 +261,22 @@
             moved = pltpu.roll(packed[k], (PC + share * (j - q)) % PC, 1)
             block = jnp.where(lane == j, moved, block)
         blocks.append(block.astype(BF16))
-    template = jnp.concatenate(blocks, 0)
-    template_ref[...] = template
+    return blocks
+
+
+def template_body(exps, *refs):
+    rows = TR // exps
+    for q, block in enumerate(unpack(exps, refs[:exps])):
+        refs[exps][rows * q : rows * (q + 1)] = block
+
+
+def cut_body(exps, *refs):
+    template = jnp.concatenate(unpack(exps, refs[:exps]), 0)
+    z_ref, m1_ref, m2_ref = refs[exps : exps + 3]
+    own_ref, n1_ref, n2_ref, n3_ref = refs[exps + 3 :]
+    height = z_ref.shape[0] - PR
+    half = height // 2
+    base = half * exps
     sub16 = iota((PR, PC), 0)
     hots = []
     for ref, at, first, invalid in (
@@ -277,42 +308,44 @@
     n3_ref[...] = head
 
 
-def subtract_body(tiles, matched_ref, own_ref, n1_ref, n2_ref, n3_ref, dest_ref, off_ref, out_ref):
-    tile = lax.axis_index("tile")
+def subtract_body(matched_ref, own_ref, n1_ref, n2_ref, n3_ref, z_ref, out_ref):
     height = own_ref.shape[0]
     half = height // 2
-    lane = iota((PR, PC), 1)
-    sub = iota((PR, PC), 0)
+    lane = iota((height, PC), 1)
+    sub16 = iota((PR, PC), 0)
+    top = iota((height, PC), 0) < half
+    meta = z_ref[height : height + PR]
     heads = [n1_ref[height : height + PR], n2_ref[height : height + PR], n3_ref[...]]
     heads.append(jnp.zeros((PC - REACH * PR, PC), BF16))
     heads = jnp.concatenate(heads, 0)
     for c in range(2):
-        hots, backs = [], []
-        for rb in range(height // PR):
-            rel, offset = piece_scalars(dest_ref, off_ref, 2 * rb + c, tile, tiles)
-            at = half * c + (PR * rb) % half
-            middle = n1_ref[at : at + PR].astype(F32)
-            if PR * rb < half:
-                backs.append(jnp.where(rel == 0, own_ref[at : at + PR].astype(F32), middle))
-            else:
-                backs.append(jnp.where(rel == 2, n2_ref[at : at + PR].astype(F32), middle))
-            over = sub + (offset - TR)
-            hots.append(jnp.where((over >= 0) & (lane == over + PR * rel), 1.0, 0.0).astype(BF16))
-        back = jnp.concatenate(backs, 0) + dot(jnp.concatenate(hots, 0), heads)
+        scale = jnp.where(sub16 == 3 * c, 32.0, jnp.where(sub16 == 3 * c + 1, 1.0, 0.0))
+        over = dot(meta, scale.astype(BF16), 0, 0) - TR
+        step = dot(meta, jnp.where(sub16 == 3 * c + 2, 1.0, 0.0).astype(BF16), 0, 0)
+        at = jnp.where(over >= 0.0, over + PR * step, -1.0).astype(jnp.int32)
+        own, mid, far = (r[half * c : half * (c + 1)].astype(F32) for r in (own_ref, n1_ref, n2_ref))
+        inner = jnp.concatenate([mid, mid], 0)
+        outer = jnp.concatenate([own, far], 0)
+        back = jnp.where(step == jnp.where(top, 0.0, 2.0), outer, inner)
+        back += dot(jnp.where(lane == at, 1.0, 0.0).astype(BF16), heads)
         out_ref[:, PC * c : PC * (c + 1)] = (matched_ref[:, PC * c : PC * (c + 1)] - back).astype(BF16)
 
 
 VM = pl.BlockSpec(memory_space=pltpu.VMEM)
-SM = pl.BlockSpec(memory_space=pltpu.SMEM)
-
-
-def call(body, outs, specs, name):
+HBM = pl.BlockSpec(memory_space=pltpu.HBM)
+
+
+def call(body, outs, specs, name, scratch=(), micros=1):
     return pl.pallas_call(
         body,
         out_shape=tuple(jax.ShapeDtypeStruct(s, t) for s, t in outs),
         in_specs=specs,
         out_specs=tuple(VM for _ in outs),
+        scratch_shapes=scratch,
         compiler_params=PARAMS,
+        cost_estimate=pl.CostEstimate(
+            flops=micros * 10**9, bytes_accessed=micros * 10**6, transcendentals=0
+        ),
         name=name,
     )
 
@@ -328,41 +361,47 @@
 def program_of(exps, tiles):
     def body(science, mask_bits, variance, kernel_poly, basis_rows, basis_cols, destination, row_offset):
         height, across = science.shape[2:]
-        bases = basis_rows.shape[0]
         half = height // 2
-        dest, off = destination.reshape(-1), row_offset.reshape(-1)
         message = ((height + PR, PC), BF16)
+        args = (
+            basis_rows, basis_cols, science.reshape(height, across),
+            jnp.transpose(kernel_poly, (0, 3, 1, 2)), mask_bits.reshape(height, across),
+            variance.reshape(height, across), destination.reshape(-1), row_offset.reshape(-1),
+        )
+        args = tuple(pltpu.with_memory_space_constraint(a, pltpu.HBM) for a in args)
+        small = (3, 6, 7)
         matched, *z = call(
             lambda *r: match_body(exps, tiles, *r),
             [((height, across), F32)] + [message] * exps,
-            [VM, VM, VM, SM, VM, VM, SM, SM],
+            [HBM] * len(args),
             "match",
-        )(
-            science.reshape(height, across), mask_bits.reshape(height, across),
-            variance.reshape(height, across), kernel_poly.reshape(bases, 3),
-            basis_rows, basis_cols, dest, off,
-        )
+            [(pltpu.SMEM if i in small else pltpu.VMEM)(a.shape, a.dtype) for i, a in enumerate(args)]
+            + [pltpu.SemaphoreType.DMA((len(args),))],
+        )(*args)
         z = [z[0]] + [along_exp(z[k], k, exps) for k in range(1, exps)]
         big = ((half * exps + PR * meta_tiles(exps) + 2 * PR, PC), BF16)
         m1, m2, m3 = call(
             lambda *r: pick_body(exps, *r), [big, big, ((2 * PR, PC), BF16)], [VM] * exps, "pick"
         )(*z)
         m1, m2, m3 = (along_tile(m, i + 1, tiles) for i, m in enumerate((m1, m2, m3)))
+        (own,) = call(lambda *r: own_body(exps, *r), [((TR, PC), F32)], [VM] * exps, "own")(*z)
         (packed,) = call(
-            lambda *r: sum_body(exps, *r), [((TR // exps, PC), BF16)], [VM] * (exps + 3), "sum"
-        )(*z, m1, m2, m3)
-        all_packed = [packed] + [along_exp(packed, k, exps) for k in range(1, exps)]
-        template, own, n1, n2, n3 = call(
+            lambda *r: sum_body(exps, *r), [((TR // exps, PC), BF16)], [VM] * 4, "sum"
+        )(own, m1, m2, m3)
+        packed = [packed] + [along_exp(packed, k, exps) for k in range(1, exps)]
+        own, n1, n2, n3 = call(
             lambda *r: cut_body(exps, *r),
-            [((TR, PC), BF16), ((height, PC), BF16), message, message, ((PR, PC), BF16)],
+            [((height, PC), BF16), message, message, ((PR, PC), BF16)],
             [VM] * (exps + 3),
             "cut",
-        )(*all_packed, z[0], m1, m2)
+        )(*packed, z[0], m1, m2)
         n1, n2, n3 = (along_tile(n, -1 - i, tiles) for i, n in enumerate((n1, n2, n3)))
+        (template,) = call(
+            lambda *r: template_body(exps, *r), [((TR, PC), BF16)], [VM] * exps, "template"
+        )(*packed)
         (difference,) = call(
-            lambda *r: subtract_body(tiles, *r), [((height, across), BF16)],
-            [VM] * 5 + [SM] * 2, "subtract",
-        )(matched, own, n1, n2, n3, dest, off)
+            subtract_body, [((height, across), BF16)], [VM] * 6, "subtract"
+        )(matched, own, n1, n2, n3, z[0])
         return template, difference[None, None]
 
     return body

time: 41.9 us -> 38.8 us (0.926)
  local copies, waits for them, and re-layouts: 4.03 us -> 0 us
  Pallas kernels: 5.68 us -> 6.52 us
  starting transfers between devices: 16 us -> 16.8 us
  waiting for transfers between devices: 15.2 us -> 14.6 us
    unnamed x14 -> x0, local copies, waits for them, and re-layouts: 3.28 us -> none
    ppermute x6, waiting for transfers between devices: 10 us -> 8.43 us  [along_exp(): return lax.ppermute(x, 'exp', [(i, i ^ k) for i in range(exps)])]
    ppermute x6, waiting for transfers between devices: 5.18 us -> 6.2 us  [along_tile(): lax.ppermute(x, 'tile', [(i, (i + by) % tiles) for i in range(tiles)])]
    ppermute x6, starting transfers between devices: 5.84 us -> 6.64 us  [along_tile(): lax.ppermute(x, 'tile', [(i, (i + by) % tiles) for i in range(tiles)])]
    reshape x1 -> x0, local copies, waits for them, and re-layouts: 0.76 us -> none  [body(): kernel_poly.reshape(bases, 3)]
    pallas_call x3 -> x5, Pallas kernels: 3.73 us -> 4.17 us  [the longest x1 1.09 us: body(): call(subtract_body, [((height, across), BF16)], [VM] * 6, 'subtract')]
  transfers between devices with their start and end apart: 12 -> 12, of which waited for: 7 -> 8; matrix products, arithmetic and copies ran while one was open for 0% -> 0% of each run, Pallas kernels for 0% -> 4%
where the time goes in v2:
time: 38.8 us; the launch traced here: 38.6 us
  starting transfers between devices  16.8 us (43%)
  waiting for transfers between devices  14.6 us (38%)
  Pallas kernels  6.52 us (17%)
  between operations  0.69 us (2%)
    ppermute x6, starting transfers between devices, along_exp(): return lax.ppermute(x, 'exp', [(i, i ^ k) for i in range(exps)])  10.2 us
    ppermute x6, waiting for transfers between devices, along_exp(): return lax.ppermute(x, 'exp', [(i, i ^ k) for i in range(exps)])  8.43 us
    ppermute x6, starting transfers between devices, along_tile(): lax.ppermute(x, 'tile', [(i, (i + by) % tiles) for i in range(tiles)])  6.64 us
    ppermute x6, waiting for transfers between devices, along_tile(): lax.ppermute(x, 'tile', [(i, (i + by) % tiles) for i in range(tiles)])  6.2 us
    pallas_call x1, Pallas kernels, body(): call(lambda *r: match_body(exps, tiles, *r), [((height, across), F32)] +...  2.07 us
    pallas_call x1, Pallas kernels, body(): call(subtract_body, [((height, across), BF16)], [VM] * 6, 'subtract')  1.09 us
    pallas_call x1, Pallas kernels, body(): call(lambda *r: template_body(exps, *r), [((TR, PC), BF16)], [VM] * exps,...  1.04 us
    pallas_call x1, Pallas kernels, body(): call(lambda *r: sum_body(exps, *r), [((TR // exps, PC), BF16)], [VM] * 4,...  0.91 us
  transfers between devices with their start and end apart: 12, of which 8 were waited for; matrix products, arithmetic and copies ran while one was open for 0% of the time, Pallas kernels for 4%

profile of v2, /device:TPU:0, one launch (start us, length us, event | category | flops | bytes accessed | tf_op | source)
XLA Modules:
  0.0 38.6 jit_solution(15821313264819023592)
XLA Ops:
  0.6 2.1 %match.1 = (f32[128,256]{1,0:T(8,128)S(1)}, bf16[144,128]{1,0:T(8,128)(2,1)S(1)}, bf16[144,128]{1,0:T(8,128)(2,1)S(1)}, bf16[144,128]{1,0:T(8,128)(2,1)S(1)}, bf16[144,128]{1,0:T(8,128)(2,1)S(1)}) custom-call(bf16[8,31]{1,0:T(8,128)(2,1)} %r_0_.1, bf16[8,31]{1,0:T(8,128)(2,1)} %r_1_.1, bf16[128,256]{1,0:T(8,128)(2,1)} %bitcast.8, f32[1,3,1,8]{3,2,1,0:T(1,128)} %bitcast.10, ...), custom_call_target="tpu_custom_call" | custom-call | flops 1000000000 | bytes 1000000 | tf_op jit(solution)/shard_map/match/pallas_call | solution.py:373
  2.7 3.1 %collective-permute-start = (bf16[144,128]{1,0:T(8,128)(2,1)S(1)}, bf16[144,128]{1,0:T(8,128)(2,1)S(1)}, u32[]{:S(2)}, u32[]{:S(2)}) collective-permute-start(bf16[144,128]{1,0:T(8,128)(2,1)S(1)} %get-tuple-element.15), channel_id=1, source_target_pairs={{0,8},{8,0},{16,24},{24,16},{1,9},{9,1},{17,25},{25,17},{2,10},{10... | collective-permute-start | bytes 110600 | tf_op jit(solution)/shard_map/ppermute | solution.py:354
  5.8 2.6 %collective-permute-start.1 = (bf16[144,128]{1,0:T(8,128)(2,1)S(1)}, bf16[144,128]{1,0:T(8,128)(2,1)S(1)}, u32[]{:S(2)}, u32[]{:S(2)}) collective-permute-start(bf16[144,128]{1,0:T(8,128)(2,1)S(1)} %get-tuple-element.16), channel_id=1, source_target_pairs={{0,16},{8,24},{16,0},{24,8},{1,17},{9,25},{17,1},{25,9},{2,18},{10... | collective-permute-start | bytes 110600 | tf_op jit(solution)/shard_map/ppermute | solution.py:354
  8.4 2.9 %collective-permute-done.1.r_2_ = bf16[144,128]{1,0:T(8,128)(2,1)S(1)} collective-permute-done((bf16[144,128]{1,0:T(8,128)(2,1)S(1)}, bf16[144,128]{1,0:T(8,128)(2,1)S(1)}, u32[]{:S(2)}, u32[]{:S(2)}) %collective-permute-start.1) | collective-permute-done | bytes 36896 | tf_op jit(solution)/shard_map/ppermute | solution.py:354
  11.4 2.8 %collective-permute-done.2.r_3_ = bf16[144,128]{1,0:T(8,128)(2,1)S(1)} collective-permute-done((bf16[144,128]{1,0:T(8,128)(2,1)S(1)}, bf16[144,128]{1,0:T(8,128)(2,1)S(1)}, u32[]{:S(2)}, u32[]{:S(2)}) %collective-permute-start.2) | collective-permute-done | bytes 36896 | tf_op jit(solution)/shard_map/ppermute | solution.py:354
  14.2 0.3 pick.1
  14.5 0.1 collective-permute-start.5
  14.5 1.6 %collective-permute-start.3 = (bf16[304,128]{1,0:T(8,128)(2,1)S(1)}, bf16[304,128]{1,0:T(8,128)(2,1)S(1)}, u32[]{:S(2)}, u32[]{:S(2)}) collective-permute-start(bf16[304,128]{1,0:T(8,128)(2,1)S(1)} %get-tuple-element.18), channel_id=1, source_target_pairs={{0,1},{1,2},{2,3},{3,4},{4,5},{5,6},{6,7},{7,0},{8,9},{9,10},{10,1... | collective-permute-start | bytes 233480 | tf_op jit(solution)/shard_map/ppermute | solution.py:358
  16.1 1.5 %collective-permute-start.4 = (bf16[304,128]{1,0:T(8,128)(2,1)S(1)}, bf16[304,128]{1,0:T(8,128)(2,1)S(1)}, u32[]{:S(2)}, u32[]{:S(2)}) collective-permute-start(bf16[304,128]{1,0:T(8,128)(2,1)S(1)} %get-tuple-element.19), channel_id=1, source_target_pairs={{0,2},{1,3},{2,4},{3,5},{4,6},{5,7},{6,0},{7,1},{8,10},{9,11},{10,... | collective-permute-start | bytes 233480 | tf_op jit(solution)/shard_map/ppermute | solution.py:358
  17.6 0.5 %own.1.r_0_ = f32[1024,128]{1,0:T(8,128)S(1)} custom-call(bf16[144,128]{1,0:T(8,128)(2,1)S(1)} %get-tuple-element.14.r_0_.r_4_.z_ref, bf16[144,128]{1,0:T(8,128)(2,1)S(1)} %collective-permute-done.r_1_, bf16[144,128]{1,0:T(8,128)(2,1)S(1)} %collective-permute-done.1.r_2_, bf16[144,128]{1,0:T(8,128)(2,1)S(1)} %collective-permute-done.2.r_3_), custom_call_target="tpu_custom_call" | custom-call | flops 1000000000 | bytes 1000000 | tf_op jit(solution)/shard_map/own/pallas_call | solution.py:387
  18.1 1.2 %collective-permute-done.3.r_1_.r_5_ = bf16[304,128]{1,0:T(8,128)(2,1)S(1)} collective-permute-done((bf16[304,128]{1,0:T(8,128)(2,1)S(1)}, bf16[304,128]{1,0:T(8,128)(2,1)S(1)}, u32[]{:S(2)}, u32[]{:S(2)}) %collective-permute-start.3) | collective-permute-done | bytes 77856 | tf_op jit(solution)/shard_map/ppermute | solution.py:358
  19.4 2.1 %collective-permute-done.4.r_2_.r_6_ = bf16[304,128]{1,0:T(8,128)(2,1)S(1)} collective-permute-done((bf16[304,128]{1,0:T(8,128)(2,1)S(1)}, bf16[304,128]{1,0:T(8,128)(2,1)S(1)}, u32[]{:S(2)}, u32[]{:S(2)}) %collective-permute-start.4) | collective-permute-done | bytes 77856 | tf_op jit(solution)/shard_map/ppermute | solution.py:358
  21.4 0.9 %sum.1.r_0_ = bf16[256,128]{1,0:T(8,128)(2,1)S(1)} custom-call(f32[1024,128]{1,0:T(8,128)S(1)} %own.1.r_0_, bf16[304,128]{1,0:T(8,128)(2,1)S(1)} %collective-permute-done.3.r_1_.r_5_, bf16[304,128]{1,0:T(8,128)(2,1)S(1)} %collective-permute-done.4.r_2_.r_6_, bf16[32,128]{1,0:T(8,128)(2,1)S(1)} %collective-permute-done.5.r_3_), custom_call_target="tpu_custom_call" | custom-call | flops 1000000000 | bytes 1000000 | tf_op jit(solution)/shard_map/sum/pallas_call | solution.py:388
  22.4 0.6 %collective-permute-start.8 = (bf16[256,128]{1,0:T(8,128)(2,1)S(1)}, bf16[256,128]{1,0:T(8,128)(2,1)S(1)}, u32[]{:S(2)}, u32[]{:S(2)}) collective-permute-start(bf16[256,128]{1,0:T(8,128)(2,1)S(1)} %sum.1.r_0_), channel_id=1, source_target_pairs={{0,24},{8,16},{16,8},{24,0},{1,25},{9,17},{17,9},{25,1},{2,26},{10... | collective-permute-start | bytes 196616 | tf_op jit(solution)/shard_map/ppermute | solution.py:354
  22.9 3.9 %collective-permute-start.6 = (bf16[256,128]{1,0:T(8,128)(2,1)S(1)}, bf16[256,128]{1,0:T(8,128)(2,1)S(1)}, u32[]{:S(2)}, u32[]{:S(2)}) collective-permute-start(bf16[256,128]{1,0:T(8,128)(2,1)S(1)} %sum.1.r_0_), channel_id=1, source_target_pairs={{0,8},{8,0},{16,24},{24,16},{1,9},{9,1},{17,25},{25,17},{2,10},{10... | collective-permute-start | bytes 196616 | tf_op jit(solution)/shard_map/ppermute | solution.py:354
  26.8 1.9 %collective-permute-done.8.r_3_ = bf16[256,128]{1,0:T(8,128)(2,1)S(1)} collective-permute-done((bf16[256,128]{1,0:T(8,128)(2,1)S(1)}, bf16[256,128]{1,0:T(8,128)(2,1)S(1)}, u32[]{:S(2)}, u32[]{:S(2)}) %collective-permute-start.8) | collective-permute-done | bytes 65568 | tf_op jit(solution)/shard_map/ppermute | solution.py:354
  28.7 0.8 %collective-permute-done.7.r_2_ = bf16[256,128]{1,0:T(8,128)(2,1)S(1)} collective-permute-done((bf16[256,128]{1,0:T(8,128)(2,1)S(1)}, bf16[256,128]{1,0:T(8,128)(2,1)S(1)}, u32[]{:S(2)}, u32[]{:S(2)}) %collective-permute-start.7) | collective-permute-done | bytes 65568 | tf_op jit(solution)/shard_map/ppermute | solution.py:354
  29.5 0.6 %cut.1 = (bf16[128,128]{1,0:T(8,128)(2,1)S(1)}, bf16[144,128]{1,0:T(8,128)(2,1)S(1)}, bf16[144,128]{1,0:T(8,128)(2,1)S(1)}, bf16[16,128]{1,0:T(8,128)(2,1)S(1)}) custom-call(bf16[256,128]{1,0:T(8,128)(2,1)S(1)} %sum.1.r_0_, bf16[256,128]{1,0:T(8,128)(2,1)S(1)} %collective-permute-done.6.r_1_, bf16[256,128]{1,0:T(8,128)(2,1)S(1)} %collective-permute-done.7.r_2_, ...), custom_call_target="tpu_custom_call" | custom-call | flops 1000000000 | bytes 1000000 | tf_op jit(solution)/shard_map/cut/pallas_call | solution.py:392
  30.1 1.4 %collective-permute-start.11 = (bf16[16,128]{1,0:T(8,128)(2,1)S(1)}, bf16[16,128]{1,0:T(8,128)(2,1)S(1)}, u32[]{:S(2)}, u32[]{:S(2)}) collective-permute-start(bf16[16,128]{1,0:T(8,128)(2,1)S(1)} %get-tuple-element.25), channel_id=1, source_target_pairs={{0,5},{1,6},{2,7},{3,0},{4,1},{5,2},{6,3},{7,4},{8,13},{9,14},{10,... | collective-permute-start | bytes 12296 | tf_op jit(solution)/shard_map/ppermute | solution.py:358
  31.5 2.1 %collective-permute-start.9 = (bf16[144,128]{1,0:T(8,128)(2,1)S(1)}, bf16[144,128]{1,0:T(8,128)(2,1)S(1)}, u32[]{:S(2)}, u32[]{:S(2)}) collective-permute-start(bf16[144,128]{1,0:T(8,128)(2,1)S(1)} %get-tuple-element.23), channel_id=1, source_target_pairs={{0,7},{1,0},{2,1},{3,2},{4,3},{5,4},{6,5},{7,6},{8,15},{9,8},{10,9... | collective-permute-start | bytes 110600 | tf_op jit(solution)/shard_map/ppermute | solution.py:358
  33.6 1.0 %template.1 = bf16[1024,128]{1,0:T(8,128)(2,1)} custom-call(bf16[256,128]{1,0:T(8,128)(2,1)S(1)} %sum.1.r_0_, bf16[256,128]{1,0:T(8,128)(2,1)S(1)} %collective-permute-done.6.r_1_, bf16[256,128]{1,0:T(8,128)(2,1)S(1)} %collective-permute-done.7.r_2_, bf16[256,128]{1,0:T(8,128)(2,1)S(1)} %collective-permute-done.8.r_3_), custom_call_target="tpu_custom_call" | custom-call | flops 1000000000 | bytes 1000000 | tf_op jit(solution)/shard_map/template/pallas_call | solution.py:399
  34.6 0.6 %collective-permute-done.9.n1_ref = bf16[144,128]{1,0:T(8,128)(2,1)S(1)} collective-permute-done((bf16[144,128]{1,0:T(8,128)(2,1)S(1)}, bf16[144,128]{1,0:T(8,128)(2,1)S(1)}, u32[]{:S(2)}, u32[]{:S(2)}) %collective-permute-start.9) | collective-permute-done | bytes 36896 | tf_op jit(solution)/shard_map/ppermute | solution.py:358
  35.2 2.3 %collective-permute-done.10.n2_ref = bf16[144,128]{1,0:T(8,128)(2,1)S(1)} collective-permute-done((bf16[144,128]{1,0:T(8,128)(2,1)S(1)}, bf16[144,128]{1,0:T(8,128)(2,1)S(1)}, u32[]{:S(2)}, u32[]{:S(2)}) %collective-permute-start.10) | collective-permute-done | bytes 36896 | tf_op jit(solution)/shard_map/ppermute | solution.py:358
  37.6 1.1 %subtract.1 = bf16[128,256]{1,0:T(8,128)(2,1)} custom-call(f32[128,256]{1,0:T(8,128)S(1)} %get-tuple-element.21.matched_ref, bf16[128,128]{1,0:T(8,128)(2,1)S(1)} %get-tuple-element.22.own_ref, bf16[144,128]{1,0:T(8,128)(2,1)S(1)} %collective-permute-done.9.n1_ref, bf16[144,128]{1,0:T(8,128)(2,1)S(1)} %collective-permute-done.10.n2_ref, ...), custom_call_target="tpu_custom_call" | custom-call | flops 1000000000 | bytes 1000000 | tf_op jit(solution)/shard_map/subtract/pallas_call | solution.py:402
  (7 shorter events, 0.0 us)
Async XLA Ops:
  2.7 5.7 %collective-permute-start = (bf16[144,128]{1,0:T(8,128)(2,1)S(1)}, bf16[144,128]{1,0:T(8,128)(2,1)S(1)}, u32[]{:S(2)}, u32[]{:S(2)}) collective-permute-start(bf16[144,128]{1,0:T(8,128)(2,1)S(1)} %get-tuple-element.15), channel_id=1, source_target_pairs={{0,8},{8,0},{16,24},{24,16},{1,9},{9,1},{17,25},{25,17},{2,10},{10... | collective-permute-start | bytes 110600 | tf_op jit(solution)/shard_map/ppermute | solution.py:354
  5.8 5.5 %collective-permute-start.1 = (bf16[144,128]{1,0:T(8,128)(2,1)S(1)}, bf16[144,128]{1,0:T(8,128)(2,1)S(1)}, u32[]{:S(2)}, u32[]{:S(2)}) collective-permute-start(bf16[144,128]{1,0:T(8,128)(2,1)S(1)} %get-tuple-element.16), channel_id=1, source_target_pairs={{0,16},{8,24},{16,0},{24,8},{1,17},{9,25},{17,1},{25,9},{2,18},{10... | collective-permute-start | bytes 110600 | tf_op jit(solution)/shard_map/ppermute | solution.py:354
  8.4 5.8 %collective-permute-start.2 = (bf16[144,128]{1,0:T(8,128)(2,1)S(1)}, bf16[144,128]{1,0:T(8,128)(2,1)S(1)}, u32[]{:S(2)}, u32[]{:S(2)}) collective-permute-start(bf16[144,128]{1,0:T(8,128)(2,1)S(1)} %get-tuple-element.17), channel_id=1, source_target_pairs={{0,24},{8,16},{16,8},{24,0},{1,25},{9,17},{17,9},{25,1},{2,26},{10... | collective-permute-start | bytes 110600 | tf_op jit(solution)/shard_map/ppermute | solution.py:354
  14.5 3.7 %collective-permute-start.5 = (bf16[32,128]{1,0:T(8,128)(2,1)S(1)}, bf16[32,128]{1,0:T(8,128)(2,1)S(1)}, u32[]{:S(2)}, u32[]{:S(2)}) collective-permute-start(bf16[32,128]{1,0:T(8,128)(2,1)S(1)} %get-tuple-element.20), channel_id=1, source_target_pairs={{0,3},{1,4},{2,5},{3,6},{4,7},{5,0},{6,1},{7,2},{8,11},{9,12},{10,... | collective-permute-start | bytes 24584 | tf_op jit(solution)/shard_map/ppermute | solution.py:358
  14.5 4.9 %collective-permute-start.3 = (bf16[304,128]{1,0:T(8,128)(2,1)S(1)}, bf16[304,128]{1,0:T(8,128)(2,1)S(1)}, u32[]{:S(2)}, u32[]{:S(2)}) collective-permute-start(bf16[304,128]{1,0:T(8,128)(2,1)S(1)} %get-tuple-element.18), channel_id=1, source_target_pairs={{0,1},{1,2},{2,3},{3,4},{4,5},{5,6},{6,7},{7,0},{8,9},{9,10},{10,1... | collective-permute-start | bytes 233480 | tf_op jit(solution)/shard_map/ppermute | solution.py:358
  16.1 5.3 %collective-permute-start.4 = (bf16[304,128]{1,0:T(8,128)(2,1)S(1)}, bf16[304,128]{1,0:T(8,128)(2,1)S(1)}, u32[]{:S(2)}, u32[]{:S(2)}) collective-permute-start(bf16[304,128]{1,0:T(8,128)(2,1)S(1)} %get-tuple-element.19), channel_id=1, source_target_pairs={{0,2},{1,3},{2,4},{3,5},{4,6},{5,7},{6,0},{7,1},{8,10},{9,11},{10,... | collective-permute-start | bytes 233480 | tf_op jit(solution)/shard_map/ppermute | solution.py:358
  22.4 6.3 %collective-permute-start.8 = (bf16[256,128]{1,0:T(8,128)(2,1)S(1)}, bf16[256,128]{1,0:T(8,128)(2,1)S(1)}, u32[]{:S(2)}, u32[]{:S(2)}) collective-permute-start(bf16[256,128]{1,0:T(8,128)(2,1)S(1)} %sum.1.r_0_), channel_id=1, source_target_pairs={{0,24},{8,16},{16,8},{24,0},{1,25},{9,17},{17,9},{25,1},{2,26},{10... | collective-permute-start | bytes 196616 | tf_op jit(solution)/shard_map/ppermute | solution.py:354
  22.9 6.6 %collective-permute-start.7 = (bf16[256,128]{1,0:T(8,128)(2,1)S(1)}, bf16[256,128]{1,0:T(8,128)(2,1)S(1)}, u32[]{:S(2)}, u32[]{:S(2)}) collective-permute-start(bf16[256,128]{1,0:T(8,128)(2,1)S(1)} %sum.1.r_0_), channel_id=1, source_target_pairs={{0,16},{8,24},{16,0},{24,8},{1,17},{9,25},{17,1},{25,9},{2,18},{10... | collective-permute-start | bytes 196616 | tf_op jit(solution)/shard_map/ppermute | solution.py:354
  22.9 6.6 %collective-permute-start.6 = (bf16[256,128]{1,0:T(8,128)(2,1)S(1)}, bf16[256,128]{1,0:T(8,128)(2,1)S(1)}, u32[]{:S(2)}, u32[]{:S(2)}) collective-permute-start(bf16[256,128]{1,0:T(8,128)(2,1)S(1)} %sum.1.r_0_), channel_id=1, source_target_pairs={{0,8},{8,0},{16,24},{24,16},{1,9},{9,1},{17,25},{25,17},{2,10},{10... | collective-permute-start | bytes 196616 | tf_op jit(solution)/shard_map/ppermute | solution.py:354
  30.1 4.5 %collective-permute-start.11 = (bf16[16,128]{1,0:T(8,128)(2,1)S(1)}, bf16[16,128]{1,0:T(8,128)(2,1)S(1)}, u32[]{:S(2)}, u32[]{:S(2)}) collective-permute-start(bf16[16,128]{1,0:T(8,128)(2,1)S(1)} %get-tuple-element.25), channel_id=1, source_target_pairs={{0,5},{1,6},{2,7},{3,0},{4,1},{5,2},{6,3},{7,4},{8,13},{9,14},{10,... | collective-permute-start | bytes 12296 | tf_op jit(solution)/shard_map/ppermute | solution.py:358
  31.5 3.7 %collective-permute-start.9 = (bf16[144,128]{1,0:T(8,128)(2,1)S(1)}, bf16[144,128]{1,0:T(8,128)(2,1)S(1)}, u32[]{:S(2)}, u32[]{:S(2)}) collective-permute-start(bf16[144,128]{1,0:T(8,128)(2,1)S(1)} %get-tuple-element.23), channel_id=1, source_target_pairs={{0,7},{1,0},{2,1},{3,2},{4,3},{5,4},{6,5},{7,6},{8,15},{9,8},{10,9... | collective-permute-start | bytes 110600 | tf_op jit(solution)/shard_map/ppermute | solution.py:358
  33.6 4.0 %collective-permute-start.10 = (bf16[144,128]{1,0:T(8,128)(2,1)S(1)}, bf16[144,128]{1,0:T(8,128)(2,1)S(1)}, u32[]{:S(2)}, u32[]{:S(2)}) collective-permute-start(bf16[144,128]{1,0:T(8,128)(2,1)S(1)} %get-tuple-element.24), channel_id=1, source_target_pairs={{0,6},{1,7},{2,0},{3,1},{4,2},{5,3},{6,4},{7,5},{8,14},{9,15},{10,... | collective-permute-start | bytes 110600 | tf_op jit(solution)/shard_map/ppermute | solution.py:358

commit v3 on v2

v3 whole, which is shorter than its diff:
```python
import jax
import jax.numpy as jnp
from jax import lax
from jax.experimental import pallas as pl
from jax.experimental.pallas import tpu as pltpu
from jax.sharding import PartitionSpec as P


PR = 16
PC = 128
TR = 1024
F32 = jnp.float32
BF16 = jnp.bfloat16
SENT = 32.0
REACH = 3
PARAMS = pltpu.CompilerParams(vmem_limit_bytes=24 * 1024 * 1024)


def iota(shape, dim):
    return lax.broadcasted_iota(jnp.int32, shape, dim)


def dot(a, b, ca=1, cb=0):
    return lax.dot_general(a, b, (((ca,), (cb,)), ((), ())), preferred_element_type=F32)


def circulant(taps, reverse):
    count, ks = taps.shape
    half = ks // 2
    tap, lane = iota((ks, PC), 0), iota((ks, PC), 1)
    place = (half - tap) if reverse else (tap - half)
    pick = jnp.where((place + PC) % PC == lane, 1.0, 0.0).astype(BF16)
    row = dot(taps, pick)
    return [
        pltpu.roll(jnp.broadcast_to(row[b : b + 1], (PC, PC)), 0, 1, stride=1, stride_axis=0)
        for b in range(count)
    ]


def same_row(places, first, count):
    row = iota((count, PC), 0).astype(BF16)
    one, zero = jnp.ones((count, PC), BF16), jnp.zeros((count, PC), BF16)
    return jnp.concatenate(
        [jnp.where(row == (p - float(first)).astype(BF16), one, zero) for p in places], 1
    )


def meta_rows(meta, half):
    hi, lo, step = (meta[3 * half + i : 3 * half + i + 1] for i in range(3))
    return hi, lo, step


def spill_at(hi, lo, step):
    over = hi * 32.0 + lo - TR
    return jnp.where(over >= 0.0, over + PR * step, -1.0)


def meta_tiles(exps):
    return -(-2 * exps // PR)


def piece_scalars(dest_ref, off_ref, p, tile, tiles):
    target = dest_ref[p]
    offset = off_ref[p]
    offset = jnp.where(target == tiles - 1, jnp.minimum(offset, TR - PR), offset)
    return (target - tile + tiles) % tiles, offset


def match_body(exps, tiles, *refs):
    args, matched_ref, z_refs = refs[:8], refs[8], refs[9 : 9 + exps]
    held, sems = refs[9 + exps : 17 + exps], refs[17 + exps]
    copies = [pltpu.make_async_copy(a, h, sems.at[i]) for i, (a, h) in enumerate(zip(args, held))]
    for copy in copies:
        copy.start()
    brow_ref, bcol_ref, sci_ref, poly_ref, mask_ref, var_ref, dest_ref, off_ref = held
    exp, tile = lax.axis_index("exp"), lax.axis_index("tile")
    height, across = sci_ref.shape
    bases = brow_ref.shape[0]
    copies[0].wait()
    copies[1].wait()
    d = iota((PC, PC), 1) - iota((PC, PC), 0)
    zero = jnp.zeros((PC, PC), F32)
    cols = circulant(bcol_ref[...], True)
    rows = circulant(brow_ref[...], False)
    copies[2].wait()
    copies[3].wait()
    sci = sci_ref[...]
    y = (iota((height, across), 0).astype(F32) - (height - 1) / 2.0) / (height / 2.0)
    x = (iota((height, across), 1).astype(F32) - (across - 1) / 2.0) / (across / 2.0)
    matched = jnp.zeros((height, across), F32)
    for b in range(bases):
        mid = jnp.where(jnp.abs(d) < PC // 2, cols[b], zero)
        up = jnp.where(d < -(PC // 2), cols[b], zero)
        low = jnp.where(d > PC // 2, cols[b], zero)
        band = jnp.concatenate(
            [jnp.concatenate([mid, up], 1), jnp.concatenate([low, mid], 1)], 0
        ).astype(BF16)
        first = dot(sci, band).astype(BF16)
        row_band = jnp.where(jnp.abs(d) < PC // 2, rows[b], zero).astype(BF16)
        second = dot(row_band, first)
        matched += (poly_ref[0, 0, 0, b] + poly_ref[0, 1, 0, b] * y + poly_ref[0, 2, 0, b] * x) * second
    matched_ref[...] = matched
    for copy in copies[4:]:
        copy.wait()
    rejected = jnp.bitwise_and(mask_ref[...], 7) != 0
    weight = jnp.where(rejected, 0.0, 1.0 / var_ref[...].astype(F32))
    weighted = matched * weight
    half = height // 2
    share = PC // exps
    parts = refs[18 + exps]
    for h in range(2):
        for i, image in enumerate((weighted, weight)):
            rows_of = image[half * h : half * (h + 1)]
            stacked = jnp.concatenate([rows_of[:, :PC], rows_of[:, PC:]], 0)
            parts[2 * h + i] = stacked.T.astype(parts.dtype)
    lane = iota((1, PC), 1)
    sub = iota((PR, PC), 0)
    meta = jnp.zeros((PR, PC), F32)
    per_half = half // PR
    for h in range(2):
        pos = jnp.zeros((1, PC), jnp.int32)
        step = jnp.zeros((1, PC), jnp.int32)
        for c in range(2):
            for rb in range(per_half):
                piece = 2 * (per_half * h + rb) + c
                rel, offset = piece_scalars(dest_ref, off_ref, piece, tile, tiles)
                here = lane // PR == per_half * c + rb
                pos = jnp.where(here, offset + lane % PR, pos)
                step = jnp.where(here, rel, step)
        for i, v in enumerate((pos // 32, pos % 32, step)):
            meta = jnp.where(sub == 3 * h + i, v.astype(F32), meta)
    meta = meta.astype(BF16)
    for k in range(exps):
        at = pl.multiple_of(share * jnp.bitwise_xor(exp, k), share)
        for g in range(4):
            z_refs[k][share * g : share * (g + 1)] = parts[g, pl.ds(at, share)].astype(BF16)
        z_refs[k][4 * share : 4 * share + PR] = meta


def pick_body(exps, *refs):
    z_refs, (m1_ref, m2_ref, m3_ref) = refs[:exps], refs[exps:]
    share = PC // exps
    pair = 2 * share
    sub16 = iota((PR, PC), 0)
    spill_row = iota((REACH * PR, PC), 0).astype(F32)
    spill = jnp.zeros((REACH * PR, PC), F32)
    metas = [[jnp.zeros((PR, PC), F32) for _ in range(meta_tiles(exps))] for _ in range(2)]
    for k in range(exps):
        top, bottom = z_refs[k][0:pair], z_refs[k][pair : 2 * pair]
        meta = z_refs[k][2 * pair : 2 * pair + PR].astype(F32)
        (hi0, lo0, step0), (hi1, lo1, step1) = meta_rows(meta, 0), meta_rows(meta, 1)
        use_top = step0 == 1.0
        mixed = jnp.where(use_top, top.astype(F32), bottom.astype(F32)).astype(BF16)
        m1_ref[pair * k : pair * (k + 1)] = mixed
        m2_ref[pair * k : pair * (k + 1)] = bottom
        for data, at in ((top, spill_at(hi0, lo0, step0)), (bottom, spill_at(hi1, lo1, step1))):
            hot = jnp.where(spill_row == at, 1.0, 0.0).astype(BF16)
            spill += dot(hot, jnp.concatenate([data] * (PC // pair), 0), 1, 1)
        values = (
            (jnp.where(use_top, hi0, jnp.where(step1 == 1.0, hi1, -SENT)), jnp.where(use_top, lo0, lo1)),
            (jnp.where(step1 == 2.0, hi1, -SENT), lo1),
        )
        at, row = 2 * k // PR, 2 * k % PR
        for tiles_of, rows_of in zip(metas, values):
            for i, v in enumerate(rows_of):
                tiles_of[at] = jnp.where(sub16 == row + i, v, tiles_of[at])
    coarse = spill.astype(BF16)
    fine = (spill - coarse.astype(F32)).astype(BF16)
    both = jnp.where(
        iota((REACH * PR, PC), 1) < pair, coarse.astype(F32), fine.astype(F32)
    ).astype(BF16)
    base = pair * exps
    for s, (ref, tiles_of) in enumerate(((m1_ref, metas[0]), (m2_ref, metas[1]))):
        for i, m in enumerate(tiles_of):
            ref[base + PR * i : base + PR * (i + 1)] = m.astype(BF16)
        at = base + PR * len(tiles_of)
        ref[at : at + PR] = both[PR * s : PR * (s + 1)]
    m3_ref[...] = both[2 * PR :]


BLOCK = 256


def own_body(exps, *refs):
    z_refs, out_ref = refs[:exps], refs[exps]
    share = PC // exps
    pair = 2 * share
    data = jnp.concatenate([z[0:pair] for z in z_refs], 1)
    places = []
    for z in z_refs:
        hi, lo, step = meta_rows(z[2 * pair : 2 * pair + PR].astype(F32), 0)
        places.append(jnp.where(step == 0.0, hi * 32.0 + lo, -1.0))
    for q in range(TR // BLOCK):
        hot = same_row(places, BLOCK * q, BLOCK)
        out_ref[:, BLOCK * q : BLOCK * (q + 1)] = dot(data, hot, 1, 1)


def message_places(ref, exps, k):
    base = 2 * PC // exps * exps
    at, row = base + PR * (2 * k // PR), 2 * k % PR
    meta = ref[at : at + PR].astype(F32)
    return meta[row : row + 1] * 32.0 + meta[row + 1 : row + 2]


def sum_body(exps, own_ref, m1_ref, m2_ref, m3_ref, out_ref):
    share = PC // exps
    pair = 2 * share
    at = pair * exps + PR * meta_tiles(exps)
    refs = (m1_ref, m2_ref)
    data = jnp.concatenate([r[pair * k : pair * (k + 1)] for r in refs for k in range(exps)], 1)
    places = [message_places(r, exps, k) for r in refs for k in range(exps)]
    spill = m3_ref[...].astype(F32)
    for r in refs:
        spill += r[at : at + PR].astype(F32)
    spill += pltpu.roll(spill, PC - pair, 1)
    spill = jnp.concatenate([spill, jnp.zeros((PC - PR, PC), F32)], 0).T[:pair]
    for q in range(TR // BLOCK):
        lanes = slice(BLOCK * q, BLOCK * (q + 1))
        total = dot(data, same_row(places, BLOCK * q, BLOCK), 1, 1) + own_ref[:, lanes]
        if q == 0:
            total = jnp.concatenate([total[:, :PC] + spill, total[:, PC:]], 1)
        out_ref[:, lanes] = (total[:share] / jnp.maximum(total[share:], 1.0)).astype(BF16)


def cut_body(exps, *refs):
    packed_refs, (z_ref, m1_ref, m2_ref) = refs[:exps], refs[exps : exps + 3]
    tile_ref, own_ref, n1_ref, n2_ref, n3_ref = refs[exps + 3 :]
    exp = lax.axis_index("exp")
    share = PC // exps
    for k in range(exps):
        at = pl.multiple_of(share * jnp.bitwise_xor(exp, k), share)
        tile_ref[pl.ds(at, share)] = packed_refs[k][...].astype(tile_ref.dtype)
    tile = tile_ref[...].astype(BF16)
    hi, lo, step = meta_rows(z_ref[4 * share : 4 * share + PR].astype(F32), 0)
    places = [
        jnp.where(step == 0.0, hi * 32.0 + lo, -1.0),
        message_places(m1_ref, exps, 0),
        message_places(m2_ref, exps, 0),
    ]
    hot = jnp.concatenate([same_row(places, BLOCK * q, BLOCK) for q in range(TR // BLOCK)], 0)
    cut = dot(tile, hot).astype(BF16)
    head = tile[:, :PC].astype(F32).T[:PR].astype(BF16)
    own_ref[...] = cut[:, :PC]
    n1_ref[0:PC] = cut[:, PC : 2 * PC]
    n1_ref[PC : PC + PR] = head
    n2_ref[0:PC] = cut[:, 2 * PC :]
    n2_ref[PC : PC + PR] = head
    n3_ref[...] = head


def template_body(tile_ref, out_ref):
    for i in range(TR // PC):
        lanes = slice(PC * i, PC * (i + 1))
        out_ref[lanes] = tile_ref[:, lanes].astype(F32).T.astype(BF16)


def subtract_body(exps, matched_ref, own_ref, n1_ref, n2_ref, n3_ref, z_ref, out_ref):
    half = matched_ref.shape[0] // 2
    at = 4 * (PC // exps)
    meta = z_ref[at : at + PR].astype(F32)
    heads = [n1_ref[PC : PC + PR], n2_ref[PC : PC + PR], n3_ref[...]]
    heads.append(jnp.zeros((PC - REACH * PR, PC), BF16))
    heads = jnp.concatenate(heads, 0)
    row = iota((PC, PC), 0).astype(F32)
    middle = n1_ref[0:PC].astype(F32)
    for h, (ref, outer) in enumerate(((own_ref, 0.0), (n2_ref, 2.0))):
        hi, lo, step = meta_rows(meta, h)
        hot = jnp.where(row == spill_at(hi, lo, step), 1.0, 0.0).astype(BF16)
        back = jnp.where(step == outer, ref[0:PC].astype(F32), middle) + dot(heads, hot, 0, 0)
        back = back.T
        rows = slice(half * h, half * (h + 1))
        for c in range(2):
            lanes = slice(PC * c, PC * (c + 1))
            out_ref[rows, lanes] = (matched_ref[rows, lanes] - back[half * c : half * (c + 1)]).astype(BF16)


VM = pl.BlockSpec(memory_space=pltpu.VMEM)
HBM = pl.BlockSpec(memory_space=pltpu.HBM)


def call(body, outs, specs, scratch=(), micros=1):
    return pl.pallas_call(
        body,
        out_shape=tuple(jax.ShapeDtypeStruct(s, t) for s, t in outs),
        in_specs=specs,
        out_specs=tuple(VM for _ in outs),
        scratch_shapes=scratch,
        compiler_params=PARAMS,
        cost_estimate=pl.CostEstimate(
            flops=micros * 10**9, bytes_accessed=micros * 10**6, transcendentals=0
        ),
    )


def along_exp(x, k, exps):
    return lax.ppermute(x, "exp", [(i, i ^ k) for i in range(exps)])


def along_tile(x, by, tiles):
    return lax.ppermute(x, "tile", [(i, (i + by) % tiles) for i in range(tiles)])


def program_of(exps, tiles):
    def steps(science, mask_bits, variance, kernel_poly, basis_rows, basis_cols, destination, row_offset):
        height, across = science.shape[2:]
        share = PC // exps
        packs = BF16 if share % 16 == 0 else F32
        message = ((4 * share + PR, PC), BF16)
        args = (
            basis_rows, basis_cols, science.reshape(height, across),
            jnp.transpose(kernel_poly, (0, 3, 1, 2)), mask_bits.reshape(height, across),
            variance.reshape(height, across), destination.reshape(-1), row_offset.reshape(-1),
        )
        args = tuple(pltpu.with_memory_space_constraint(a, pltpu.HBM) for a in args)
        small = (3, 6, 7)
        matched, *z = call(
            lambda *r: match_body(exps, tiles, *r),
            [((height, across), F32)] + [message] * exps,
            [HBM] * len(args),
            [(pltpu.SMEM if i in small else pltpu.VMEM)(a.shape, a.dtype) for i, a in enumerate(args)]
            + [pltpu.SemaphoreType.DMA((len(args),)), pltpu.VMEM((4, PC, PC), packs)],
        )(*args)
        z = [z[0]] + [along_exp(z[k], k, exps) for k in range(1, exps)]
        big = ((2 * share * exps + PR * meta_tiles(exps) + PR, PC), BF16)
        m1, m2, m3 = call(lambda *r: pick_body(exps, *r), [big, big, ((PR, PC), BF16)], [VM] * exps)(*z)
        m1, m2, m3 = (along_tile(m, i + 1, tiles) for i, m in enumerate((m1, m2, m3)))
        (own,) = call(lambda *r: own_body(exps, *r), [((2 * share, TR), F32)], [VM] * exps)(*z)
        (packed,) = call(lambda *r: sum_body(exps, *r), [((share, TR), BF16)], [VM] * 4)(own, m1, m2, m3)
        packed = [packed] + [along_exp(packed, k, exps) for k in range(1, exps)]
        back = ((PC + PR, PC), BF16)
        tile, own, n1, n2, n3 = call(
            lambda *r: cut_body(exps, *r),
            [((PC, TR), packs), ((PC, PC), BF16), back, back, ((PR, PC), BF16)],
            [VM] * (exps + 3),
        )(*packed, z[0], m1, m2)
        n1, n2, n3 = (along_tile(n, -1 - i, tiles) for i, n in enumerate((n1, n2, n3)))
        (template,) = call(template_body, [((TR, PC), BF16)], [VM])(tile)
        (difference,) = call(
            lambda *r: subtract_body(exps, *r), [((height, across), BF16)], [VM] * 6
        )(matched, own, n1, n2, n3, z[0])
        return template, difference[None, None]

    return steps


def solution(mesh):
    placed = (
        P("exp", "tile", None, None),
        P("exp", "tile", None, None),
        P("exp", "tile", None, None),
        P("exp", "tile", None, None),
        P(),
        P(),
        P("exp", "tile", None, None),
        P("exp", "tile", None),
    )
    return jax.shard_map(
        program_of(mesh.shape["exp"], mesh.shape["tile"]),
        mesh=mesh,
        in_specs=placed,
        out_specs=(P("tile", None), P("exp", "tile", None, None)),
        check_vma=False,
    )
```

time: 38.8 us -> 38 us (0.979)
  Pallas kernels: 6.52 us -> 5.54 us
    pallas_call x7, Pallas kernels: 6.52 us -> 5.54 us  [the longest x1 1.98 us: steps(): call(lambda *r: match_body(exps, tiles, *r), [((height, across), F32)] +...]
  transfers between devices with their start and end apart: 12 -> 12, of which waited for: 8 -> 8; matrix products, arithmetic and copies ran while one was open for 0% -> 0% of each run, Pallas kernels for 4% -> 3%
where the time goes in v3:
time: 38 us; the launch traced here: 37.8 us
  starting transfers between devices  16.8 us (44%)
  waiting for transfers between devices  14.9 us (39%)
  Pallas kernels  5.54 us (15%)
  between operations  0.69 us (2%)
    ppermute x6, starting transfers between devices, along_exp(): return lax.ppermute(x, 'exp', [(i, i ^ k) for i in range(exps)])  10.2 us
    ppermute x6, waiting for transfers between devices, along_exp(): return lax.ppermute(x, 'exp', [(i, i ^ k) for i in range(exps)])  8.43 us
    ppermute x6, starting transfers between devices, along_tile(): lax.ppermute(x, 'tile', [(i, (i + by) % tiles) for i in range(tiles)])  6.59 us
    ppermute x6, waiting for transfers between devices, along_tile(): lax.ppermute(x, 'tile', [(i, (i + by) % tiles) for i in range(tiles)])  6.42 us
    pallas_call x1, Pallas kernels, steps(): call(lambda *r: match_body(exps, tiles, *r), [((height, across), F32)] +...  1.98 us
    pallas_call x1, Pallas kernels, steps(): call(lambda *r: subtract_body(exps, *r), [((height, across), BF16)], [VM]...  0.91 us
    pallas_call x1, Pallas kernels, steps(): template, = call(template_body, [((TR, PC), BF16)], [VM])(tile)  0.84 us
    pallas_call x1, Pallas kernels, steps(): call(lambda *r: sum_body(exps, *r), [((share, TR), BF16)], [VM] * 4)  0.77 us
  transfers between devices with their start and end apart: 12, of which 8 were waited for; matrix products, arithmetic and copies ran while one was open for 0% of the time, Pallas kernels for 3%

profile of v3, /device:TPU:0, one launch (start us, length us, event | category | flops | bytes accessed | tf_op | source)
XLA Modules:
  0.0 37.8 jit_solution(14893482164250015324)
XLA Ops:
  0.6 2.0 %shard_map.95 = (f32[128,256]{1,0:T(8,128)S(1)}, bf16[144,128]{1,0:T(8,128)(2,1)S(1)}, bf16[144,128]{1,0:T(8,128)(2,1)S(1)}, bf16[144,128]{1,0:T(8,128)(2,1)S(1)}, bf16[144,128]{1,0:T(8,128)(2,1)S(1)}) custom-call(bf16[8,31]{1,0:T(8,128)(2,1)} %r_0_.1, bf16[8,31]{1,0:T(8,128)(2,1)} %r_1_.1, bf16[128,256]{1,0:T(8,128)(2,1)} %bitcast.8, ...), custom_call_target="tpu_custom_call" | custom-call | flops 1000000000 | bytes 1000000 | tf_op jit(solution)/shard_map/pallas_call | solution.py:316
  2.6 3.1 %collective-permute-start = (bf16[144,128]{1,0:T(8,128)(2,1)S(1)}, bf16[144,128]{1,0:T(8,128)(2,1)S(1)}, u32[]{:S(2)}, u32[]{:S(2)}) collective-permute-start(bf16[144,128]{1,0:T(8,128)(2,1)S(1)} %get-tuple-element.16), channel_id=1, source_target_pairs={{0,8},{8,0},{16,24},{24,16},{1,9},{9,1},{17,25},{25,17},{2,10},{10... | collective-permute-start | bytes 110600 | tf_op jit(solution)/shard_map/ppermute | solution.py:296
  5.7 2.6 %collective-permute-start.1 = (bf16[144,128]{1,0:T(8,128)(2,1)S(1)}, bf16[144,128]{1,0:T(8,128)(2,1)S(1)}, u32[]{:S(2)}, u32[]{:S(2)}) collective-permute-start(bf16[144,128]{1,0:T(8,128)(2,1)S(1)} %get-tuple-element.17), channel_id=1, source_target_pairs={{0,16},{8,24},{16,0},{24,8},{1,17},{9,25},{17,1},{25,9},{2,18},{10... | collective-permute-start | bytes 110600 | tf_op jit(solution)/shard_map/ppermute | solution.py:296
  8.3 2.9 %collective-permute-done.1.r_2_ = bf16[144,128]{1,0:T(8,128)(2,1)S(1)} collective-permute-done((bf16[144,128]{1,0:T(8,128)(2,1)S(1)}, bf16[144,128]{1,0:T(8,128)(2,1)S(1)}, u32[]{:S(2)}, u32[]{:S(2)}) %collective-permute-start.1) | collective-permute-done | bytes 36896 | tf_op jit(solution)/shard_map/ppermute | solution.py:296
  11.3 2.8 %collective-permute-done.2.r_3_ = bf16[144,128]{1,0:T(8,128)(2,1)S(1)} collective-permute-done((bf16[144,128]{1,0:T(8,128)(2,1)S(1)}, bf16[144,128]{1,0:T(8,128)(2,1)S(1)}, u32[]{:S(2)}, u32[]{:S(2)}) %collective-permute-start.2) | collective-permute-done | bytes 36896 | tf_op jit(solution)/shard_map/ppermute | solution.py:296
  14.1 0.3 shard_map.97
  14.4 0.1 collective-permute-start.5
  14.4 1.6 %collective-permute-start.3 = (bf16[288,128]{1,0:T(8,128)(2,1)S(1)}, bf16[288,128]{1,0:T(8,128)(2,1)S(1)}, u32[]{:S(2)}, u32[]{:S(2)}) collective-permute-start(bf16[288,128]{1,0:T(8,128)(2,1)S(1)} %get-tuple-element.19), channel_id=1, source_target_pairs={{0,1},{1,2},{2,3},{3,4},{4,5},{5,6},{6,7},{7,0},{8,9},{9,10},{10,1... | collective-permute-start | bytes 221192 | tf_op jit(solution)/shard_map/ppermute | solution.py:300
  16.1 1.5 %collective-permute-start.4 = (bf16[288,128]{1,0:T(8,128)(2,1)S(1)}, bf16[288,128]{1,0:T(8,128)(2,1)S(1)}, u32[]{:S(2)}, u32[]{:S(2)}) collective-permute-start(bf16[288,128]{1,0:T(8,128)(2,1)S(1)} %get-tuple-element.20), channel_id=1, source_target_pairs={{0,2},{1,3},{2,4},{3,5},{4,6},{5,7},{6,0},{7,1},{8,10},{9,11},{10,... | collective-permute-start | bytes 221192 | tf_op jit(solution)/shard_map/ppermute | solution.py:300
  17.6 0.4 %shard_map.96.r_0_ = f32[64,1024]{1,0:T(8,128)S(1)} custom-call(bf16[144,128]{1,0:T(8,128)(2,1)S(1)} %get-tuple-element.15.r_0_.r_4_.r_5_, bf16[144,128]{1,0:T(8,128)(2,1)S(1)} %collective-permute-done.r_1_, bf16[144,128]{1,0:T(8,128)(2,1)S(1)} %collective-permute-done.1.r_2_, bf16[144,128]{1,0:T(8,128)(2,1)S(1)} %collective-permute-done.2.r_3_), custom_call_target="tpu_custom_call" | custom-call | flops 1000000000 | bytes 1000000 | tf_op jit(solution)/shard_map/pallas_call | solution.py:327
  18.0 1.2 %collective-permute-done.3.r_1_.r_5_ = bf16[288,128]{1,0:T(8,128)(2,1)S(1)} collective-permute-done((bf16[288,128]{1,0:T(8,128)(2,1)S(1)}, bf16[288,128]{1,0:T(8,128)(2,1)S(1)}, u32[]{:S(2)}, u32[]{:S(2)}) %collective-permute-start.3) | collective-permute-done | bytes 73760 | tf_op jit(solution)/shard_map/ppermute | solution.py:300
  19.2 2.1 %collective-permute-done.4.r_2_.r_6_ = bf16[288,128]{1,0:T(8,128)(2,1)S(1)} collective-permute-done((bf16[288,128]{1,0:T(8,128)(2,1)S(1)}, bf16[288,128]{1,0:T(8,128)(2,1)S(1)}, u32[]{:S(2)}, u32[]{:S(2)}) %collective-permute-start.4) | collective-permute-done | bytes 73760 | tf_op jit(solution)/shard_map/ppermute | solution.py:300
  21.3 0.8 %shard_map.98.r_0_ = bf16[32,1024]{1,0:T(8,128)(2,1)S(1)} custom-call(f32[64,1024]{1,0:T(8,128)S(1)} %shard_map.96.r_0_, bf16[288,128]{1,0:T(8,128)(2,1)S(1)} %collective-permute-done.3.r_1_.r_5_, bf16[288,128]{1,0:T(8,128)(2,1)S(1)} %collective-permute-done.4.r_2_.r_6_, bf16[16,128]{1,0:T(8,128)(2,1)S(1)} %collective-permute-done.5.r_3_), custom_call_target="tpu_custom_call" | custom-call | flops 1000000000 | bytes 1000000 | tf_op jit(solution)/shard_map/pallas_call | solution.py:328
  22.1 0.6 %collective-permute-start.8 = (bf16[32,1024]{1,0:T(8,128)(2,1)S(1)}, bf16[32,1024]{1,0:T(8,128)(2,1)S(1)}, u32[]{:S(2)}, u32[]{:S(2)}) collective-permute-start(bf16[32,1024]{1,0:T(8,128)(2,1)S(1)} %shard_map.98.r_0_), channel_id=1, source_target_pairs={{0,24},{8,16},{16,8},{24,0},{1,25},{9,17},{17,9},{25,1},{2,26},{10... | collective-permute-start | bytes 196616 | tf_op jit(solution)/shard_map/ppermute | solution.py:296
  22.7 3.9 %collective-permute-start.6 = (bf16[32,1024]{1,0:T(8,128)(2,1)S(1)}, bf16[32,1024]{1,0:T(8,128)(2,1)S(1)}, u32[]{:S(2)}, u32[]{:S(2)}) collective-permute-start(bf16[32,1024]{1,0:T(8,128)(2,1)S(1)} %shard_map.98.r_0_), channel_id=1, source_target_pairs={{0,8},{8,0},{16,24},{24,16},{1,9},{9,1},{17,25},{25,17},{2,10},{10... | collective-permute-start | bytes 196616 | tf_op jit(solution)/shard_map/ppermute | solution.py:296
  26.6 1.9 %collective-permute-done.8.r_3_ = bf16[32,1024]{1,0:T(8,128)(2,1)S(1)} collective-permute-done((bf16[32,1024]{1,0:T(8,128)(2,1)S(1)}, bf16[32,1024]{1,0:T(8,128)(2,1)S(1)}, u32[]{:S(2)}, u32[]{:S(2)}) %collective-permute-start.8) | collective-permute-done | bytes 65568 | tf_op jit(solution)/shard_map/ppermute | solution.py:296
  28.4 0.8 %collective-permute-done.7.r_2_ = bf16[32,1024]{1,0:T(8,128)(2,1)S(1)} collective-permute-done((bf16[32,1024]{1,0:T(8,128)(2,1)S(1)}, bf16[32,1024]{1,0:T(8,128)(2,1)S(1)}, u32[]{:S(2)}, u32[]{:S(2)}) %collective-permute-start.7) | collective-permute-done | bytes 65568 | tf_op jit(solution)/shard_map/ppermute | solution.py:296
  29.2 0.3 shard_map.99
  29.5 1.3 %collective-permute-start.11 = (bf16[16,128]{1,0:T(8,128)(2,1)S(1)}, bf16[16,128]{1,0:T(8,128)(2,1)S(1)}, u32[]{:S(2)}, u32[]{:S(2)}) collective-permute-start(bf16[16,128]{1,0:T(8,128)(2,1)S(1)} %get-tuple-element.27), channel_id=1, source_target_pairs={{0,5},{1,6},{2,7},{3,0},{4,1},{5,2},{6,3},{7,4},{8,13},{9,14},{10,... | collective-permute-start | bytes 12296 | tf_op jit(solution)/shard_map/ppermute | solution.py:300
  30.9 2.1 %collective-permute-start.9 = (bf16[144,128]{1,0:T(8,128)(2,1)S(1)}, bf16[144,128]{1,0:T(8,128)(2,1)S(1)}, u32[]{:S(2)}, u32[]{:S(2)}) collective-permute-start(bf16[144,128]{1,0:T(8,128)(2,1)S(1)} %get-tuple-element.25), channel_id=1, source_target_pairs={{0,7},{1,0},{2,1},{3,2},{4,3},{5,4},{6,5},{7,6},{8,15},{9,8},{10,9... | collective-permute-start | bytes 110600 | tf_op jit(solution)/shard_map/ppermute | solution.py:300
  33.0 0.8 %shard_map.100 = bf16[1024,128]{1,0:T(8,128)(2,1)} custom-call(bf16[128,1024]{1,0:T(8,128)(2,1)S(1)} %get-tuple-element.22.tile_ref), custom_call_target="tpu_custom_call" | custom-call | flops 1000000000 | bytes 1000000 | tf_op jit(solution)/shard_map/pallas_call | solution.py:337
  33.8 0.8 %collective-permute-done.9.r_2_ = bf16[144,128]{1,0:T(8,128)(2,1)S(1)} collective-permute-done((bf16[144,128]{1,0:T(8,128)(2,1)S(1)}, bf16[144,128]{1,0:T(8,128)(2,1)S(1)}, u32[]{:S(2)}, u32[]{:S(2)}) %collective-permute-start.9) | collective-permute-done | bytes 36896 | tf_op jit(solution)/shard_map/ppermute | solution.py:300
  34.6 2.3 %collective-permute-done.10.r_3_ = bf16[144,128]{1,0:T(8,128)(2,1)S(1)} collective-permute-done((bf16[144,128]{1,0:T(8,128)(2,1)S(1)}, bf16[144,128]{1,0:T(8,128)(2,1)S(1)}, u32[]{:S(2)}, u32[]{:S(2)}) %collective-permute-start.10) | collective-permute-done | bytes 36896 | tf_op jit(solution)/shard_map/ppermute | solution.py:300
  36.9 0.9 %shard_map.101 = bf16[128,256]{1,0:T(8,128)(2,1)} custom-call(f32[128,256]{1,0:T(8,128)S(1)} %get-tuple-element.23.r_0_, bf16[128,128]{1,0:T(8,128)(2,1)S(1)} %get-tuple-element.24.r_1_, bf16[144,128]{1,0:T(8,128)(2,1)S(1)} %collective-permute-done.9.r_2_, bf16[144,128]{1,0:T(8,128)(2,1)S(1)} %collective-permute-done.10.r_3_, ...), custom_call_target="tpu_custom_call" | custom-call | flops 1000000000 | bytes 1000000 | tf_op jit(solution)/shard_map/pallas_call | solution.py:338
  (7 shorter events, 0.0 us)
Async XLA Ops:
  2.6 5.7 %collective-permute-start = (bf16[144,128]{1,0:T(8,128)(2,1)S(1)}, bf16[144,128]{1,0:T(8,128)(2,1)S(1)}, u32[]{:S(2)}, u32[]{:S(2)}) collective-permute-start(bf16[144,128]{1,0:T(8,128)(2,1)S(1)} %get-tuple-element.16), channel_id=1, source_target_pairs={{0,8},{8,0},{16,24},{24,16},{1,9},{9,1},{17,25},{25,17},{2,10},{10... | collective-permute-start | bytes 110600 | tf_op jit(solution)/shard_map/ppermute | solution.py:296
  5.7 5.5 %collective-permute-start.1 = (bf16[144,128]{1,0:T(8,128)(2,1)S(1)}, bf16[144,128]{1,0:T(8,128)(2,1)S(1)}, u32[]{:S(2)}, u32[]{:S(2)}) collective-permute-start(bf16[144,128]{1,0:T(8,128)(2,1)S(1)} %get-tuple-element.17), channel_id=1, source_target_pairs={{0,16},{8,24},{16,0},{24,8},{1,17},{9,25},{17,1},{25,9},{2,18},{10... | collective-permute-start | bytes 110600 | tf_op jit(solution)/shard_map/ppermute | solution.py:296
  8.3 5.8 %collective-permute-start.2 = (bf16[144,128]{1,0:T(8,128)(2,1)S(1)}, bf16[144,128]{1,0:T(8,128)(2,1)S(1)}, u32[]{:S(2)}, u32[]{:S(2)}) collective-permute-start(bf16[144,128]{1,0:T(8,128)(2,1)S(1)} %get-tuple-element.18), channel_id=1, source_target_pairs={{0,24},{8,16},{16,8},{24,0},{1,25},{9,17},{17,9},{25,1},{2,26},{10... | collective-permute-start | bytes 110600 | tf_op jit(solution)/shard_map/ppermute | solution.py:296
  14.4 3.6 %collective-permute-start.5 = (bf16[16,128]{1,0:T(8,128)(2,1)S(1)}, bf16[16,128]{1,0:T(8,128)(2,1)S(1)}, u32[]{:S(2)}, u32[]{:S(2)}) collective-permute-start(bf16[16,128]{1,0:T(8,128)(2,1)S(1)} %get-tuple-element.21), channel_id=1, source_target_pairs={{0,3},{1,4},{2,5},{3,6},{4,7},{5,0},{6,1},{7,2},{8,11},{9,12},{10,... | collective-permute-start | bytes 12296 | tf_op jit(solution)/shard_map/ppermute | solution.py:300
  14.4 4.8 %collective-permute-start.3 = (bf16[288,128]{1,0:T(8,128)(2,1)S(1)}, bf16[288,128]{1,0:T(8,128)(2,1)S(1)}, u32[]{:S(2)}, u32[]{:S(2)}) collective-permute-start(bf16[288,128]{1,0:T(8,128)(2,1)S(1)} %get-tuple-element.19), channel_id=1, source_target_pairs={{0,1},{1,2},{2,3},{3,4},{4,5},{5,6},{6,7},{7,0},{8,9},{9,10},{10,1... | collective-permute-start | bytes 221192 | tf_op jit(solution)/shard_map/ppermute | solution.py:300
  16.1 5.3 %collective-permute-start.4 = (bf16[288,128]{1,0:T(8,128)(2,1)S(1)}, bf16[288,128]{1,0:T(8,128)(2,1)S(1)}, u32[]{:S(2)}, u32[]{:S(2)}) collective-permute-start(bf16[288,128]{1,0:T(8,128)(2,1)S(1)} %get-tuple-element.20), channel_id=1, source_target_pairs={{0,2},{1,3},{2,4},{3,5},{4,6},{5,7},{6,0},{7,1},{8,10},{9,11},{10,... | collective-permute-start | bytes 221192 | tf_op jit(solution)/shard_map/ppermute | solution.py:300
  22.1 6.3 %collective-permute-start.8 = (bf16[32,1024]{1,0:T(8,128)(2,1)S(1)}, bf16[32,1024]{1,0:T(8,128)(2,1)S(1)}, u32[]{:S(2)}, u32[]{:S(2)}) collective-permute-start(bf16[32,1024]{1,0:T(8,128)(2,1)S(1)} %shard_map.98.r_0_), channel_id=1, source_target_pairs={{0,24},{8,16},{16,8},{24,0},{1,25},{9,17},{17,9},{25,1},{2,26},{10... | collective-permute-start | bytes 196616 | tf_op jit(solution)/shard_map/ppermute | solution.py:296
  22.7 6.6 %collective-permute-start.7 = (bf16[32,1024]{1,0:T(8,128)(2,1)S(1)}, bf16[32,1024]{1,0:T(8,128)(2,1)S(1)}, u32[]{:S(2)}, u32[]{:S(2)}) collective-permute-start(bf16[32,1024]{1,0:T(8,128)(2,1)S(1)} %shard_map.98.r_0_), channel_id=1, source_target_pairs={{0,16},{8,24},{16,0},{24,8},{1,17},{9,25},{17,1},{25,9},{2,18},{10... | collective-permute-start | bytes 196616 | tf_op jit(solution)/shard_map/ppermute | solution.py:296
  22.7 6.6 %collective-permute-start.6 = (bf16[32,1024]{1,0:T(8,128)(2,1)S(1)}, bf16[32,1024]{1,0:T(8,128)(2,1)S(1)}, u32[]{:S(2)}, u32[]{:S(2)}) collective-permute-start(bf16[32,1024]{1,0:T(8,128)(2,1)S(1)} %shard_map.98.r_0_), channel_id=1, source_target_pairs={{0,8},{8,0},{16,24},{24,16},{1,9},{9,1},{17,25},{25,17},{2,10},{10... | collective-permute-start | bytes 196616 | tf_op jit(solution)/shard_map/ppermute | solution.py:296
  29.5 4.3 %collective-permute-start.11 = (bf16[16,128]{1,0:T(8,128)(2,1)S(1)}, bf16[16,128]{1,0:T(8,128)(2,1)S(1)}, u32[]{:S(2)}, u32[]{:S(2)}) collective-permute-start(bf16[16,128]{1,0:T(8,128)(2,1)S(1)} %get-tuple-element.27), channel_id=1, source_target_pairs={{0,5},{1,6},{2,7},{3,0},{4,1},{5,2},{6,3},{7,4},{8,13},{9,14},{10,... | collective-permute-start | bytes 12296 | tf_op jit(solution)/shard_map/ppermute | solution.py:300
  30.9 3.7 %collective-permute-start.9 = (bf16[144,128]{1,0:T(8,128)(2,1)S(1)}, bf16[144,128]{1,0:T(8,128)(2,1)S(1)}, u32[]{:S(2)}, u32[]{:S(2)}) collective-permute-start(bf16[144,128]{1,0:T(8,128)(2,1)S(1)} %get-tuple-element.25), channel_id=1, source_target_pairs={{0,7},{1,0},{2,1},{3,2},{4,3},{5,4},{6,5},{7,6},{8,15},{9,8},{10,9... | collective-permute-start | bytes 110600 | tf_op jit(solution)/shard_map/ppermute | solution.py:300
  33.0 4.0 %collective-permute-start.10 = (bf16[144,128]{1,0:T(8,128)(2,1)S(1)}, bf16[144,128]{1,0:T(8,128)(2,1)S(1)}, u32[]{:S(2)}, u32[]{:S(2)}) collective-permute-start(bf16[144,128]{1,0:T(8,128)(2,1)S(1)} %get-tuple-element.26), channel_id=1, source_target_pairs={{0,6},{1,7},{2,0},{3,1},{4,2},{5,3},{6,4},{7,5},{8,14},{9,15},{10,... | collective-permute-start | bytes 110600 | tf_op jit(solution)/shard_map/ppermute | solution.py:300

commit v4 on v3

--- a/solution.py
+++ b/solution.py
@@ -57,13 +57,6 @@
 
 def meta_tiles(exps):
     return -(-2 * exps // PR)
-
-
-def piece_scalars(dest_ref, off_ref, p, tile, tiles):
-    target = dest_ref[p]
-    offset = off_ref[p]
-    offset = jnp.where(target == tiles - 1, jnp.minimum(offset, TR - PR), offset)
-    return (target - tile + tiles) % tiles, offset
 
 
 def match_body(exps, tiles, *refs):
@@ -82,54 +75,59 @@
     zero = jnp.zeros((PC, PC), F32)
     cols = circulant(bcol_ref[...], True)
     rows = circulant(brow_ref[...], False)
-    copies[2].wait()
-    copies[3].wait()
+    for copy in copies[2:]:
+        copy.wait()
+    half = height // 2
+    share = PC // exps
+    pieces = dest_ref.shape[1]
+    target, offset = dest_ref[...], off_ref[...]
+    offset = jnp.where(target == tiles - 1, jnp.minimum(offset, TR - PR), offset)
+    step = target - tile
+    step = jnp.where(step < 0, step + tiles, step)
+    known = jnp.concatenate(
+        [(offset // 32).astype(F32), (offset % 32).astype(F32), step.astype(F32)]
+        + [jnp.zeros((PR - 3, pieces), F32)],
+        0,
+    ).astype(BF16)
+    piece, lane = iota((pieces, PC), 0), iota((pieces, PC), 1)
+    per_half = half // PR
+    sub = iota((PR, PC), 0)
+    meta = jnp.zeros((PR, PC), F32)
+    for h in range(2):
+        under = 2 * (per_half * h + lane // PR % per_half) + lane // half
+        spread = dot(known, jnp.where(piece == under, 1.0, 0.0).astype(BF16))
+        pos = (spread[0:1] * 32.0 + spread[1:2]).astype(jnp.int32) + iota((1, PC), 1) % PR
+        for i, v in enumerate(((pos // 32).astype(F32), (pos % 32).astype(F32), spread[2:3])):
+            meta = jnp.where(sub == 3 * h + i, v, meta)
+    meta = meta.astype(BF16)
     sci = sci_ref[...]
-    y = (iota((height, across), 0).astype(F32) - (height - 1) / 2.0) / (height / 2.0)
-    x = (iota((height, across), 1).astype(F32) - (across - 1) / 2.0) / (across / 2.0)
+    y = (iota((height, 1), 0).astype(F32) - (height - 1) / 2.0) / (height / 2.0)
+    x = (iota((1, across), 1).astype(F32) - (across - 1) / 2.0) / (across / 2.0)
     matched = jnp.zeros((height, across), F32)
+    bands = []
     for b in range(bases):
         mid = jnp.where(jnp.abs(d) < PC // 2, cols[b], zero)
         up = jnp.where(d < -(PC // 2), cols[b], zero)
         low = jnp.where(d > PC // 2, cols[b], zero)
-        band = jnp.concatenate(
-            [jnp.concatenate([mid, up], 1), jnp.concatenate([low, mid], 1)], 0
-        ).astype(BF16)
-        first = dot(sci, band).astype(BF16)
+        bands.append(
+            jnp.concatenate([jnp.concatenate([mid, up], 1), jnp.concatenate([low, mid], 1)], 0).astype(BF16)
+        )
+    first = dot(sci, jnp.concatenate(bands, 1)).astype(BF16)
+    for b in range(bases):
         row_band = jnp.where(jnp.abs(d) < PC // 2, rows[b], zero).astype(BF16)
-        second = dot(row_band, first)
-        matched += (poly_ref[0, 0, 0, b] + poly_ref[0, 1, 0, b] * y + poly_ref[0, 2, 0, b] * x) * second
+        second = dot(row_band, first[:, across * b : across * (b + 1)])
+        along = jnp.broadcast_to(poly_ref[0, 0, 0, b] + poly_ref[0, 1, 0, b] * y, (height, across))
+        matched += (along + poly_ref[0, 2, 0, b] * x) * second
     matched_ref[...] = matched
-    for copy in copies[4:]:
-        copy.wait()
     rejected = jnp.bitwise_and(mask_ref[...], 7) != 0
     weight = jnp.where(rejected, 0.0, 1.0 / var_ref[...].astype(F32))
     weighted = matched * weight
-    half = height // 2
-    share = PC // exps
     parts = refs[18 + exps]
     for h in range(2):
         for i, image in enumerate((weighted, weight)):
             rows_of = image[half * h : half * (h + 1)]
             stacked = jnp.concatenate([rows_of[:, :PC], rows_of[:, PC:]], 0)
             parts[2 * h + i] = stacked.T.astype(parts.dtype)
-    lane = iota((1, PC), 1)
-    sub = iota((PR, PC), 0)
-    meta = jnp.zeros((PR, PC), F32)
-    per_half = half // PR
-    for h in range(2):
-        pos = jnp.zeros((1, PC), jnp.int32)
-        step = jnp.zeros((1, PC), jnp.int32)
-        for c in range(2):
-            for rb in range(per_half):
-                piece = 2 * (per_half * h + rb) + c
-                rel, offset = piece_scalars(dest_ref, off_ref, piece, tile, tiles)
-                here = lane // PR == per_half * c + rb
-                pos = jnp.where(here, offset + lane % PR, pos)
-                step = jnp.where(here, rel, step)
-        for i, v in enumerate((pos // 32, pos % 32, step)):
-            meta = jnp.where(sub == 3 * h + i, v.astype(F32), meta)
-    meta = meta.astype(BF16)
     for k in range(exps):
         at = pl.multiple_of(share * jnp.bitwise_xor(exp, k), share)
         for g in range(4):
@@ -202,56 +200,69 @@
     return meta[row : row + 1] * 32.0 + meta[row + 1 : row + 2]
 
 
-def sum_body(exps, own_ref, m1_ref, m2_ref, m3_ref, out_ref):
+def message_sums(exps, prior_ref, ref, q):
+    pair = 2 * PC // exps
+    data = jnp.concatenate([ref[pair * k : pair * (k + 1)] for k in range(exps)], 1)
+    places = [message_places(ref, exps, k) for k in range(exps)]
+    lanes = slice(BLOCK * q, BLOCK * (q + 1))
+    return dot(data, same_row(places, BLOCK * q, BLOCK), 1, 1) + prior_ref[:, lanes]
+
+
+def far_body(exps, own_ref, m2_ref, out_ref):
+    for q in range(TR // BLOCK):
+        out_ref[:, BLOCK * q : BLOCK * (q + 1)] = message_sums(exps, own_ref, m2_ref, q)
+
+
+def sum_body(exps, far_ref, m1_ref, m2_ref, m3_ref, out_ref):
     share = PC // exps
     pair = 2 * share
     at = pair * exps + PR * meta_tiles(exps)
-    refs = (m1_ref, m2_ref)
-    data = jnp.concatenate([r[pair * k : pair * (k + 1)] for r in refs for k in range(exps)], 1)
-    places = [message_places(r, exps, k) for r in refs for k in range(exps)]
     spill = m3_ref[...].astype(F32)
-    for r in refs:
+    for r in (m1_ref, m2_ref):
         spill += r[at : at + PR].astype(F32)
     spill += pltpu.roll(spill, PC - pair, 1)
     spill = jnp.concatenate([spill, jnp.zeros((PC - PR, PC), F32)], 0).T[:pair]
     for q in range(TR // BLOCK):
-        lanes = slice(BLOCK * q, BLOCK * (q + 1))
-        total = dot(data, same_row(places, BLOCK * q, BLOCK), 1, 1) + own_ref[:, lanes]
+        total = message_sums(exps, far_ref, m1_ref, q)
         if q == 0:
             total = jnp.concatenate([total[:, :PC] + spill, total[:, PC:]], 1)
+        lanes = slice(BLOCK * q, BLOCK * (q + 1))
         out_ref[:, lanes] = (total[:share] / jnp.maximum(total[share:], 1.0)).astype(BF16)
 
 
+def place_body(exps, m1_ref, m2_ref, z_ref, hot_ref, own_ref):
+    share = PC // exps
+    hi, lo, step = meta_rows(z_ref[4 * share : 4 * share + PR].astype(F32), 0)
+    own = [jnp.where(step == 0.0, hi * 32.0 + lo, -1.0)]
+    others = [message_places(r, exps, 0) for r in (m1_ref, m2_ref)]
+    for q in range(TR // BLOCK):
+        rows = slice(BLOCK * q, BLOCK * (q + 1))
+        hot_ref[rows] = same_row(others, BLOCK * q, BLOCK)
+        own_ref[rows] = same_row(own, BLOCK * q, BLOCK)
+
+
 def cut_body(exps, *refs):
-    packed_refs, (z_ref, m1_ref, m2_ref) = refs[:exps], refs[exps : exps + 3]
-    tile_ref, own_ref, n1_ref, n2_ref, n3_ref = refs[exps + 3 :]
+    packed_refs, hot_ref, (tile_ref, n1_ref, n2_ref, n3_ref) = refs[:exps], refs[exps], refs[exps + 1 :]
     exp = lax.axis_index("exp")
     share = PC // exps
     for k in range(exps):
         at = pl.multiple_of(share * jnp.bitwise_xor(exp, k), share)
         tile_ref[pl.ds(at, share)] = packed_refs[k][...].astype(tile_ref.dtype)
     tile = tile_ref[...].astype(BF16)
-    hi, lo, step = meta_rows(z_ref[4 * share : 4 * share + PR].astype(F32), 0)
-    places = [
-        jnp.where(step == 0.0, hi * 32.0 + lo, -1.0),
-        message_places(m1_ref, exps, 0),
-        message_places(m2_ref, exps, 0),
-    ]
-    hot = jnp.concatenate([same_row(places, BLOCK * q, BLOCK) for q in range(TR // BLOCK)], 0)
-    cut = dot(tile, hot).astype(BF16)
+    cut = dot(tile, hot_ref[...]).astype(BF16)
     head = tile[:, :PC].astype(F32).T[:PR].astype(BF16)
-    own_ref[...] = cut[:, :PC]
-    n1_ref[0:PC] = cut[:, PC : 2 * PC]
+    n1_ref[0:PC] = cut[:, :PC]
     n1_ref[PC : PC + PR] = head
-    n2_ref[0:PC] = cut[:, 2 * PC :]
+    n2_ref[0:PC] = cut[:, PC:]
     n2_ref[PC : PC + PR] = head
     n3_ref[...] = head
 
 
-def template_body(tile_ref, out_ref):
+def template_body(tile_ref, hot_ref, out_ref, own_ref):
     for i in range(TR // PC):
         lanes = slice(PC * i, PC * (i + 1))
         out_ref[lanes] = tile_ref[:, lanes].astype(F32).T.astype(BF16)
+    own_ref[...] = dot(tile_ref[...].astype(BF16), hot_ref[...]).astype(BF16)
 
 
 def subtract_body(exps, matched_ref, own_ref, n1_ref, n2_ref, n3_ref, z_ref, out_ref):
@@ -309,15 +320,14 @@
         args = (
             basis_rows, basis_cols, science.reshape(height, across),
             jnp.transpose(kernel_poly, (0, 3, 1, 2)), mask_bits.reshape(height, across),
-            variance.reshape(height, across), destination.reshape(-1), row_offset.reshape(-1),
+            variance.reshape(height, across), destination.reshape(1, -1), row_offset.reshape(1, -1),
         )
         args = tuple(pltpu.with_memory_space_constraint(a, pltpu.HBM) for a in args)
-        small = (3, 6, 7)
         matched, *z = call(
             lambda *r: match_body(exps, tiles, *r),
             [((height, across), F32)] + [message] * exps,
             [HBM] * len(args),
-            [(pltpu.SMEM if i in small else pltpu.VMEM)(a.shape, a.dtype) for i, a in enumerate(args)]
+            [(pltpu.SMEM if i == 3 else pltpu.VMEM)(a.shape, a.dtype) for i, a in enumerate(args)]
             + [pltpu.SemaphoreType.DMA((len(args),)), pltpu.VMEM((4, PC, PC), packs)],
         )(*args)
         z = [z[0]] + [along_exp(z[k], k, exps) for k in range(1, exps)]
@@ -325,16 +335,18 @@
         m1, m2, m3 = call(lambda *r: pick_body(exps, *r), [big, big, ((PR, PC), BF16)], [VM] * exps)(*z)
         m1, m2, m3 = (along_tile(m, i + 1, tiles) for i, m in enumerate((m1, m2, m3)))
         (own,) = call(lambda *r: own_body(exps, *r), [((2 * share, TR), F32)], [VM] * exps)(*z)
-        (packed,) = call(lambda *r: sum_body(exps, *r), [((share, TR), BF16)], [VM] * 4)(own, m1, m2, m3)
+        (far,) = call(lambda *r: far_body(exps, *r), [((2 * share, TR), F32)], [VM] * 2)(own, m2)
+        (packed,) = call(lambda *r: sum_body(exps, *r), [((share, TR), BF16)], [VM] * 4)(far, m1, m2, m3)
         packed = [packed] + [along_exp(packed, k, exps) for k in range(1, exps)]
+        hot, own_hot = call(
+            lambda *r: place_body(exps, *r), [((TR, 2 * PC), BF16), ((TR, PC), BF16)], [VM] * 3
+        )(m1, m2, z[0])
         back = ((PC + PR, PC), BF16)
-        tile, own, n1, n2, n3 = call(
-            lambda *r: cut_body(exps, *r),
-            [((PC, TR), packs), ((PC, PC), BF16), back, back, ((PR, PC), BF16)],
-            [VM] * (exps + 3),
-        )(*packed, z[0], m1, m2)
+        tile, n1, n2, n3 = call(
+            lambda *r: cut_body(exps, *r), [((PC, TR), packs), back, back, ((PR, PC), BF16)], [VM] * (exps + 1)
+        )(*packed, hot)
         n1, n2, n3 = (along_tile(n, -1 - i, tiles) for i, n in enumerate((n1, n2, n3)))
-        (template,) = call(template_body, [((TR, PC), BF16)], [VM])(tile)
+        template, own = call(template_body, [((TR, PC), BF16), ((PC, PC), BF16)], [VM] * 2)(tile, own_hot)
         (difference,) = call(
             lambda *r: subtract_body(exps, *r), [((height, across), BF16)], [VM] * 6
         )(matched, own, n1, n2, n3, z[0])

time: 38 us -> 36.5 us (0.961)
  waiting for transfers between devices: 14.9 us -> 13.8 us
  starting transfers between devices: 16.8 us -> 16.3 us
    ppermute x6, waiting for transfers between devices: 6.42 us -> 5.11 us  [along_tile(): lax.ppermute(x, 'tile', [(i, (i + by) % tiles) for i in range(tiles)])]
    pallas_call x2 -> x4, Pallas kernels: 1.15 us -> 1.73 us  [the longest x1 0.92 us: steps(): call(template_body, [((TR, PC), BF16), ((PC, PC), BF16)], [VM] * 2)]
    ppermute x6, starting transfers between devices: 6.59 us -> 6.18 us  [along_tile(): lax.ppermute(x, 'tile', [(i, (i + by) % tiles) for i in range(tiles)])]
  transfers between devices with their start and end apart: 12 -> 12, of which waited for: 8 -> 7; matrix products, arithmetic and copies ran while one was open for 0% -> 0% of each run, Pallas kernels for 3% -> 5%
where the time goes in v4:
time: 36.5 us; the launch traced here: 36.4 us
  starting transfers between devices  16.3 us (45%)
  waiting for transfers between devices  13.8 us (38%)
  Pallas kernels  5.56 us (15%)
  between operations  0.7 us (2%)
    ppermute x6, starting transfers between devices, along_exp(): return lax.ppermute(x, 'exp', [(i, i ^ k) for i in range(exps)])  10.2 us
    ppermute x6, waiting for transfers between devices, along_exp(): return lax.ppermute(x, 'exp', [(i, i ^ k) for i in range(exps)])  8.67 us
    ppermute x6, starting transfers between devices, along_tile(): lax.ppermute(x, 'tile', [(i, (i + by) % tiles) for i in range(tiles)])  6.18 us
    ppermute x6, waiting for transfers between devices, along_tile(): lax.ppermute(x, 'tile', [(i, (i + by) % tiles) for i in range(tiles)])  5.11 us
    pallas_call x1, Pallas kernels, steps(): call(lambda *r: match_body(exps, tiles, *r), [((height, across), F32)] +...  1.74 us
    pallas_call x1, Pallas kernels, steps(): call(template_body, [((TR, PC), BF16), ((PC, PC), BF16)], [VM] * 2)  0.92 us
    pallas_call x1, Pallas kernels, steps(): call(lambda *r: subtract_body(exps, *r), [((height, across), BF16)], [VM]...  0.91 us
  transfers between devices with their start and end apart: 12, of which 7 were waited for; matrix products, arithmetic and copies ran while one was open for 0% of the time, Pallas kernels for 5%

profile of v4, /device:TPU:0, one launch (start us, length us, event | category | flops | bytes accessed | tf_op | source)
XLA Modules:
  0.0 36.4 jit_solution(14863371384523740622)
XLA Ops:
  0.6 1.7 %shard_map.95 = (f32[128,256]{1,0:T(8,128)S(1)}, bf16[144,128]{1,0:T(8,128)(2,1)S(1)}, bf16[144,128]{1,0:T(8,128)(2,1)S(1)}, bf16[144,128]{1,0:T(8,128)(2,1)S(1)}, bf16[144,128]{1,0:T(8,128)(2,1)S(1)}) custom-call(bf16[8,31]{1,0:T(8,128)(2,1)} %r_0_.1, bf16[8,31]{1,0:T(8,128)(2,1)} %r_1_.1, bf16[128,256]{1,0:T(8,128)(2,1)} %bitcast.8, ...), custom_call_target="tpu_custom_call" | custom-call | flops 1000000000 | bytes 1000000 | tf_op jit(solution)/shard_map/pallas_call | solution.py:326
  2.4 3.1 %collective-permute-start = (bf16[144,128]{1,0:T(8,128)(2,1)S(1)}, bf16[144,128]{1,0:T(8,128)(2,1)S(1)}, u32[]{:S(2)}, u32[]{:S(2)}) collective-permute-start(bf16[144,128]{1,0:T(8,128)(2,1)S(1)} %get-tuple-element.19), channel_id=1, source_target_pairs={{0,8},{8,0},{16,24},{24,16},{1,9},{9,1},{17,25},{25,17},{2,10},{10... | collective-permute-start | bytes 110600 | tf_op jit(solution)/shard_map/ppermute | solution.py:307
  5.5 2.6 %collective-permute-start.1 = (bf16[144,128]{1,0:T(8,128)(2,1)S(1)}, bf16[144,128]{1,0:T(8,128)(2,1)S(1)}, u32[]{:S(2)}, u32[]{:S(2)}) collective-permute-start(bf16[144,128]{1,0:T(8,128)(2,1)S(1)} %get-tuple-element.20), channel_id=1, source_target_pairs={{0,16},{8,24},{16,0},{24,8},{1,17},{9,25},{17,1},{25,9},{2,18},{10... | collective-permute-start | bytes 110600 | tf_op jit(solution)/shard_map/ppermute | solution.py:307
  8.1 2.9 %collective-permute-done.1.r_2_ = bf16[144,128]{1,0:T(8,128)(2,1)S(1)} collective-permute-done((bf16[144,128]{1,0:T(8,128)(2,1)S(1)}, bf16[144,128]{1,0:T(8,128)(2,1)S(1)}, u32[]{:S(2)}, u32[]{:S(2)}) %collective-permute-start.1) | collective-permute-done | bytes 36896 | tf_op jit(solution)/shard_map/ppermute | solution.py:307
  11.0 2.8 %collective-permute-done.2.r_3_ = bf16[144,128]{1,0:T(8,128)(2,1)S(1)} collective-permute-done((bf16[144,128]{1,0:T(8,128)(2,1)S(1)}, bf16[144,128]{1,0:T(8,128)(2,1)S(1)}, u32[]{:S(2)}, u32[]{:S(2)}) %collective-permute-start.2) | collective-permute-done | bytes 36896 | tf_op jit(solution)/shard_map/ppermute | solution.py:307
  13.8 0.3 shard_map.97
  14.2 1.5 %collective-permute-start.3 = (bf16[288,128]{1,0:T(8,128)(2,1)S(1)}, bf16[288,128]{1,0:T(8,128)(2,1)S(1)}, u32[]{:S(2)}, u32[]{:S(2)}) collective-permute-start(bf16[288,128]{1,0:T(8,128)(2,1)S(1)} %get-tuple-element.22), channel_id=1, source_target_pairs={{0,2},{1,3},{2,4},{3,5},{4,6},{5,7},{6,0},{7,1},{8,10},{9,11},{10,... | collective-permute-start | bytes 221192 | tf_op jit(solution)/shard_map/ppermute | solution.py:311
  15.7 1.3 %collective-permute-start.4 = (bf16[288,128]{1,0:T(8,128)(2,1)S(1)}, bf16[288,128]{1,0:T(8,128)(2,1)S(1)}, u32[]{:S(2)}, u32[]{:S(2)}) collective-permute-start(bf16[288,128]{1,0:T(8,128)(2,1)S(1)} %get-tuple-element.23), channel_id=1, source_target_pairs={{0,1},{1,2},{2,3},{3,4},{4,5},{5,6},{6,7},{7,0},{8,9},{9,10},{10,1... | collective-permute-start | bytes 221192 | tf_op jit(solution)/shard_map/ppermute | solution.py:311
  17.0 0.4 %shard_map.96.r_0_ = f32[64,1024]{1,0:T(8,128)S(1)} custom-call(bf16[144,128]{1,0:T(8,128)(2,1)S(1)} %get-tuple-element.18.r_0_.r_2_.r_5_, bf16[144,128]{1,0:T(8,128)(2,1)S(1)} %collective-permute-done.r_1_, bf16[144,128]{1,0:T(8,128)(2,1)S(1)} %collective-permute-done.1.r_2_, bf16[144,128]{1,0:T(8,128)(2,1)S(1)} %collective-permute-done.2.r_3_), custom_call_target="tpu_custom_call" | custom-call | flops 1000000000 | bytes 1000000 | tf_op jit(solution)/shard_map/pallas_call | solution.py:337
  17.5 2.2 %collective-permute-done.3.r_1_.r_2_ = bf16[288,128]{1,0:T(8,128)(2,1)S(1)} collective-permute-done((bf16[288,128]{1,0:T(8,128)(2,1)S(1)}, bf16[288,128]{1,0:T(8,128)(2,1)S(1)}, u32[]{:S(2)}, u32[]{:S(2)}) %collective-permute-start.3) | collective-permute-done | bytes 73760 | tf_op jit(solution)/shard_map/ppermute | solution.py:311
  19.7 0.4 %shard_map.98.r_0_ = f32[64,1024]{1,0:T(8,128)S(1)} custom-call(f32[64,1024]{1,0:T(8,128)S(1)} %shard_map.96.r_0_, bf16[288,128]{1,0:T(8,128)(2,1)S(1)} %collective-permute-done.3.r_1_.r_2_), custom_call_target="tpu_custom_call" | custom-call | flops 1000000000 | bytes 1000000 | tf_op jit(solution)/shard_map/pallas_call | solution.py:338
  20.1 0.9 %collective-permute-done.4.r_1_.r_0_ = bf16[288,128]{1,0:T(8,128)(2,1)S(1)} collective-permute-done((bf16[288,128]{1,0:T(8,128)(2,1)S(1)}, bf16[288,128]{1,0:T(8,128)(2,1)S(1)}, u32[]{:S(2)}, u32[]{:S(2)}) %collective-permute-start.4) | collective-permute-done | bytes 73760 | tf_op jit(solution)/shard_map/ppermute | solution.py:311
  21.1 0.5 %shard_map.99.r_0_ = bf16[32,1024]{1,0:T(8,128)(2,1)S(1)} custom-call(f32[64,1024]{1,0:T(8,128)S(1)} %shard_map.98.r_0_, bf16[288,128]{1,0:T(8,128)(2,1)S(1)} %collective-permute-done.4.r_1_.r_0_, bf16[288,128]{1,0:T(8,128)(2,1)S(1)} %collective-permute-done.3.r_1_.r_2_, bf16[16,128]{1,0:T(8,128)(2,1)S(1)} %collective-permute-done.5.r_3_), custom_call_target="tpu_custom_call" | custom-call | flops 1000000000 | bytes 1000000 | tf_op jit(solution)/shard_map/pallas_call | solution.py:339
  21.6 0.6 %collective-permute-start.8 = (bf16[32,1024]{1,0:T(8,128)(2,1)S(1)}, bf16[32,1024]{1,0:T(8,128)(2,1)S(1)}, u32[]{:S(2)}, u32[]{:S(2)}) collective-permute-start(bf16[32,1024]{1,0:T(8,128)(2,1)S(1)} %shard_map.99.r_0_), channel_id=1, source_target_pairs={{0,24},{8,16},{16,8},{24,0},{1,25},{9,17},{17,9},{25,1},{2,26},{10... | collective-permute-start | bytes 196616 | tf_op jit(solution)/shard_map/ppermute | solution.py:307
  22.1 3.9 %collective-permute-start.6 = (bf16[32,1024]{1,0:T(8,128)(2,1)S(1)}, bf16[32,1024]{1,0:T(8,128)(2,1)S(1)}, u32[]{:S(2)}, u32[]{:S(2)}) collective-permute-start(bf16[32,1024]{1,0:T(8,128)(2,1)S(1)} %shard_map.99.r_0_), channel_id=1, source_target_pairs={{0,8},{8,0},{16,24},{24,16},{1,9},{9,1},{17,25},{25,17},{2,10},{10... | collective-permute-start | bytes 196616 | tf_op jit(solution)/shard_map/ppermute | solution.py:307
  26.0 0.1 shard_map.100
  26.1 2.2 %collective-permute-done.8.r_3_ = bf16[32,1024]{1,0:T(8,128)(2,1)S(1)} collective-permute-done((bf16[32,1024]{1,0:T(8,128)(2,1)S(1)}, bf16[32,1024]{1,0:T(8,128)(2,1)S(1)}, u32[]{:S(2)}, u32[]{:S(2)}) %collective-permute-start.8) | collective-permute-done | bytes 65568 | tf_op jit(solution)/shard_map/ppermute | solution.py:307
  28.3 0.7 %collective-permute-done.7.r_2_ = bf16[32,1024]{1,0:T(8,128)(2,1)S(1)} collective-permute-done((bf16[32,1024]{1,0:T(8,128)(2,1)S(1)}, bf16[32,1024]{1,0:T(8,128)(2,1)S(1)}, u32[]{:S(2)}, u32[]{:S(2)}) %collective-permute-start.7) | collective-permute-done | bytes 65568 | tf_op jit(solution)/shard_map/ppermute | solution.py:307
  29.0 0.2 shard_map.101
  29.4 2.1 %collective-permute-start.9 = (bf16[144,128]{1,0:T(8,128)(2,1)S(1)}, bf16[144,128]{1,0:T(8,128)(2,1)S(1)}, u32[]{:S(2)}, u32[]{:S(2)}) collective-permute-start(bf16[144,128]{1,0:T(8,128)(2,1)S(1)} %get-tuple-element.31), channel_id=1, source_target_pairs={{0,7},{1,0},{2,1},{3,2},{4,3},{5,4},{6,5},{7,6},{8,15},{9,8},{10,9... | collective-permute-start | bytes 110600 | tf_op jit(solution)/shard_map/ppermute | solution.py:311
  31.5 1.1 %collective-permute-start.10 = (bf16[144,128]{1,0:T(8,128)(2,1)S(1)}, bf16[144,128]{1,0:T(8,128)(2,1)S(1)}, u32[]{:S(2)}, u32[]{:S(2)}) collective-permute-start(bf16[144,128]{1,0:T(8,128)(2,1)S(1)} %get-tuple-element.32), channel_id=1, source_target_pairs={{0,6},{1,7},{2,0},{3,1},{4,2},{5,3},{6,4},{7,5},{8,14},{9,15},{10,... | collective-permute-start | bytes 110600 | tf_op jit(solution)/shard_map/ppermute | solution.py:311
  32.6 0.9 %shard_map.102 = (bf16[1024,128]{1,0:T(8,128)(2,1)}, bf16[128,128]{1,0:T(8,128)(2,1)S(1)}) custom-call(bf16[128,1024]{1,0:T(8,128)(2,1)S(1)} %get-tuple-element.26.tile_ref, bf16[1024,128]{1,0:T(8,128)(2,1)S(1)} %get-tuple-element.27.hot_ref), custom_call_target="tpu_custom_call" | custom-call | flops 1000000000 | bytes 1000000 | tf_op jit(solution)/shard_map/pallas_call | solution.py:349
  33.5 2.0 %collective-permute-done.10.r_3_ = bf16[144,128]{1,0:T(8,128)(2,1)S(1)} collective-permute-done((bf16[144,128]{1,0:T(8,128)(2,1)S(1)}, bf16[144,128]{1,0:T(8,128)(2,1)S(1)}, u32[]{:S(2)}, u32[]{:S(2)}) %collective-permute-start.10) | collective-permute-done | bytes 36896 | tf_op jit(solution)/shard_map/ppermute | solution.py:311
  35.5 0.9 %shard_map.103 = bf16[128,256]{1,0:T(8,128)(2,1)} custom-call(f32[128,256]{1,0:T(8,128)S(1)} %get-tuple-element.29.r_0_, bf16[128,128]{1,0:T(8,128)(2,1)S(1)} %get-tuple-element.30.r_1_, bf16[144,128]{1,0:T(8,128)(2,1)S(1)} %collective-permute-done.9.r_2_, bf16[144,128]{1,0:T(8,128)(2,1)S(1)} %collective-permute-done.10.r_3_, ...), custom_call_target="tpu_custom_call" | custom-call | flops 1000000000 | bytes 1000000 | tf_op jit(solution)/shard_map/pallas_call | solution.py:350
  (9 shorter events, 0.1 us)
Async XLA Ops:
  2.4 5.7 %collective-permute-start = (bf16[144,128]{1,0:T(8,128)(2,1)S(1)}, bf16[144,128]{1,0:T(8,128)(2,1)S(1)}, u32[]{:S(2)}, u32[]{:S(2)}) collective-permute-start(bf16[144,128]{1,0:T(8,128)(2,1)S(1)} %get-tuple-element.19), channel_id=1, source_target_pairs={{0,8},{8,0},{16,24},{24,16},{1,9},{9,1},{17,25},{25,17},{2,10},{10... | collective-permute-start | bytes 110600 | tf_op jit(solution)/shard_map/ppermute | solution.py:307
  5.5 5.5 %collective-permute-start.1 = (bf16[144,128]{1,0:T(8,128)(2,1)S(1)}, bf16[144,128]{1,0:T(8,128)(2,1)S(1)}, u32[]{:S(2)}, u32[]{:S(2)}) collective-permute-start(bf16[144,128]{1,0:T(8,128)(2,1)S(1)} %get-tuple-element.20), channel_id=1, source_target_pairs={{0,16},{8,24},{16,0},{24,8},{1,17},{9,25},{17,1},{25,9},{2,18},{10... | collective-permute-start | bytes 110600 | tf_op jit(solution)/shard_map/ppermute | solution.py:307
  8.1 5.8 %collective-permute-start.2 = (bf16[144,128]{1,0:T(8,128)(2,1)S(1)}, bf16[144,128]{1,0:T(8,128)(2,1)S(1)}, u32[]{:S(2)}, u32[]{:S(2)}) collective-permute-start(bf16[144,128]{1,0:T(8,128)(2,1)S(1)} %get-tuple-element.21), channel_id=1, source_target_pairs={{0,24},{8,16},{16,8},{24,0},{1,25},{9,17},{17,9},{25,1},{2,26},{10... | collective-permute-start | bytes 110600 | tf_op jit(solution)/shard_map/ppermute | solution.py:307
  14.1 6.0 %collective-permute-start.5 = (bf16[16,128]{1,0:T(8,128)(2,1)S(1)}, bf16[16,128]{1,0:T(8,128)(2,1)S(1)}, u32[]{:S(2)}, u32[]{:S(2)}) collective-permute-start(bf16[16,128]{1,0:T(8,128)(2,1)S(1)} %get-tuple-element.24), channel_id=1, source_target_pairs={{0,3},{1,4},{2,5},{3,6},{4,7},{5,0},{6,1},{7,2},{8,11},{9,12},{10,... | collective-permute-start | bytes 12296 | tf_op jit(solution)/shard_map/ppermute | solution.py:311
  14.2 5.5 %collective-permute-start.3 = (bf16[288,128]{1,0:T(8,128)(2,1)S(1)}, bf16[288,128]{1,0:T(8,128)(2,1)S(1)}, u32[]{:S(2)}, u32[]{:S(2)}) collective-permute-start(bf16[288,128]{1,0:T(8,128)(2,1)S(1)} %get-tuple-element.22), channel_id=1, source_target_pairs={{0,2},{1,3},{2,4},{3,5},{4,6},{5,7},{6,0},{7,1},{8,10},{9,11},{10,... | collective-permute-start | bytes 221192 | tf_op jit(solution)/shard_map/ppermute | solution.py:311
  15.7 5.3 %collective-permute-start.4 = (bf16[288,128]{1,0:T(8,128)(2,1)S(1)}, bf16[288,128]{1,0:T(8,128)(2,1)S(1)}, u32[]{:S(2)}, u32[]{:S(2)}) collective-permute-start(bf16[288,128]{1,0:T(8,128)(2,1)S(1)} %get-tuple-element.23), channel_id=1, source_target_pairs={{0,1},{1,2},{2,3},{3,4},{4,5},{5,6},{6,7},{7,0},{8,9},{9,10},{10,1... | collective-permute-start | bytes 221192 | tf_op jit(solution)/shard_map/ppermute | solution.py:311
  21.6 6.8 %collective-permute-start.8 = (bf16[32,1024]{1,0:T(8,128)(2,1)S(1)}, bf16[32,1024]{1,0:T(8,128)(2,1)S(1)}, u32[]{:S(2)}, u32[]{:S(2)}) collective-permute-start(bf16[32,1024]{1,0:T(8,128)(2,1)S(1)} %shard_map.99.r_0_), channel_id=1, source_target_pairs={{0,24},{8,16},{16,8},{24,0},{1,25},{9,17},{17,9},{25,1},{2,26},{10... | collective-permute-start | bytes 196616 | tf_op jit(solution)/shard_map/ppermute | solution.py:307
  22.1 6.9 %collective-permute-start.7 = (bf16[32,1024]{1,0:T(8,128)(2,1)S(1)}, bf16[32,1024]{1,0:T(8,128)(2,1)S(1)}, u32[]{:S(2)}, u32[]{:S(2)}) collective-permute-start(bf16[32,1024]{1,0:T(8,128)(2,1)S(1)} %shard_map.99.r_0_), channel_id=1, source_target_pairs={{0,16},{8,24},{16,0},{24,8},{1,17},{9,25},{17,1},{25,9},{2,18},{10... | collective-permute-start | bytes 196616 | tf_op jit(solution)/shard_map/ppermute | solution.py:307
  22.1 6.9 %collective-permute-start.6 = (bf16[32,1024]{1,0:T(8,128)(2,1)S(1)}, bf16[32,1024]{1,0:T(8,128)(2,1)S(1)}, u32[]{:S(2)}, u32[]{:S(2)}) collective-permute-start(bf16[32,1024]{1,0:T(8,128)(2,1)S(1)} %shard_map.99.r_0_), channel_id=1, source_target_pairs={{0,8},{8,0},{16,24},{24,16},{1,9},{9,1},{17,25},{25,17},{2,10},{10... | collective-permute-start | bytes 196616 | tf_op jit(solution)/shard_map/ppermute | solution.py:307
  29.3 4.2 %collective-permute-start.11 = (bf16[16,128]{1,0:T(8,128)(2,1)S(1)}, bf16[16,128]{1,0:T(8,128)(2,1)S(1)}, u32[]{:S(2)}, u32[]{:S(2)}) collective-permute-start(bf16[16,128]{1,0:T(8,128)(2,1)S(1)} %get-tuple-element.33), channel_id=1, source_target_pairs={{0,5},{1,6},{2,7},{3,0},{4,1},{5,2},{6,3},{7,4},{8,13},{9,14},{10,... | collective-permute-start | bytes 12296 | tf_op jit(solution)/shard_map/ppermute | solution.py:311
  29.4 4.2 %collective-permute-start.9 = (bf16[144,128]{1,0:T(8,128)(2,1)S(1)}, bf16[144,128]{1,0:T(8,128)(2,1)S(1)}, u32[]{:S(2)}, u32[]{:S(2)}) collective-permute-start(bf16[144,128]{1,0:T(8,128)(2,1)S(1)} %get-tuple-element.31), channel_id=1, source_target_pairs={{0,7},{1,0},{2,1},{3,2},{4,3},{5,4},{6,5},{7,6},{8,15},{9,8},{10,9... | collective-permute-start | bytes 110600 | tf_op jit(solution)/shard_map/ppermute | solution.py:311
  31.5 4.0 %collective-permute-start.10 = (bf16[144,128]{1,0:T(8,128)(2,1)S(1)}, bf16[144,128]{1,0:T(8,128)(2,1)S(1)}, u32[]{:S(2)}, u32[]{:S(2)}) collective-permute-start(bf16[144,128]{1,0:T(8,128)(2,1)S(1)} %get-tuple-element.32), channel_id=1, source_target_pairs={{0,6},{1,7},{2,0},{3,1},{4,2},{5,3},{6,4},{7,5},{8,14},{9,15},{10,... | collective-permute-start | bytes 110600 | tf_op jit(solution)/shard_map/ppermute | solution.py:311

commit v5 on v4

--- a/solution.py
+++ b/solution.py
@@ -22,6 +22,18 @@
 
 def dot(a, b, ca=1, cb=0):
     return lax.dot_general(a, b, (((ca,), (cb,)), ((), ())), preferred_element_type=F32)
+
+
+def partners(exps, name):
+    far = list(range(4, exps))
+    near = {"share": ((2, 3, 1), (2, 3, 1)), "join": ((3, 1, 2), (2, 3, 1))}[name]
+    return [[0, *order[:2], *far, order[2]] for order in near]
+
+
+def met_group(exps, name, i):
+    exp, odd = lax.axis_index("exp"), lax.axis_index("tile") % 2
+    even_way, odd_way = (order[i] for order in partners(exps, name))
+    return jnp.bitwise_xor(exp, jnp.where(odd == 1, odd_way, even_way))
 
 
 def circulant(taps, reverse):
@@ -66,7 +78,7 @@
     for copy in copies:
         copy.start()
     brow_ref, bcol_ref, sci_ref, poly_ref, mask_ref, var_ref, dest_ref, off_ref = held
-    exp, tile = lax.axis_index("exp"), lax.axis_index("tile")
+    tile = lax.axis_index("tile")
     height, across = sci_ref.shape
     bases = brow_ref.shape[0]
     copies[0].wait()
@@ -129,7 +141,7 @@
             stacked = jnp.concatenate([rows_of[:, :PC], rows_of[:, PC:]], 0)
             parts[2 * h + i] = stacked.T.astype(parts.dtype)
     for k in range(exps):
-        at = pl.multiple_of(share * jnp.bitwise_xor(exp, k), share)
+        at = pl.multiple_of(share * met_group(exps, "share", k), share)
         for g in range(4):
             z_refs[k][share * g : share * (g + 1)] = parts[g, pl.ds(at, share)].astype(BF16)
         z_refs[k][4 * share : 4 * share + PR] = meta
@@ -243,10 +255,9 @@
 
 def cut_body(exps, *refs):
     packed_refs, hot_ref, (tile_ref, n1_ref, n2_ref, n3_ref) = refs[:exps], refs[exps], refs[exps + 1 :]
-    exp = lax.axis_index("exp")
     share = PC // exps
     for k in range(exps):
-        at = pl.multiple_of(share * jnp.bitwise_xor(exp, k), share)
+        at = pl.multiple_of(share * met_group(exps, "join", k), share)
         tile_ref[pl.ds(at, share)] = packed_refs[k][...].astype(tile_ref.dtype)
     tile = tile_ref[...].astype(BF16)
     cut = dot(tile, hot_ref[...]).astype(BF16)
@@ -303,8 +314,10 @@
     )
 
 
-def along_exp(x, k, exps):
-    return lax.ppermute(x, "exp", [(i, i ^ k) for i in range(exps)])
+def along_exp(x, i, exps, tiles, name):
+    ways = [order[i] for order in partners(exps, name)]
+    pairs = [(e * tiles + t, (e ^ ways[t % 2]) * tiles + t) for e in range(exps) for t in range(tiles)]
+    return lax.ppermute(x, ("exp", "tile"), pairs)
 
 
 def along_tile(x, by, tiles):
@@ -330,14 +343,14 @@
             [(pltpu.SMEM if i == 3 else pltpu.VMEM)(a.shape, a.dtype) for i, a in enumerate(args)]
             + [pltpu.SemaphoreType.DMA((len(args),)), pltpu.VMEM((4, PC, PC), packs)],
         )(*args)
-        z = [z[0]] + [along_exp(z[k], k, exps) for k in range(1, exps)]
+        z = [z[0]] + [along_exp(z[k], k, exps, tiles, "share") for k in range(1, exps)]
         big = ((2 * share * exps + PR * meta_tiles(exps) + PR, PC), BF16)
         m1, m2, m3 = call(lambda *r: pick_body(exps, *r), [big, big, ((PR, PC), BF16)], [VM] * exps)(*z)
         m1, m2, m3 = (along_tile(m, i + 1, tiles) for i, m in enumerate((m1, m2, m3)))
         (own,) = call(lambda *r: own_body(exps, *r), [((2 * share, TR), F32)], [VM] * exps)(*z)
         (far,) = call(lambda *r: far_body(exps, *r), [((2 * share, TR), F32)], [VM] * 2)(own, m2)
         (packed,) = call(lambda *r: sum_body(exps, *r), [((share, TR), BF16)], [VM] * 4)(far, m1, m2, m3)
-        packed = [packed] + [along_exp(packed, k, exps) for k in range(1, exps)]
+        packed = [packed] + [along_exp(packed, k, exps, tiles, "join") for k in range(1, exps)]
         hot, own_hot = call(
             lambda *r: place_body(exps, *r), [((TR, 2 * PC), BF16), ((TR, PC), BF16)], [VM] * 3
         )(m1, m2, z[0])

time: 36.5 us -> 36.4 us (level)
  no operation moved by 1% of the time
where the time goes in v5:
time: 36.4 us; the launch traced here: 36.3 us
  starting transfers between devices  16.3 us (45%)
  waiting for transfers between devices  13.7 us (38%)
  Pallas kernels  5.56 us (15%)
  between operations  0.7 us (2%)
    ppermute x6, starting transfers between devices, along_exp(): return lax.ppermute(x, ('exp', 'tile'), pairs)  10.2 us
    ppermute x6, waiting for transfers between devices, along_exp(): return lax.ppermute(x, ('exp', 'tile'), pairs)  8.49 us
    ppermute x6, starting transfers between devices, along_tile(): lax.ppermute(x, 'tile', [(i, (i + by) % tiles) for i in range(tiles)])  6.18 us
    ppermute x6, waiting for transfers between devices, along_tile(): lax.ppermute(x, 'tile', [(i, (i + by) % tiles) for i in range(tiles)])  5.17 us
    pallas_call x1, Pallas kernels, steps(): call(lambda *r: match_body(exps, tiles, *r), [((height, across), F32)] +...  1.74 us
    pallas_call x1, Pallas kernels, steps(): call(template_body, [((TR, PC), BF16), ((PC, PC), BF16)], [VM] * 2)  0.92 us
    pallas_call x1, Pallas kernels, steps(): call(lambda *r: subtract_body(exps, *r), [((height, across), BF16)], [VM]...  0.91 us
  transfers between devices with their start and end apart: 12, of which 7 were waited for; matrix products, arithmetic and copies ran while one was open for 0% of the time, Pallas kernels for 5%

profile of v5, /device:TPU:0, one launch (start us, length us, event | category | flops | bytes accessed | tf_op | source)
XLA Modules:
  0.0 36.3 jit_solution(9604868131293082558)
XLA Ops:
  0.6 1.7 %shard_map.95 = (f32[128,256]{1,0:T(8,128)S(1)}, bf16[144,128]{1,0:T(8,128)(2,1)S(1)}, bf16[144,128]{1,0:T(8,128)(2,1)S(1)}, bf16[144,128]{1,0:T(8,128)(2,1)S(1)}, bf16[144,128]{1,0:T(8,128)(2,1)S(1)}) custom-call(bf16[8,31]{1,0:T(8,128)(2,1)} %r_0_.1, bf16[8,31]{1,0:T(8,128)(2,1)} %r_1_.1, bf16[128,256]{1,0:T(8,128)(2,1)} %bitcast.8, ...), custom_call_target="tpu_custom_call" | custom-call | flops 1000000000 | bytes 1000000 | tf_op jit(solution)/shard_map/pallas_call | solution.py:339
  2.4 4.1 %collective-permute-start = (bf16[144,128]{1,0:T(8,128)(2,1)S(1)}, bf16[144,128]{1,0:T(8,128)(2,1)S(1)}, u32[]{:S(2)}, u32[]{:S(2)}) collective-permute-start(bf16[144,128]{1,0:T(8,128)(2,1)S(1)} %get-tuple-element.19), channel_id=1, source_target_pairs={{0,16},{1,17},{2,18},{3,19},{4,20},{5,21},{6,22},{7,23},{8,24},{9,... | collective-permute-start | bytes 110600 | tf_op jit(solution)/shard_map/ppermute | solution.py:320
  6.5 1.3 %collective-permute-start.1 = (bf16[144,128]{1,0:T(8,128)(2,1)S(1)}, bf16[144,128]{1,0:T(8,128)(2,1)S(1)}, u32[]{:S(2)}, u32[]{:S(2)}) collective-permute-start(bf16[144,128]{1,0:T(8,128)(2,1)S(1)} %get-tuple-element.20), channel_id=1, source_target_pairs={{0,24},{1,25},{2,26},{3,27},{4,28},{5,29},{6,30},{7,31},{8,16},{9,... | collective-permute-start | bytes 110600 | tf_op jit(solution)/shard_map/ppermute | solution.py:320
  8.1 0.7 %collective-permute-done.r_1_ = bf16[144,128]{1,0:T(8,128)(2,1)S(1)} collective-permute-done((bf16[144,128]{1,0:T(8,128)(2,1)S(1)}, bf16[144,128]{1,0:T(8,128)(2,1)S(1)}, u32[]{:S(2)}, u32[]{:S(2)}) %collective-permute-start) | collective-permute-done | bytes 36896 | tf_op jit(solution)/shard_map/ppermute | solution.py:320
  8.8 3.4 %collective-permute-done.1.r_2_ = bf16[144,128]{1,0:T(8,128)(2,1)S(1)} collective-permute-done((bf16[144,128]{1,0:T(8,128)(2,1)S(1)}, bf16[144,128]{1,0:T(8,128)(2,1)S(1)}, u32[]{:S(2)}, u32[]{:S(2)}) %collective-permute-start.1) | collective-permute-done | bytes 36896 | tf_op jit(solution)/shard_map/ppermute | solution.py:320
  12.3 0.3 shard_map.97
  12.6 1.5 %collective-permute-start.3 = (bf16[288,128]{1,0:T(8,128)(2,1)S(1)}, bf16[288,128]{1,0:T(8,128)(2,1)S(1)}, u32[]{:S(2)}, u32[]{:S(2)}) collective-permute-start(bf16[288,128]{1,0:T(8,128)(2,1)S(1)} %get-tuple-element.22), channel_id=1, source_target_pairs={{0,2},{1,3},{2,4},{3,5},{4,6},{5,7},{6,0},{7,1},{8,10},{9,11},{10,... | collective-permute-start | bytes 221192 | tf_op jit(solution)/shard_map/ppermute | solution.py:324
  14.2 1.3 %collective-permute-start.4 = (bf16[288,128]{1,0:T(8,128)(2,1)S(1)}, bf16[288,128]{1,0:T(8,128)(2,1)S(1)}, u32[]{:S(2)}, u32[]{:S(2)}) collective-permute-start(bf16[288,128]{1,0:T(8,128)(2,1)S(1)} %get-tuple-element.23), channel_id=1, source_target_pairs={{0,1},{1,2},{2,3},{3,4},{4,5},{5,6},{6,7},{7,0},{8,9},{9,10},{10,1... | collective-permute-start | bytes 221192 | tf_op jit(solution)/shard_map/ppermute | solution.py:324
  15.5 0.4 %shard_map.96.r_0_ = f32[64,1024]{1,0:T(8,128)S(1)} custom-call(bf16[144,128]{1,0:T(8,128)(2,1)S(1)} %get-tuple-element.18.r_0_.r_2_.r_5_, bf16[144,128]{1,0:T(8,128)(2,1)S(1)} %collective-permute-done.r_1_, bf16[144,128]{1,0:T(8,128)(2,1)S(1)} %collective-permute-done.1.r_2_, bf16[144,128]{1,0:T(8,128)(2,1)S(1)} %collective-permute-done.2.r_3_), custom_call_target="tpu_custom_call" | custom-call | flops 1000000000 | bytes 1000000 | tf_op jit(solution)/shard_map/pallas_call | solution.py:350
  15.9 2.2 %collective-permute-done.3.r_1_.r_2_ = bf16[288,128]{1,0:T(8,128)(2,1)S(1)} collective-permute-done((bf16[288,128]{1,0:T(8,128)(2,1)S(1)}, bf16[288,128]{1,0:T(8,128)(2,1)S(1)}, u32[]{:S(2)}, u32[]{:S(2)}) %collective-permute-start.3) | collective-permute-done | bytes 73760 | tf_op jit(solution)/shard_map/ppermute | solution.py:324
  18.1 0.4 %shard_map.98.r_0_ = f32[64,1024]{1,0:T(8,128)S(1)} custom-call(f32[64,1024]{1,0:T(8,128)S(1)} %shard_map.96.r_0_, bf16[288,128]{1,0:T(8,128)(2,1)S(1)} %collective-permute-done.3.r_1_.r_2_), custom_call_target="tpu_custom_call" | custom-call | flops 1000000000 | bytes 1000000 | tf_op jit(solution)/shard_map/pallas_call | solution.py:351
  18.6 0.9 %collective-permute-done.4.r_1_.r_0_ = bf16[288,128]{1,0:T(8,128)(2,1)S(1)} collective-permute-done((bf16[288,128]{1,0:T(8,128)(2,1)S(1)}, bf16[288,128]{1,0:T(8,128)(2,1)S(1)}, u32[]{:S(2)}, u32[]{:S(2)}) %collective-permute-start.4) | collective-permute-done | bytes 73760 | tf_op jit(solution)/shard_map/ppermute | solution.py:324
  19.5 0.5 %shard_map.99.r_0_ = bf16[32,1024]{1,0:T(8,128)(2,1)S(1)} custom-call(f32[64,1024]{1,0:T(8,128)S(1)} %shard_map.98.r_0_, bf16[288,128]{1,0:T(8,128)(2,1)S(1)} %collective-permute-done.4.r_1_.r_0_, bf16[288,128]{1,0:T(8,128)(2,1)S(1)} %collective-permute-done.3.r_1_.r_2_, bf16[16,128]{1,0:T(8,128)(2,1)S(1)} %collective-permute-done.5.r_3_), custom_call_target="tpu_custom_call" | custom-call | flops 1000000000 | bytes 1000000 | tf_op jit(solution)/shard_map/pallas_call | solution.py:352
  20.0 1.3 %collective-permute-start.8 = (bf16[32,1024]{1,0:T(8,128)(2,1)S(1)}, bf16[32,1024]{1,0:T(8,128)(2,1)S(1)}, u32[]{:S(2)}, u32[]{:S(2)}) collective-permute-start(bf16[32,1024]{1,0:T(8,128)(2,1)S(1)} %shard_map.99.r_0_), channel_id=1, source_target_pairs={{0,16},{1,9},{2,18},{3,11},{4,20},{5,13},{6,22},{7,15},{8,24},{9,1... | collective-permute-start | bytes 196616 | tf_op jit(solution)/shard_map/ppermute | solution.py:320
  21.3 1.4 %collective-permute-start.7 = (bf16[32,1024]{1,0:T(8,128)(2,1)S(1)}, bf16[32,1024]{1,0:T(8,128)(2,1)S(1)}, u32[]{:S(2)}, u32[]{:S(2)}) collective-permute-start(bf16[32,1024]{1,0:T(8,128)(2,1)S(1)} %shard_map.99.r_0_), channel_id=1, source_target_pairs={{0,8},{1,25},{2,10},{3,27},{4,12},{5,29},{6,14},{7,31},{8,0},{9,17... | collective-permute-start | bytes 196616 | tf_op jit(solution)/shard_map/ppermute | solution.py:320
  22.7 1.7 %collective-permute-start.6 = (bf16[32,1024]{1,0:T(8,128)(2,1)S(1)}, bf16[32,1024]{1,0:T(8,128)(2,1)S(1)}, u32[]{:S(2)}, u32[]{:S(2)}) collective-permute-start(bf16[32,1024]{1,0:T(8,128)(2,1)S(1)} %shard_map.99.r_0_), channel_id=1, source_target_pairs={{0,24},{1,17},{2,26},{3,19},{4,28},{5,21},{6,30},{7,23},{8,16},{9,... | collective-permute-start | bytes 196616 | tf_op jit(solution)/shard_map/ppermute | solution.py:320
  24.5 2.9 %collective-permute-done.8.r_3_ = bf16[32,1024]{1,0:T(8,128)(2,1)S(1)} collective-permute-done((bf16[32,1024]{1,0:T(8,128)(2,1)S(1)}, bf16[32,1024]{1,0:T(8,128)(2,1)S(1)}, u32[]{:S(2)}, u32[]{:S(2)}) %collective-permute-start.8) | collective-permute-done | bytes 65568 | tf_op jit(solution)/shard_map/ppermute | solution.py:320
  27.5 1.4 %collective-permute-done.6.r_1_ = bf16[32,1024]{1,0:T(8,128)(2,1)S(1)} collective-permute-done((bf16[32,1024]{1,0:T(8,128)(2,1)S(1)}, bf16[32,1024]{1,0:T(8,128)(2,1)S(1)}, u32[]{:S(2)}, u32[]{:S(2)}) %collective-permute-start.6) | collective-permute-done | bytes 65568 | tf_op jit(solution)/shard_map/ppermute | solution.py:320
  28.9 0.2 shard_map.101
  29.2 2.2 %collective-permute-start.9 = (bf16[144,128]{1,0:T(8,128)(2,1)S(1)}, bf16[144,128]{1,0:T(8,128)(2,1)S(1)}, u32[]{:S(2)}, u32[]{:S(2)}) collective-permute-start(bf16[144,128]{1,0:T(8,128)(2,1)S(1)} %get-tuple-element.31), channel_id=1, source_target_pairs={{0,7},{1,0},{2,1},{3,2},{4,3},{5,4},{6,5},{7,6},{8,15},{9,8},{10,9... | collective-permute-start | bytes 110600 | tf_op jit(solution)/shard_map/ppermute | solution.py:324
  31.4 1.0 %collective-permute-start.10 = (bf16[144,128]{1,0:T(8,128)(2,1)S(1)}, bf16[144,128]{1,0:T(8,128)(2,1)S(1)}, u32[]{:S(2)}, u32[]{:S(2)}) collective-permute-start(bf16[144,128]{1,0:T(8,128)(2,1)S(1)} %get-tuple-element.32), channel_id=1, source_target_pairs={{0,6},{1,7},{2,0},{3,1},{4,2},{5,3},{6,4},{7,5},{8,14},{9,15},{10,... | collective-permute-start | bytes 110600 | tf_op jit(solution)/shard_map/ppermute | solution.py:324
  32.4 0.9 %shard_map.102 = (bf16[1024,128]{1,0:T(8,128)(2,1)}, bf16[128,128]{1,0:T(8,128)(2,1)S(1)}) custom-call(bf16[128,1024]{1,0:T(8,128)(2,1)S(1)} %get-tuple-element.26.tile_ref, bf16[1024,128]{1,0:T(8,128)(2,1)S(1)} %get-tuple-element.27.hot_ref), custom_call_target="tpu_custom_call" | custom-call | flops 1000000000 | bytes 1000000 | tf_op jit(solution)/shard_map/pallas_call | solution.py:362
  33.3 2.0 %collective-permute-done.10.r_3_ = bf16[144,128]{1,0:T(8,128)(2,1)S(1)} collective-permute-done((bf16[144,128]{1,0:T(8,128)(2,1)S(1)}, bf16[144,128]{1,0:T(8,128)(2,1)S(1)}, u32[]{:S(2)}, u32[]{:S(2)}) %collective-permute-start.10) | collective-permute-done | bytes 36896 | tf_op jit(solution)/shard_map/ppermute | solution.py:324
  35.4 0.9 %shard_map.103 = bf16[128,256]{1,0:T(8,128)(2,1)} custom-call(f32[128,256]{1,0:T(8,128)S(1)} %get-tuple-element.29.r_0_, bf16[128,128]{1,0:T(8,128)(2,1)S(1)} %get-tuple-element.30.r_1_, bf16[144,128]{1,0:T(8,128)(2,1)S(1)} %collective-permute-done.9.r_2_, bf16[144,128]{1,0:T(8,128)(2,1)S(1)} %collective-permute-done.10.r_3_, ...), custom_call_target="tpu_custom_call" | custom-call | flops 1000000000 | bytes 1000000 | tf_op jit(solution)/shard_map/pallas_call | solution.py:363
  (9 shorter events, 0.5 us)
Async XLA Ops:
  2.4 6.5 %collective-permute-start = (bf16[144,128]{1,0:T(8,128)(2,1)S(1)}, bf16[144,128]{1,0:T(8,128)(2,1)S(1)}, u32[]{:S(2)}, u32[]{:S(2)}) collective-permute-start(bf16[144,128]{1,0:T(8,128)(2,1)S(1)} %get-tuple-element.19), channel_id=1, source_target_pairs={{0,16},{1,17},{2,18},{3,19},{4,20},{5,21},{6,22},{7,23},{8,24},{9,... | collective-permute-start | bytes 110600 | tf_op jit(solution)/shard_map/ppermute | solution.py:320
  6.5 5.8 %collective-permute-start.1 = (bf16[144,128]{1,0:T(8,128)(2,1)S(1)}, bf16[144,128]{1,0:T(8,128)(2,1)S(1)}, u32[]{:S(2)}, u32[]{:S(2)}) collective-permute-start(bf16[144,128]{1,0:T(8,128)(2,1)S(1)} %get-tuple-element.20), channel_id=1, source_target_pairs={{0,24},{1,25},{2,26},{3,27},{4,28},{5,29},{6,30},{7,31},{8,16},{9,... | collective-permute-start | bytes 110600 | tf_op jit(solution)/shard_map/ppermute | solution.py:320
  7.9 4.4 %collective-permute-start.2 = (bf16[144,128]{1,0:T(8,128)(2,1)S(1)}, bf16[144,128]{1,0:T(8,128)(2,1)S(1)}, u32[]{:S(2)}, u32[]{:S(2)}) collective-permute-start(bf16[144,128]{1,0:T(8,128)(2,1)S(1)} %get-tuple-element.21), channel_id=1, source_target_pairs={{0,8},{1,9},{2,10},{3,11},{4,12},{5,13},{6,14},{7,15},{8,0},{9,1},... | collective-permute-start | bytes 110600 | tf_op jit(solution)/shard_map/ppermute | solution.py:320
  12.6 6.0 %collective-permute-start.5 = (bf16[16,128]{1,0:T(8,128)(2,1)S(1)}, bf16[16,128]{1,0:T(8,128)(2,1)S(1)}, u32[]{:S(2)}, u32[]{:S(2)}) collective-permute-start(bf16[16,128]{1,0:T(8,128)(2,1)S(1)} %get-tuple-element.24), channel_id=1, source_target_pairs={{0,3},{1,4},{2,5},{3,6},{4,7},{5,0},{6,1},{7,2},{8,11},{9,12},{10,... | collective-permute-start | bytes 12296 | tf_op jit(solution)/shard_map/ppermute | solution.py:324
  12.6 5.5 %collective-permute-start.3 = (bf16[288,128]{1,0:T(8,128)(2,1)S(1)}, bf16[288,128]{1,0:T(8,128)(2,1)S(1)}, u32[]{:S(2)}, u32[]{:S(2)}) collective-permute-start(bf16[288,128]{1,0:T(8,128)(2,1)S(1)} %get-tuple-element.22), channel_id=1, source_target_pairs={{0,2},{1,3},{2,4},{3,5},{4,6},{5,7},{6,0},{7,1},{8,10},{9,11},{10,... | collective-permute-start | bytes 221192 | tf_op jit(solution)/shard_map/ppermute | solution.py:324
  14.2 5.3 %collective-permute-start.4 = (bf16[288,128]{1,0:T(8,128)(2,1)S(1)}, bf16[288,128]{1,0:T(8,128)(2,1)S(1)}, u32[]{:S(2)}, u32[]{:S(2)}) collective-permute-start(bf16[288,128]{1,0:T(8,128)(2,1)S(1)} %get-tuple-element.23), channel_id=1, source_target_pairs={{0,1},{1,2},{2,3},{3,4},{4,5},{5,6},{6,7},{7,0},{8,9},{9,10},{10,1... | collective-permute-start | bytes 221192 | tf_op jit(solution)/shard_map/ppermute | solution.py:324
  20.0 7.5 %collective-permute-start.8 = (bf16[32,1024]{1,0:T(8,128)(2,1)S(1)}, bf16[32,1024]{1,0:T(8,128)(2,1)S(1)}, u32[]{:S(2)}, u32[]{:S(2)}) collective-permute-start(bf16[32,1024]{1,0:T(8,128)(2,1)S(1)} %shard_map.99.r_0_), channel_id=1, source_target_pairs={{0,16},{1,9},{2,18},{3,11},{4,20},{5,13},{6,22},{7,15},{8,24},{9,1... | collective-permute-start | bytes 196616 | tf_op jit(solution)/shard_map/ppermute | solution.py:320
  21.3 6.2 %collective-permute-start.7 = (bf16[32,1024]{1,0:T(8,128)(2,1)S(1)}, bf16[32,1024]{1,0:T(8,128)(2,1)S(1)}, u32[]{:S(2)}, u32[]{:S(2)}) collective-permute-start(bf16[32,1024]{1,0:T(8,128)(2,1)S(1)} %shard_map.99.r_0_), channel_id=1, source_target_pairs={{0,8},{1,25},{2,10},{3,27},{4,12},{5,29},{6,14},{7,31},{8,0},{9,17... | collective-permute-start | bytes 196616 | tf_op jit(solution)/shard_map/ppermute | solution.py:320
  22.7 6.2 %collective-permute-start.6 = (bf16[32,1024]{1,0:T(8,128)(2,1)S(1)}, bf16[32,1024]{1,0:T(8,128)(2,1)S(1)}, u32[]{:S(2)}, u32[]{:S(2)}) collective-permute-start(bf16[32,1024]{1,0:T(8,128)(2,1)S(1)} %shard_map.99.r_0_), channel_id=1, source_target_pairs={{0,24},{1,17},{2,26},{3,19},{4,28},{5,21},{6,30},{7,23},{8,16},{9,... | collective-permute-start | bytes 196616 | tf_op jit(solution)/shard_map/ppermute | solution.py:320
  29.1 4.2 %collective-permute-start.11 = (bf16[16,128]{1,0:T(8,128)(2,1)S(1)}, bf16[16,128]{1,0:T(8,128)(2,1)S(1)}, u32[]{:S(2)}, u32[]{:S(2)}) collective-permute-start(bf16[16,128]{1,0:T(8,128)(2,1)S(1)} %get-tuple-element.33), channel_id=1, source_target_pairs={{0,5},{1,6},{2,7},{3,0},{4,1},{5,2},{6,3},{7,4},{8,13},{9,14},{10,... | collective-permute-start | bytes 12296 | tf_op jit(solution)/shard_map/ppermute | solution.py:324
  29.2 4.2 %collective-permute-start.9 = (bf16[144,128]{1,0:T(8,128)(2,1)S(1)}, bf16[144,128]{1,0:T(8,128)(2,1)S(1)}, u32[]{:S(2)}, u32[]{:S(2)}) collective-permute-start(bf16[144,128]{1,0:T(8,128)(2,1)S(1)} %get-tuple-element.31), channel_id=1, source_target_pairs={{0,7},{1,0},{2,1},{3,2},{4,3},{5,4},{6,5},{7,6},{8,15},{9,8},{10,9... | collective-permute-start | bytes 110600 | tf_op jit(solution)/shard_map/ppermute | solution.py:324
  31.4 4.0 %collective-permute-start.10 = (bf16[144,128]{1,0:T(8,128)(2,1)S(1)}, bf16[144,128]{1,0:T(8,128)(2,1)S(1)}, u32[]{:S(2)}, u32[]{:S(2)}) collective-permute-start(bf16[144,128]{1,0:T(8,128)(2,1)S(1)} %get-tuple-element.32), channel_id=1, source_target_pairs={{0,6},{1,7},{2,0},{3,1},{4,2},{5,3},{6,4},{7,5},{8,14},{9,15},{10,... | collective-permute-start | bytes 110600 | tf_op jit(solution)/shard_map/ppermute | solution.py:324

commit v6 on v4

--- a/solution.py
+++ b/solution.py
@@ -13,7 +13,9 @@
 BF16 = jnp.bfloat16
 SENT = 32.0
 REACH = 3
-PARAMS = pltpu.CompilerParams(vmem_limit_bytes=24 * 1024 * 1024)
+GRANT = 24 * 1024 * 1024
+PARAMS = pltpu.CompilerParams(vmem_limit_bytes=GRANT)
+PACKED = pltpu.CompilerParams(vmem_limit_bytes=GRANT)
 
 
 def iota(shape, dim):
@@ -289,14 +291,14 @@
 HBM = pl.BlockSpec(memory_space=pltpu.HBM)
 
 
-def call(body, outs, specs, scratch=(), micros=1):
+def call(body, outs, specs, name, scratch=(), micros=1):
     return pl.pallas_call(
         body,
         out_shape=tuple(jax.ShapeDtypeStruct(s, t) for s, t in outs),
         in_specs=specs,
         out_specs=tuple(VM for _ in outs),
         scratch_shapes=scratch,
-        compiler_params=PARAMS,
+        compiler_params=PACKED if name in ("own", "far", "sum") else PARAMS,
         cost_estimate=pl.CostEstimate(
             flops=micros * 10**9, bytes_accessed=micros * 10**6, transcendentals=0
         ),
@@ -327,28 +329,38 @@
             lambda *r: match_body(exps, tiles, *r),
             [((height, across), F32)] + [message] * exps,
             [HBM] * len(args),
+            "match",
             [(pltpu.SMEM if i == 3 else pltpu.VMEM)(a.shape, a.dtype) for i, a in enumerate(args)]
             + [pltpu.SemaphoreType.DMA((len(args),)), pltpu.VMEM((4, PC, PC), packs)],
         )(*args)
         z = [z[0]] + [along_exp(z[k], k, exps) for k in range(1, exps)]
         big = ((2 * share * exps + PR * meta_tiles(exps) + PR, PC), BF16)
-        m1, m2, m3 = call(lambda *r: pick_body(exps, *r), [big, big, ((PR, PC), BF16)], [VM] * exps)(*z)
+        m1, m2, m3 = call(
+            lambda *r: pick_body(exps, *r), [big, big, ((PR, PC), BF16)], [VM] * exps, "pick"
+        )(*z)
         m1, m2, m3 = (along_tile(m, i + 1, tiles) for i, m in enumerate((m1, m2, m3)))
-        (own,) = call(lambda *r: own_body(exps, *r), [((2 * share, TR), F32)], [VM] * exps)(*z)
-        (far,) = call(lambda *r: far_body(exps, *r), [((2 * share, TR), F32)], [VM] * 2)(own, m2)
-        (packed,) = call(lambda *r: sum_body(exps, *r), [((share, TR), BF16)], [VM] * 4)(far, m1, m2, m3)
+        (own,) = call(lambda *r: own_body(exps, *r), [((2 * share, TR), F32)], [VM] * exps, "own")(*z)
+        (far,) = call(lambda *r: far_body(exps, *r), [((2 * share, TR), F32)], [VM] * 2, "far")(own, m2)
+        (packed,) = call(
+            lambda *r: sum_body(exps, *r), [((share, TR), BF16)], [VM] * 4, "sum"
+        )(far, m1, m2, m3)
         packed = [packed] + [along_exp(packed, k, exps) for k in range(1, exps)]
         hot, own_hot = call(
-            lambda *r: place_body(exps, *r), [((TR, 2 * PC), BF16), ((TR, PC), BF16)], [VM] * 3
+            lambda *r: place_body(exps, *r), [((TR, 2 * PC), BF16), ((TR, PC), BF16)], [VM] * 3, "place"
         )(m1, m2, z[0])
         back = ((PC + PR, PC), BF16)
         tile, n1, n2, n3 = call(
-            lambda *r: cut_body(exps, *r), [((PC, TR), packs), back, back, ((PR, PC), BF16)], [VM] * (exps + 1)
+            lambda *r: cut_body(exps, *r),
+            [((PC, TR), packs), back, back, ((PR, PC), BF16)],
+            [VM] * (exps + 1),
+            "cut",
         )(*packed, hot)
         n1, n2, n3 = (along_tile(n, -1 - i, tiles) for i, n in enumerate((n1, n2, n3)))
-        template, own = call(template_body, [((TR, PC), BF16), ((PC, PC), BF16)], [VM] * 2)(tile, own_hot)
+        template, own = call(
+            template_body, [((TR, PC), BF16), ((PC, PC), BF16)], [VM] * 2, "template"
+        )(tile, own_hot)
         (difference,) = call(
-            lambda *r: subtract_body(exps, *r), [((height, across), BF16)], [VM] * 6
+            lambda *r: subtract_body(exps, *r), [((height, across), BF16)], [VM] * 6, "subtract"
         )(matched, own, n1, n2, n3, z[0])
         return template, difference[None, None]
 

time: 36.5 us -> 36.5 us (level)
  no operation moved by 1% of the time
where the time goes in v6:
time: 36.5 us; the launch traced here: 36.4 us
  starting transfers between devices  16.3 us (45%)
  waiting for transfers between devices  13.8 us (38%)
  Pallas kernels  5.56 us (15%)
  between operations  0.7 us (2%)
    ppermute x6, starting transfers between devices, along_exp(): return lax.ppermute(x, 'exp', [(i, i ^ k) for i in range(exps)])  10.2 us
    ppermute x6, waiting for transfers between devices, along_exp(): return lax.ppermute(x, 'exp', [(i, i ^ k) for i in range(exps)])  8.67 us
    ppermute x6, starting transfers between devices, along_tile(): lax.ppermute(x, 'tile', [(i, (i + by) % tiles) for i in range(tiles)])  6.18 us
    ppermute x6, waiting for transfers between devices, along_tile(): lax.ppermute(x, 'tile', [(i, (i + by) % tiles) for i in range(tiles)])  5.11 us
    pallas_call x1, Pallas kernels, steps(): call(lambda *r: match_body(exps, tiles, *r), [((height, across), F32)] +...  1.74 us
    pallas_call x1, Pallas kernels, steps(): call(template_body, [((TR, PC), BF16), ((PC, PC), BF16)], [VM] * 2, 'temp...  0.92 us
    pallas_call x1, Pallas kernels, steps(): call(lambda *r: subtract_body(exps, *r), [((height, across), BF16)], [VM]...  0.91 us
  transfers between devices with their start and end apart: 12, of which 7 were waited for; matrix products, arithmetic and copies ran while one was open for 0% of the time, Pallas kernels for 5%

profile of v6, /device:TPU:0, one launch (start us, length us, event | category | flops | bytes accessed | tf_op | source)
XLA Modules:
  0.0 36.4 jit_solution(14863371384523740622)
XLA Ops:
  0.6 1.7 %shard_map.95 = (f32[128,256]{1,0:T(8,128)S(1)}, bf16[144,128]{1,0:T(8,128)(2,1)S(1)}, bf16[144,128]{1,0:T(8,128)(2,1)S(1)}, bf16[144,128]{1,0:T(8,128)(2,1)S(1)}, bf16[144,128]{1,0:T(8,128)(2,1)S(1)}) custom-call(bf16[8,31]{1,0:T(8,128)(2,1)} %r_0_.1, bf16[8,31]{1,0:T(8,128)(2,1)} %r_1_.1, bf16[128,256]{1,0:T(8,128)(2,1)} %bitcast.8, ...), custom_call_target="tpu_custom_call" | custom-call | flops 1000000000 | bytes 1000000 | tf_op jit(solution)/shard_map/pallas_call | solution.py:328
  2.4 3.1 %collective-permute-start = (bf16[144,128]{1,0:T(8,128)(2,1)S(1)}, bf16[144,128]{1,0:T(8,128)(2,1)S(1)}, u32[]{:S(2)}, u32[]{:S(2)}) collective-permute-start(bf16[144,128]{1,0:T(8,128)(2,1)S(1)} %get-tuple-element.19), channel_id=1, source_target_pairs={{0,8},{8,0},{16,24},{24,16},{1,9},{9,1},{17,25},{25,17},{2,10},{10... | collective-permute-start | bytes 110600 | tf_op jit(solution)/shard_map/ppermute | solution.py:309
  5.5 2.6 %collective-permute-start.1 = (bf16[144,128]{1,0:T(8,128)(2,1)S(1)}, bf16[144,128]{1,0:T(8,128)(2,1)S(1)}, u32[]{:S(2)}, u32[]{:S(2)}) collective-permute-start(bf16[144,128]{1,0:T(8,128)(2,1)S(1)} %get-tuple-element.20), channel_id=1, source_target_pairs={{0,16},{8,24},{16,0},{24,8},{1,17},{9,25},{17,1},{25,9},{2,18},{10... | collective-permute-start | bytes 110600 | tf_op jit(solution)/shard_map/ppermute | solution.py:309
  8.1 2.9 %collective-permute-done.1.r_2_ = bf16[144,128]{1,0:T(8,128)(2,1)S(1)} collective-permute-done((bf16[144,128]{1,0:T(8,128)(2,1)S(1)}, bf16[144,128]{1,0:T(8,128)(2,1)S(1)}, u32[]{:S(2)}, u32[]{:S(2)}) %collective-permute-start.1) | collective-permute-done | bytes 36896 | tf_op jit(solution)/shard_map/ppermute | solution.py:309
  11.0 2.8 %collective-permute-done.2.r_3_ = bf16[144,128]{1,0:T(8,128)(2,1)S(1)} collective-permute-done((bf16[144,128]{1,0:T(8,128)(2,1)S(1)}, bf16[144,128]{1,0:T(8,128)(2,1)S(1)}, u32[]{:S(2)}, u32[]{:S(2)}) %collective-permute-start.2) | collective-permute-done | bytes 36896 | tf_op jit(solution)/shard_map/ppermute | solution.py:309
  13.8 0.3 shard_map.97
  14.2 1.5 %collective-permute-start.3 = (bf16[288,128]{1,0:T(8,128)(2,1)S(1)}, bf16[288,128]{1,0:T(8,128)(2,1)S(1)}, u32[]{:S(2)}, u32[]{:S(2)}) collective-permute-start(bf16[288,128]{1,0:T(8,128)(2,1)S(1)} %get-tuple-element.22), channel_id=1, source_target_pairs={{0,2},{1,3},{2,4},{3,5},{4,6},{5,7},{6,0},{7,1},{8,10},{9,11},{10,... | collective-permute-start | bytes 221192 | tf_op jit(solution)/shard_map/ppermute | solution.py:313
  15.7 1.3 %collective-permute-start.4 = (bf16[288,128]{1,0:T(8,128)(2,1)S(1)}, bf16[288,128]{1,0:T(8,128)(2,1)S(1)}, u32[]{:S(2)}, u32[]{:S(2)}) collective-permute-start(bf16[288,128]{1,0:T(8,128)(2,1)S(1)} %get-tuple-element.23), channel_id=1, source_target_pairs={{0,1},{1,2},{2,3},{3,4},{4,5},{5,6},{6,7},{7,0},{8,9},{9,10},{10,1... | collective-permute-start | bytes 221192 | tf_op jit(solution)/shard_map/ppermute | solution.py:313
  17.0 0.4 %shard_map.96.r_0_ = f32[64,1024]{1,0:T(8,128)S(1)} custom-call(bf16[144,128]{1,0:T(8,128)(2,1)S(1)} %get-tuple-element.18.r_0_.r_2_.r_5_, bf16[144,128]{1,0:T(8,128)(2,1)S(1)} %collective-permute-done.r_1_, bf16[144,128]{1,0:T(8,128)(2,1)S(1)} %collective-permute-done.1.r_2_, bf16[144,128]{1,0:T(8,128)(2,1)S(1)} %collective-permute-done.2.r_3_), custom_call_target="tpu_custom_call" | custom-call | flops 1000000000 | bytes 1000000 | tf_op jit(solution)/shard_map/pallas_call | solution.py:342
  17.5 2.2 %collective-permute-done.3.r_1_.r_2_ = bf16[288,128]{1,0:T(8,128)(2,1)S(1)} collective-permute-done((bf16[288,128]{1,0:T(8,128)(2,1)S(1)}, bf16[288,128]{1,0:T(8,128)(2,1)S(1)}, u32[]{:S(2)}, u32[]{:S(2)}) %collective-permute-start.3) | collective-permute-done | bytes 73760 | tf_op jit(solution)/shard_map/ppermute | solution.py:313
  19.7 0.4 %shard_map.98.r_0_ = f32[64,1024]{1,0:T(8,128)S(1)} custom-call(f32[64,1024]{1,0:T(8,128)S(1)} %shard_map.96.r_0_, bf16[288,128]{1,0:T(8,128)(2,1)S(1)} %collective-permute-done.3.r_1_.r_2_), custom_call_target="tpu_custom_call" | custom-call | flops 1000000000 | bytes 1000000 | tf_op jit(solution)/shard_map/pallas_call | solution.py:343
  20.1 0.9 %collective-permute-done.4.r_1_.r_0_ = bf16[288,128]{1,0:T(8,128)(2,1)S(1)} collective-permute-done((bf16[288,128]{1,0:T(8,128)(2,1)S(1)}, bf16[288,128]{1,0:T(8,128)(2,1)S(1)}, u32[]{:S(2)}, u32[]{:S(2)}) %collective-permute-start.4) | collective-permute-done | bytes 73760 | tf_op jit(solution)/shard_map/ppermute | solution.py:313
  21.1 0.5 %shard_map.99.r_0_ = bf16[32,1024]{1,0:T(8,128)(2,1)S(1)} custom-call(f32[64,1024]{1,0:T(8,128)S(1)} %shard_map.98.r_0_, bf16[288,128]{1,0:T(8,128)(2,1)S(1)} %collective-permute-done.4.r_1_.r_0_, bf16[288,128]{1,0:T(8,128)(2,1)S(1)} %collective-permute-done.3.r_1_.r_2_, bf16[16,128]{1,0:T(8,128)(2,1)S(1)} %collective-permute-done.5.r_3_), custom_call_target="tpu_custom_call" | custom-call | flops 1000000000 | bytes 1000000 | tf_op jit(solution)/shard_map/pallas_call | solution.py:344
  21.6 0.6 %collective-permute-start.8 = (bf16[32,1024]{1,0:T(8,128)(2,1)S(1)}, bf16[32,1024]{1,0:T(8,128)(2,1)S(1)}, u32[]{:S(2)}, u32[]{:S(2)}) collective-permute-start(bf16[32,1024]{1,0:T(8,128)(2,1)S(1)} %shard_map.99.r_0_), channel_id=1, source_target_pairs={{0,24},{8,16},{16,8},{24,0},{1,25},{9,17},{17,9},{25,1},{2,26},{10... | collective-permute-start | bytes 196616 | tf_op jit(solution)/shard_map/ppermute | solution.py:309
  22.1 3.9 %collective-permute-start.6 = (bf16[32,1024]{1,0:T(8,128)(2,1)S(1)}, bf16[32,1024]{1,0:T(8,128)(2,1)S(1)}, u32[]{:S(2)}, u32[]{:S(2)}) collective-permute-start(bf16[32,1024]{1,0:T(8,128)(2,1)S(1)} %shard_map.99.r_0_), channel_id=1, source_target_pairs={{0,8},{8,0},{16,24},{24,16},{1,9},{9,1},{17,25},{25,17},{2,10},{10... | collective-permute-start | bytes 196616 | tf_op jit(solution)/shard_map/ppermute | solution.py:309
  26.0 0.1 shard_map.100
  26.1 2.2 %collective-permute-done.8.r_3_ = bf16[32,1024]{1,0:T(8,128)(2,1)S(1)} collective-permute-done((bf16[32,1024]{1,0:T(8,128)(2,1)S(1)}, bf16[32,1024]{1,0:T(8,128)(2,1)S(1)}, u32[]{:S(2)}, u32[]{:S(2)}) %collective-permute-start.8) | collective-permute-done | bytes 65568 | tf_op jit(solution)/shard_map/ppermute | solution.py:309
  28.3 0.7 %collective-permute-done.7.r_2_ = bf16[32,1024]{1,0:T(8,128)(2,1)S(1)} collective-permute-done((bf16[32,1024]{1,0:T(8,128)(2,1)S(1)}, bf16[32,1024]{1,0:T(8,128)(2,1)S(1)}, u32[]{:S(2)}, u32[]{:S(2)}) %collective-permute-start.7) | collective-permute-done | bytes 65568 | tf_op jit(solution)/shard_map/ppermute | solution.py:309
  29.0 0.2 shard_map.101
  29.4 2.1 %collective-permute-start.9 = (bf16[144,128]{1,0:T(8,128)(2,1)S(1)}, bf16[144,128]{1,0:T(8,128)(2,1)S(1)}, u32[]{:S(2)}, u32[]{:S(2)}) collective-permute-start(bf16[144,128]{1,0:T(8,128)(2,1)S(1)} %get-tuple-element.31), channel_id=1, source_target_pairs={{0,7},{1,0},{2,1},{3,2},{4,3},{5,4},{6,5},{7,6},{8,15},{9,8},{10,9... | collective-permute-start | bytes 110600 | tf_op jit(solution)/shard_map/ppermute | solution.py:313
  31.5 1.1 %collective-permute-start.10 = (bf16[144,128]{1,0:T(8,128)(2,1)S(1)}, bf16[144,128]{1,0:T(8,128)(2,1)S(1)}, u32[]{:S(2)}, u32[]{:S(2)}) collective-permute-start(bf16[144,128]{1,0:T(8,128)(2,1)S(1)} %get-tuple-element.32), channel_id=1, source_target_pairs={{0,6},{1,7},{2,0},{3,1},{4,2},{5,3},{6,4},{7,5},{8,14},{9,15},{10,... | collective-permute-start | bytes 110600 | tf_op jit(solution)/shard_map/ppermute | solution.py:313
  32.6 0.9 %shard_map.102 = (bf16[1024,128]{1,0:T(8,128)(2,1)}, bf16[128,128]{1,0:T(8,128)(2,1)S(1)}) custom-call(bf16[128,1024]{1,0:T(8,128)(2,1)S(1)} %get-tuple-element.26.tile_ref, bf16[1024,128]{1,0:T(8,128)(2,1)S(1)} %get-tuple-element.27.hot_ref), custom_call_target="tpu_custom_call" | custom-call | flops 1000000000 | bytes 1000000 | tf_op jit(solution)/shard_map/pallas_call | solution.py:359
  33.5 2.0 %collective-permute-done.10.r_3_ = bf16[144,128]{1,0:T(8,128)(2,1)S(1)} collective-permute-done((bf16[144,128]{1,0:T(8,128)(2,1)S(1)}, bf16[144,128]{1,0:T(8,128)(2,1)S(1)}, u32[]{:S(2)}, u32[]{:S(2)}) %collective-permute-start.10) | collective-permute-done | bytes 36896 | tf_op jit(solution)/shard_map/ppermute | solution.py:313
  35.5 0.9 %shard_map.103 = bf16[128,256]{1,0:T(8,128)(2,1)} custom-call(f32[128,256]{1,0:T(8,128)S(1)} %get-tuple-element.29.r_0_, bf16[128,128]{1,0:T(8,128)(2,1)S(1)} %get-tuple-element.30.r_1_, bf16[144,128]{1,0:T(8,128)(2,1)S(1)} %collective-permute-done.9.r_2_, bf16[144,128]{1,0:T(8,128)(2,1)S(1)} %collective-permute-done.10.r_3_, ...), custom_call_target="tpu_custom_call" | custom-call | flops 1000000000 | bytes 1000000 | tf_op jit(solution)/shard_map/pallas_call | solution.py:362
  (9 shorter events, 0.1 us)
Async XLA Ops:
  2.4 5.7 %collective-permute-start = (bf16[144,128]{1,0:T(8,128)(2,1)S(1)}, bf16[144,128]{1,0:T(8,128)(2,1)S(1)}, u32[]{:S(2)}, u32[]{:S(2)}) collective-permute-start(bf16[144,128]{1,0:T(8,128)(2,1)S(1)} %get-tuple-element.19), channel_id=1, source_target_pairs={{0,8},{8,0},{16,24},{24,16},{1,9},{9,1},{17,25},{25,17},{2,10},{10... | collective-permute-start | bytes 110600 | tf_op jit(solution)/shard_map/ppermute | solution.py:309
  5.5 5.5 %collective-permute-start.1 = (bf16[144,128]{1,0:T(8,128)(2,1)S(1)}, bf16[144,128]{1,0:T(8,128)(2,1)S(1)}, u32[]{:S(2)}, u32[]{:S(2)}) collective-permute-start(bf16[144,128]{1,0:T(8,128)(2,1)S(1)} %get-tuple-element.20), channel_id=1, source_target_pairs={{0,16},{8,24},{16,0},{24,8},{1,17},{9,25},{17,1},{25,9},{2,18},{10... | collective-permute-start | bytes 110600 | tf_op jit(solution)/shard_map/ppermute | solution.py:309
  8.1 5.8 %collective-permute-start.2 = (bf16[144,128]{1,0:T(8,128)(2,1)S(1)}, bf16[144,128]{1,0:T(8,128)(2,1)S(1)}, u32[]{:S(2)}, u32[]{:S(2)}) collective-permute-start(bf16[144,128]{1,0:T(8,128)(2,1)S(1)} %get-tuple-element.21), channel_id=1, source_target_pairs={{0,24},{8,16},{16,8},{24,0},{1,25},{9,17},{17,9},{25,1},{2,26},{10... | collective-permute-start | bytes 110600 | tf_op jit(solution)/shard_map/ppermute | solution.py:309
  14.1 6.0 %collective-permute-start.5 = (bf16[16,128]{1,0:T(8,128)(2,1)S(1)}, bf16[16,128]{1,0:T(8,128)(2,1)S(1)}, u32[]{:S(2)}, u32[]{:S(2)}) collective-permute-start(bf16[16,128]{1,0:T(8,128)(2,1)S(1)} %get-tuple-element.24), channel_id=1, source_target_pairs={{0,3},{1,4},{2,5},{3,6},{4,7},{5,0},{6,1},{7,2},{8,11},{9,12},{10,... | collective-permute-start | bytes 12296 | tf_op jit(solution)/shard_map/ppermute | solution.py:313
  14.2 5.5 %collective-permute-start.3 = (bf16[288,128]{1,0:T(8,128)(2,1)S(1)}, bf16[288,128]{1,0:T(8,128)(2,1)S(1)}, u32[]{:S(2)}, u32[]{:S(2)}) collective-permute-start(bf16[288,128]{1,0:T(8,128)(2,1)S(1)} %get-tuple-element.22), channel_id=1, source_target_pairs={{0,2},{1,3},{2,4},{3,5},{4,6},{5,7},{6,0},{7,1},{8,10},{9,11},{10,... | collective-permute-start | bytes 221192 | tf_op jit(solution)/shard_map/ppermute | solution.py:313
  15.7 5.3 %collective-permute-start.4 = (bf16[288,128]{1,0:T(8,128)(2,1)S(1)}, bf16[288,128]{1,0:T(8,128)(2,1)S(1)}, u32[]{:S(2)}, u32[]{:S(2)}) collective-permute-start(bf16[288,128]{1,0:T(8,128)(2,1)S(1)} %get-tuple-element.23), channel_id=1, source_target_pairs={{0,1},{1,2},{2,3},{3,4},{4,5},{5,6},{6,7},{7,0},{8,9},{9,10},{10,1... | collective-permute-start | bytes 221192 | tf_op jit(solution)/shard_map/ppermute | solution.py:313
  21.6 6.8 %collective-permute-start.8 = (bf16[32,1024]{1,0:T(8,128)(2,1)S(1)}, bf16[32,1024]{1,0:T(8,128)(2,1)S(1)}, u32[]{:S(2)}, u32[]{:S(2)}) collective-permute-start(bf16[32,1024]{1,0:T(8,128)(2,1)S(1)} %shard_map.99.r_0_), channel_id=1, source_target_pairs={{0,24},{8,16},{16,8},{24,0},{1,25},{9,17},{17,9},{25,1},{2,26},{10... | collective-permute-start | bytes 196616 | tf_op jit(solution)/shard_map/ppermute | solution.py:309
  22.1 6.9 %collective-permute-start.7 = (bf16[32,1024]{1,0:T(8,128)(2,1)S(1)}, bf16[32,1024]{1,0:T(8,128)(2,1)S(1)}, u32[]{:S(2)}, u32[]{:S(2)}) collective-permute-start(bf16[32,1024]{1,0:T(8,128)(2,1)S(1)} %shard_map.99.r_0_), channel_id=1, source_target_pairs={{0,16},{8,24},{16,0},{24,8},{1,17},{9,25},{17,1},{25,9},{2,18},{10... | collective-permute-start | bytes 196616 | tf_op jit(solution)/shard_map/ppermute | solution.py:309
  22.1 6.9 %collective-permute-start.6 = (bf16[32,1024]{1,0:T(8,128)(2,1)S(1)}, bf16[32,1024]{1,0:T(8,128)(2,1)S(1)}, u32[]{:S(2)}, u32[]{:S(2)}) collective-permute-start(bf16[32,1024]{1,0:T(8,128)(2,1)S(1)} %shard_map.99.r_0_), channel_id=1, source_target_pairs={{0,8},{8,0},{16,24},{24,16},{1,9},{9,1},{17,25},{25,17},{2,10},{10... | collective-permute-start | bytes 196616 | tf_op jit(solution)/shard_map/ppermute | solution.py:309
  29.3 4.2 %collective-permute-start.11 = (bf16[16,128]{1,0:T(8,128)(2,1)S(1)}, bf16[16,128]{1,0:T(8,128)(2,1)S(1)}, u32[]{:S(2)}, u32[]{:S(2)}) collective-permute-start(bf16[16,128]{1,0:T(8,128)(2,1)S(1)} %get-tuple-element.33), channel_id=1, source_target_pairs={{0,5},{1,6},{2,7},{3,0},{4,1},{5,2},{6,3},{7,4},{8,13},{9,14},{10,... | collective-permute-start | bytes 12296 | tf_op jit(solution)/shard_map/ppermute | solution.py:313
  29.4 4.2 %collective-permute-start.9 = (bf16[144,128]{1,0:T(8,128)(2,1)S(1)}, bf16[144,128]{1,0:T(8,128)(2,1)S(1)}, u32[]{:S(2)}, u32[]{:S(2)}) collective-permute-start(bf16[144,128]{1,0:T(8,128)(2,1)S(1)} %get-tuple-element.31), channel_id=1, source_target_pairs={{0,7},{1,0},{2,1},{3,2},{4,3},{5,4},{6,5},{7,6},{8,15},{9,8},{10,9... | collective-permute-start | bytes 110600 | tf_op jit(solution)/shard_map/ppermute | solution.py:313
  31.5 4.0 %collective-permute-start.10 = (bf16[144,128]{1,0:T(8,128)(2,1)S(1)}, bf16[144,128]{1,0:T(8,128)(2,1)S(1)}, u32[]{:S(2)}, u32[]{:S(2)}) collective-permute-start(bf16[144,128]{1,0:T(8,128)(2,1)S(1)} %get-tuple-element.32), channel_id=1, source_target_pairs={{0,6},{1,7},{2,0},{3,1},{4,2},{5,3},{6,4},{7,5},{8,14},{9,15},{10,... | collective-permute-start | bytes 110600 | tf_op jit(solution)/shard_map/ppermute | solution.py:313
